TPU v7x, 128 devices: a whole 4x4x4 slice. The times are simulated.
128 devices in a mesh: row: 32 (over y, x, core), col: 4 (over z).
Axes of the slice: x: 4, y: 4, z: 4, core: 2. Of those that a mesh axis runs over, the one named last changes fastest.
Arguments:
- embeddings: float32 [16384, 256], P(('col', 'row')), may hold values from -6 to 6
- levels: int32 [16384], P('row'), may hold values from 0 to 7
Outputs:
- responsibility: float32 [16384, 16384], P('row', 'col')
- availability: float32 [16384, 16384], P('row', 'col')
All inputs are finite; a program needn't handle non-finite values.
Results may differ from a plain program's by a relative error of at most 0.0003.
Values sent between devices are 32-bit elements; how exact they have to be, the bound alone decides.
No kernel may reach another device: no remote copies, remote signals or barrier semaphores. Data moves between devices by JAX's collectives and lax.ppermute only.
A program may use at most 64 MiB of HBM per device.

v0:
```python
import jax
import jax.numpy as jnp
from jax import lax
from jax.experimental import pallas as pl
from jax.experimental.pallas import tpu as pltpu
from jax.sharding import PartitionSpec as P


N_ROW, N_COL, SIDE = 32, 4, 4
SHARD, ROWS, D, LANES = 128, 512, 256, 128
BLOCKS = 32
TILE = 64
HOLE = -1e30
BOTH = ("row", "col")
F32 = jnp.float32


def row_of(y, x, core):
    return (y * SIDE + x) * 2 + core


def pairs(target):
    out = []
    for r in range(N_ROW):
        for c in range(N_COL):
            y, x, core = r // 8, r // 2 % 4, r % 2
            to_y, to_x, to_core, to_c = target(y, x, core, c)
            out.append((r * N_COL + c, row_of(to_y, to_x, to_core) * N_COL + to_c))
    return out


def plane_shift(k, stage):
    def target(y, x, core, c):
        if (core == 0) == (stage == 1):
            return y, (x + k) % SIDE, core, c
        return (y + k) % SIDE, x, core, c

    return pairs(target)


def col_shift(k):
    return pairs(lambda y, x, core, c: (y, x, core, (c + k) % N_COL))


def core_swap():
    return pairs(lambda y, x, core, c: (y, x, 1 - core, c))


def to_row_block():
    out = []
    for r in range(N_ROW):
        for j in range(N_COL):
            out.append(((4 * (r % 8) + j) * N_COL + r // 8, r * N_COL + j))
    return out


def permute(a, perm):
    return lax.ppermute(a, BOTH, perm)


def place():
    r, c = lax.axis_index("row"), lax.axis_index("col")
    return r, c


def block_of(n, r):
    k, h, m = n // 8, n // 4 % 2, n % 4
    y, x, core = r // 8, r // 2 % 4, r % 2
    own = core if h == 0 else 1 - core
    a = jnp.where(own == 0, (x - m) % 4, (x - k) % 4)
    b = jnp.where(own == 0, (y - k) % 4, (y - m) % 4)
    return b * 8 + a * 2 + own


def has_diagonal(r, c):
    return jnp.where(r // 8 == c, 1.0, 0.0).astype(F32)


def merge(a, b):
    return jnp.maximum(a[0], b[0]), jnp.maximum(jnp.minimum(a[0], b[0]), jnp.maximum(a[1], b[1]))


def insert(top, x):
    return jnp.maximum(top[0], x), jnp.maximum(top[1], jnp.minimum(top[0], x))


def compact(m1_ref, m2_ref):
    best, second = [], []
    for j in range(4):
        p = (m1_ref[j * 128 : (j + 1) * 128, :].T, m2_ref[j * 128 : (j + 1) * 128, :].T)
        size = 128
        while size > 1:
            size //= 2
            p = merge((p[0][:size], p[1][:size]), (p[0][size:], p[1][size:]))
        best.append(p[0])
        second.append(p[1])
    return jnp.concatenate(best, 0), jnp.concatenate(second, 0)


def store_pair(ref, pair):
    ref[0:4, :] = pair[0]
    ref[4:8, :] = pair[1]


def merged(refs):
    top = (refs[0][0:4, :], refs[0][4:8, :])
    for ref in refs[1:]:
        top = merge(top, (ref[0:4, :], ref[4:8, :]))
    return top


def spread(compacted, ref):
    for j in range(4):
        ref[j * 128 : (j + 1) * 128, :] = jnp.broadcast_to(compacted[j : j + 1, :], (128, 128)).T


def preference(levels_ref):
    return 0.25 * levels_ref[...].astype(F32) - 1.0


def first_diagonal(pref, best, second):
    return 0.5 * (pref - jnp.where(pref >= best, second, best))


def write_sums(acc_ref, tt_ref, diag, r, c, copies_ref):
    for n in range(BLOCKS):
        tt_ref[pl.ds(block_of(n, r), 1), :] = jnp.sum(acc_ref[n], axis=0, keepdims=True)
    f = has_diagonal(r, c)
    for j in range(4):
        at = pl.ds(4 * (r % 8) + j, 1)
        tt_ref[at, :] = tt_ref[at, :] + f * diag[j : j + 1, :]
    sums = tt_ref[...]
    for i in range(N_ROW):
        copies_ref[i * BLOCKS : (i + 1) * BLOCKS, :] = sums


def join_sums(copies_ref, tt_ref):
    parts = [copies_ref[i * BLOCKS : (i + 1) * BLOCKS, :] for i in range(N_ROW)]
    while len(parts) > 1:
        parts = [p + q for p, q in zip(parts[::2], parts[1::2])]
    tt_ref[...] = parts[0]


def diagonal_sums(tt_ref, r):
    return jnp.concatenate([tt_ref[pl.ds(4 * (r % 8) + j, 1), :] for j in range(4)], 0)


def unit_kernel(x_ref, o_ref):
    x = x_ref[...]
    o_ref[...] = x * lax.rsqrt(jnp.sum(x * x, axis=1, keepdims=True) + 1e-06)


def split(x):
    high = x.astype(jnp.bfloat16)
    return high, (x - high.astype(F32)).astype(jnp.bfloat16)


def product(a, b):
    dims = (((1,), (1,)), ((), ()))
    dot = lambda p, q: lax.dot_general(p, q, dims, preferred_element_type=F32)
    return dot(a[0], b[0]) + (dot(a[0], b[1]) + dot(a[1], b[0]))


def make_product_kernel(k, first, last):
    def kernel(*refs):
        g, own_ref, partner_ref, refs = refs[:4], refs[4], refs[5], refs[6:]
        if not first:
            in1, in2, refs = refs[0], refs[1], refs[2:]
        if last:
            levels_ref, refs = refs[0], refs[1:]
        s_ref, refs = refs[0], refs[1:]
        if last:
            bs_ref, high, low, m1_ref, m2_ref = refs
        else:
            m1_ref, m2_ref, high, low = refs
        r, c = place()
        for q in range(4):
            h, l = split(g[q][...])
            at = pl.ds(pl.multiple_of((c - q) % 4 * 128, 128), 128)
            high[at, :] = h
            low[at, :] = l
        f = has_diagonal(r, c)
        eye = lax.broadcasted_iota(jnp.int32, (128, 128), 0) == lax.broadcasted_iota(jnp.int32, (128, 128), 1)
        holes = jnp.where(eye, F32(HOLE), F32(0.0))
        for half, ref in enumerate((own_ref, partner_ref)):
            cols = split(ref[...])
            for j in range(4):
                rows = slice(j * 128, (j + 1) * 128)
                p = product((high[rows, :], low[rows, :]), cols)
                if half == 0:
                    if first:
                        top = (jnp.full((128, 128), 2 * HOLE, F32), jnp.full((128, 128), 2 * HOLE, F32))
                    else:
                        top = (in1[rows, :], in2[rows, :])
                else:
                    top = (m1_ref[rows, :], m2_ref[rows, :])
                for m in range(4):
                    n = half * 4 + m
                    here = f * jnp.where(block_of(8 * k + n, r) == 4 * (r % 8) + j, 1.0, 0.0).astype(F32)
                    block = p[:, m * 128 : (m + 1) * 128] + here * holes
                    s_ref[n, rows, :] = block
                    top = insert(top, block)
                m1_ref[rows, :] = top[0]
                m2_ref[rows, :] = top[1]
        if last:
            pair = compact(m1_ref, m2_ref)
            pref = jnp.where(f > 0.0, preference(levels_ref), 2 * HOLE)
            store_pair(bs_ref, insert(pair, pref))

    return kernel


def first_sums_kernel(*refs):
    pieces, levels_ref, s, refs = refs[:4], refs[4], refs[5:9], refs[9:]
    copies_ref, bs_ref, b_ref, s_ref, acc_ref, tt_ref = refs
    r, c = place()
    best, second = merged(pieces)
    store_pair(bs_ref, (best, second))
    spread(best, b_ref)
    spread(second, s_ref)
    acc_ref[...] = jnp.zeros_like(acc_ref)

    def body(t, carry):
        rows = pl.ds(pl.multiple_of(t * TILE, TILE), TILE)
        b = b_ref[rows, :]
        v = 0.5 * (b - s_ref[rows, :])
        for n in range(BLOCKS):
            x = jnp.where(s[n // 8][n % 8, rows, :] >= b, v, 0.0)
            acc_ref[n] += jnp.sum(x.reshape(TILE // 8, 8, LANES), axis=0)
        return carry

    lax.fori_loop(0, ROWS // TILE, body, 0)
    diag = first_diagonal(preference(levels_ref), best, second)
    write_sums(acc_ref, tt_ref, diag, r, c, copies_ref)


def second_top_kernel(*refs):
    copies_ref, bs_ref, levels_ref, b_ref, s_rep, s, refs = *refs[:5], refs[5:9], refs[9:]
    out_ref, half_ref, tt_ref, m1_ref, m2_ref = refs
    r, c = place()
    join_sums(copies_ref, tt_ref)
    for n in range(BLOCKS):
        half_ref[n] = jnp.broadcast_to(0.5 * tt_ref[pl.ds(block_of(n, r), 1), :], (8, LANES))

    def body(t, carry):
        rows = pl.ds(pl.multiple_of(t * TILE, TILE), TILE)
        b = b_ref[rows, :]
        v = 0.25 * (b - s_rep[rows, :])
        top = (jnp.full((TILE, LANES), 2 * HOLE, F32), jnp.full((TILE, LANES), 2 * HOLE, F32))
        for n in range(BLOCKS):
            x = s[n // 8][n % 8, rows, :]
            half = jnp.tile(half_ref[n], (TILE // 8, 1))
            top = insert(top, x + jnp.minimum(0.0, half - jnp.where(x >= b, v, 0.0)))
        m1_ref[rows, :] = top[0]
        m2_ref[rows, :] = top[1]
        return carry

    lax.fori_loop(0, ROWS // TILE, body, 0)
    pref = preference(levels_ref)
    diag = first_diagonal(pref, bs_ref[0:4, :], bs_ref[4:8, :])
    entry = 0.5 * (diagonal_sums(tt_ref, r) - diag) + pref
    entry = jnp.where(has_diagonal(r, c) > 0.0, entry, 2 * HOLE)
    store_pair(out_ref, insert(compact(m1_ref, m2_ref), entry))


def eye_of(j_half):
    i = lax.broadcasted_iota(jnp.int32, (TILE, LANES), 0) + j_half * TILE
    return i == lax.broadcasted_iota(jnp.int32, (TILE, LANES), 1)


def second_sums_kernel(*refs):
    pieces, sum_ref, bs_ref, levels_ref, half_ref, b_ref, s_rep, s, refs = (
        refs[:4], *refs[4:10], refs[10:14], refs[14:])
    out_hbm, copies_ref, out_ref, diag_ref, b2_ref, s2_ref, acc_ref, tt_ref, dd_ref, sem = refs
    r, c = place()
    best2, second2 = merged(pieces)
    spread(best2, b2_ref)
    spread(second2, s2_ref)
    pref = preference(levels_ref)
    diag1 = first_diagonal(pref, bs_ref[0:4, :], bs_ref[4:8, :])
    avail1 = 0.5 * (diagonal_sums(sum_ref, r) - diag1)
    entry = avail1 + pref
    diag2 = 0.5 * diag1 + 0.5 * (pref - jnp.where(entry >= best2, second2, best2))
    store_pair(diag_ref, (avail1, diag2))
    for j in range(4):
        dd_ref[j] = jnp.broadcast_to(diag2[j : j + 1, :], (8, LANES))
    acc_ref[...] = jnp.zeros_like(acc_ref)
    inside = r // 8 == c

    def copy(t):
        rows = pl.ds(pl.multiple_of(t * TILE, TILE), TILE)
        return pltpu.make_async_copy(out_ref.at[rows, :], out_hbm.at[rows, :], sem.at[t])

    def body(t, carry):
        rows = pl.ds(pl.multiple_of(t * TILE, TILE), TILE)
        b = b_ref[rows, :]
        s1 = s_rep[rows, :]
        b2 = b2_ref[rows, :]
        s2 = s2_ref[rows, :]
        v = 0.25 * (b - s1)
        bq, sq, bh, sh = 0.25 * b, 0.25 * s1, 0.5 * b2, 0.5 * s2
        for n in range(BLOCKS):
            x = s[n // 8][n % 8, rows, :]
            half = jnp.tile(half_ref[n], (TILE // 8, 1))
            hit = x >= b
            entry = x + jnp.minimum(0.0, half - jnp.where(hit, v, 0.0))
            fresh = 0.75 * x - jnp.where(hit, sq, bq) - jnp.where(entry >= b2, sh, bh)
            out_ref[rows, pl.ds(pl.multiple_of(block_of(n, r) * LANES, LANES), LANES)] = fresh
            acc_ref[n] += jnp.sum(jnp.maximum(fresh, 0.0).reshape(TILE // 8, 8, LANES), axis=0)

        @pl.when(inside)
        def _():
            at = pl.ds(pl.multiple_of((4 * (r % 8) + t // 2) * LANES, LANES), LANES)
            value = jnp.tile(dd_ref[t // 2], (TILE // 8, 1))
            out_ref[rows, at] = jnp.where(eye_of(t % 2), value, out_ref[rows, at])

        copy(t).start()
        return carry

    lax.fori_loop(0, ROWS // TILE, body, 0)
    write_sums(acc_ref, tt_ref, diag2, r, c, copies_ref)
    for t in range(ROWS // TILE):
        copy(t).wait()


def last_kernel(*refs):
    copies_ref, resp_ref, diag_ref, half_ref, b_ref, s_rep, s, refs = *refs[:6], refs[6:10], refs[10:]
    out_hbm, out_ref, half2_ref, tt_ref, dd_ref, sem = refs
    r, c = place()
    join_sums(copies_ref, tt_ref)
    for n in range(BLOCKS):
        half2_ref[n] = jnp.broadcast_to(0.5 * tt_ref[pl.ds(block_of(n, r), 1), :], (8, LANES))
    diag = 0.5 * diag_ref[0:4, :] + 0.5 * (diagonal_sums(tt_ref, r) - diag_ref[4:8, :])
    for j in range(4):
        dd_ref[j] = jnp.broadcast_to(diag[j : j + 1, :], (8, LANES))
    inside = r // 8 == c

    def copy(t):
        rows = pl.ds(pl.multiple_of(t * TILE, TILE), TILE)
        return pltpu.make_async_copy(out_ref.at[rows, :], out_hbm.at[rows, :], sem.at[t])

    def body(t, carry):
        rows = pl.ds(pl.multiple_of(t * TILE, TILE), TILE)
        b = b_ref[rows, :]
        v = 0.25 * (b - s_rep[rows, :])
        for n in range(BLOCKS):
            at = pl.ds(pl.multiple_of(block_of(n, r) * LANES, LANES), LANES)
            x = s[n // 8][n % 8, rows, :]
            half = jnp.tile(half_ref[n], (TILE // 8, 1))
            half2 = jnp.tile(half2_ref[n], (TILE // 8, 1))
            before = jnp.minimum(0.0, half - jnp.where(x >= b, v, 0.0))
            renewed = jnp.minimum(0.0, half2 - 0.5 * jnp.maximum(resp_ref[rows, at], 0.0))
            out_ref[rows, at] = 0.5 * before + renewed

        @pl.when(inside)
        def _():
            at = pl.ds(pl.multiple_of((4 * (r % 8) + t // 2) * LANES, LANES), LANES)
            value = jnp.tile(dd_ref[t // 2], (TILE // 8, 1))
            out_ref[rows, at] = jnp.where(eye_of(t % 2), value, out_ref[rows, at])

        copy(t).start()
        return carry

    lax.fori_loop(0, ROWS // TILE, body, 0)
    for t in range(ROWS // TILE):
        copy(t).wait()


def call(kernel, args, outs, scratch=(), megabytes=4):
    vmem = pl.BlockSpec(memory_space=pltpu.VMEM)
    any_space = pl.BlockSpec(memory_space=pl.ANY)
    shapes, specs = [], []
    for shape, where in outs:
        shapes.append(jax.ShapeDtypeStruct(shape, F32) if where == "hbm" else pltpu.VMEM(shape, F32))
        specs.append(any_space if where == "hbm" else vmem)
    args = [pltpu.with_memory_space_constraint(a, pltpu.VMEM) for a in args]
    return pl.pallas_call(
        kernel,
        out_shape=tuple(shapes),
        in_specs=[vmem] * len(args),
        out_specs=tuple(specs),
        scratch_shapes=list(scratch),
        compiler_params=pltpu.CompilerParams(vmem_limit_bytes=megabytes * 2**20),
    )(*args)


def exchange(pair):
    return [pair] + [permute(pair, col_shift(k)) for k in (1, 3, 2)]


def to_all_rows(copies):
    return lax.all_to_all(copies, "row", 0, 0, tiled=True)


def propagate(embeddings, levels):
    levels = levels.reshape(4, LANES)
    unit = call(unit_kernel, [embeddings], [((SHARD, D), "vmem")])[0]
    mine = permute(unit, to_row_block())
    line = [unit] + [permute(unit, plane_shift(k, 1)) for k in (1, 2, 3)]
    line = jnp.concatenate(line, axis=0)
    rows = [mine] + [permute(mine, col_shift(k)) for k in (1, 2, 3)]
    own = {0: line}
    for k in (1, 3, 2):
        own[k] = permute(line, plane_shift(k, 2))
    similar, top = {}, ()
    running = [((ROWS, LANES), "vmem")] * 2
    pair = ((8, LANES), "vmem")
    s_out = ((8, ROWS, LANES), "vmem")
    big = pltpu.VMEM((ROWS, LANES), F32)
    for k in (0, 1, 3, 2):
        partner = permute(own[k], core_swap())
        first, last = k == 0, k == 2
        args = rows + [own[k], partner, *top] + ([levels] if last else [])
        outs = [s_out] + ([pair] if last else running)
        scratch = [pltpu.VMEM((ROWS, D), jnp.bfloat16)] * 2 + ([big] * 2 if last else [])
        similar[k], *top = call(make_product_kernel(k, first, last), args, outs, scratch)
    pieces = exchange(top[0])
    s = [similar[k] for k in range(4)]
    rep = ((ROWS, LANES), "vmem")
    sums = ((BLOCKS, 8, LANES), "vmem")
    flat = ((BLOCKS, LANES), "vmem")
    copies = ((N_ROW * BLOCKS, LANES), "vmem")
    acc, tt = pltpu.VMEM((BLOCKS, 8, LANES), F32), pltpu.VMEM((BLOCKS, LANES), F32)
    small = pltpu.VMEM((4, 8, LANES), F32)
    first, bs, b_rep, s_rep = call(first_sums_kernel, pieces + [levels, *s], [copies, pair, rep, rep], [acc, tt])
    bs2, halves, first = call(
        second_top_kernel, [to_all_rows(first), bs, levels, b_rep, s_rep, *s], [pair, sums, flat], [big, big]
    )
    pieces = exchange(bs2)
    n_copies = ROWS // TILE
    out = ((ROWS, BLOCKS * LANES), "hbm")
    kept = ((ROWS, BLOCKS * LANES), "vmem")
    responsibility, second, resp, diag = call(
        second_sums_kernel,
        pieces + [first, bs, levels, halves, b_rep, s_rep, *s],
        [out, copies, kept, pair],
        [big, big, acc, tt, small, pltpu.SemaphoreType.DMA((n_copies,))],
    )
    availability = call(
        last_kernel,
        [to_all_rows(second), resp, diag, halves, b_rep, s_rep, *s],
        [out],
        [pltpu.VMEM((ROWS, BLOCKS * LANES), F32), acc, tt, small, pltpu.SemaphoreType.DMA((n_copies,))],
        megabytes=12,
    )[0]
    return responsibility, availability


def solution(mesh):
    placed = (P(("col", "row"), None), P("row"))
    return jax.shard_map(
        propagate,
        mesh=mesh,
        in_specs=placed,
        out_specs=(P("row", "col"), P("row", "col")),
        check_vma=False,
    )
```

profile of v0, /device:TPU:1, one launch (start us, length us, event | category | flops | bytes accessed | tf_op | source)
XLA Modules:
  0.0 130.2 jit_solution(10345048535571619328)
XLA Ops:
  0.6 0.9 copy-done
  1.5 0.1 shard_map.41
  1.6 3.6 %collective-permute-start.6 = (f32[128,256]{1,0:T(8,128)S(1)}, f32[128,256]{1,0:T(8,128)S(1)}, u32[]{:S(2)}, u32[]{:S(2)}) collective-permute-start(f32[128,256]{1,0:T(8,128)S(1)} %shard_map.41), channel_id=1, source_target_pairs={{0,24},{1,25},{2,26},{3,27},{4,100},{5,101},{6,102},{7,103},{8,0},... | collective-permute-start | bytes 393224 | tf_op jit(solution)/shard_map/ppermute | solution.py:58
  5.3 0.3 collective-permute-start.5
  5.6 0.7 collective-permute-start.4
  6.3 2.3 %collective-permute-done.6 = f32[128,256]{1,0:T(8,128)S(1)} collective-permute-done((f32[128,256]{1,0:T(8,128)S(1)}, f32[128,256]{1,0:T(8,128)S(1)}, u32[]{:S(2)}, u32[]{:S(2)}) %collective-permute-start.6) | collective-permute-done | bytes 131104 | tf_op jit(solution)/shard_map/ppermute | solution.py:58
  8.6 2.3 %collective-permute-done.5 = f32[128,256]{1,0:T(8,128)S(1)} collective-permute-done((f32[128,256]{1,0:T(8,128)S(1)}, f32[128,256]{1,0:T(8,128)S(1)}, u32[]{:S(2)}, u32[]{:S(2)}) %collective-permute-start.5) | collective-permute-done | bytes 131104 | tf_op jit(solution)/shard_map/ppermute | solution.py:58
  10.9 1.4 %collective-permute-done.4 = f32[128,256]{1,0:T(8,128)S(1)} collective-permute-done((f32[128,256]{1,0:T(8,128)S(1)}, f32[128,256]{1,0:T(8,128)S(1)}, u32[]{:S(2)}, u32[]{:S(2)}) %collective-permute-start.4) | collective-permute-done | bytes 131104 | tf_op jit(solution)/shard_map/ppermute | solution.py:58
  12.3 1.0 collective-permute-start.11
  13.3 1.8 %collective-permute-start.9 = (f32[512,256]{1,0:T(8,128)S(1)}, f32[512,256]{1,0:T(8,128)S(1)}, u32[]{:S(2)}, u32[]{:S(2)}) collective-permute-start(f32[512,256]{1,0:T(8,128)S(1)} %pad_maximum_fusion.refs_4_), channel_id=1, source_target_pairs={{0,96},{1,97},{2,98},{3,99},{4,28},{5,29},{6,30},{7,31},{8,104},{9... | collective-permute-start | bytes 1572872 | tf_op jit(solution)/shard_map/ppermute | solution.py:58
  15.1 1.2 collective-permute-start.7
  16.3 6.3 %collective-permute-start = (f32[128,256]{1,0:T(8,128)S(1)}, f32[128,256]{1,0:T(8,128)S(1)}, u32[]{:S(2)}, u32[]{:S(2)}) collective-permute-start(f32[128,256]{1,0:T(8,128)S(1)} %shard_map.41), channel_id=1, source_target_pairs={{0,0},{4,1},{8,2},{12,3},{16,4},{20,5},{24,6},{28,7},{32,8},{36,9}... | collective-permute-start | bytes 393224 | tf_op jit(solution)/shard_map/ppermute | solution.py:58
  22.6 0.1 collective-permute-start.13
  22.7 0.0 collective-permute-done.11.refs_4_
  22.7 1.6 %collective-permute-start.12 = (f32[512,256]{1,0:T(8,128)S(1)}, f32[512,256]{1,0:T(8,128)S(1)}, u32[]{:S(2)}, u32[]{:S(2)}) collective-permute-start(f32[512,256]{1,0:T(8,128)S(1)} %collective-permute-done.11.refs_4_), channel_id=1, source_target_pairs={{0,4},{1,5},{2,6},{3,7},{4,0},{5,1},{6,2},{7,3},{8,12},{9,13},{10,... | collective-permute-start | bytes 1572872 | tf_op jit(solution)/shard_map/ppermute | solution.py:58
  24.3 2.5 %collective-permute-done.9.refs_4_ = f32[512,256]{1,0:T(8,128)S(1)} collective-permute-done((f32[512,256]{1,0:T(8,128)S(1)}, f32[512,256]{1,0:T(8,128)S(1)}, u32[]{:S(2)}, u32[]{:S(2)}) %collective-permute-start.9) | collective-permute-done | bytes 524320 | tf_op jit(solution)/shard_map/ppermute | solution.py:58
  26.8 2.9 %collective-permute-done.7.refs_4_ = f32[512,256]{1,0:T(8,128)S(1)} collective-permute-done((f32[512,256]{1,0:T(8,128)S(1)}, f32[512,256]{1,0:T(8,128)S(1)}, u32[]{:S(2)}, u32[]{:S(2)}) %collective-permute-start.7) | collective-permute-done | bytes 524320 | tf_op jit(solution)/shard_map/ppermute | solution.py:58
  29.7 1.5 %collective-permute-start.8 = (f32[512,256]{1,0:T(8,128)S(1)}, f32[512,256]{1,0:T(8,128)S(1)}, u32[]{:S(2)}, u32[]{:S(2)}) collective-permute-start(f32[512,256]{1,0:T(8,128)S(1)} %collective-permute-done.7.refs_4_), channel_id=1, source_target_pairs={{0,4},{1,5},{2,6},{3,7},{4,0},{5,1},{6,2},{7,3},{8,12},{9,13},{10,... | collective-permute-start | bytes 1572872 | tf_op jit(solution)/shard_map/ppermute | solution.py:58
  31.2 12.0 %collective-permute-start.3 = (f32[128,256]{1,0:T(8,128)S(1)}, f32[128,256]{1,0:T(8,128)S(1)}, u32[]{:S(2)}, u32[]{:S(2)}) collective-permute-start(f32[128,256]{1,0:T(8,128)S(1)} %collective-permute-done.refs_0_), channel_id=1, source_target_pairs={{0,3},{1,0},{2,1},{3,2},{4,7},{5,4},{6,5},{7,6},{8,11},{9,8},{10,9... | collective-permute-start | bytes 393224 | tf_op jit(solution)/shard_map/ppermute | solution.py:58
  43.2 1.9 %collective-permute-done.3.refs_3_ = f32[128,256]{1,0:T(8,128)S(1)} collective-permute-done((f32[128,256]{1,0:T(8,128)S(1)}, f32[128,256]{1,0:T(8,128)S(1)}, u32[]{:S(2)}, u32[]{:S(2)}) %collective-permute-start.3) | collective-permute-done | bytes 131104 | tf_op jit(solution)/shard_map/ppermute | solution.py:58
  45.1 1.6 %collective-permute-start.2 = (f32[128,256]{1,0:T(8,128)S(1)}, f32[128,256]{1,0:T(8,128)S(1)}, u32[]{:S(2)}, u32[]{:S(2)}) collective-permute-start(f32[128,256]{1,0:T(8,128)S(1)} %collective-permute-done.refs_0_), channel_id=1, source_target_pairs={{0,2},{1,3},{2,0},{3,1},{4,6},{5,7},{6,4},{7,5},{8,10},{9,11},{10,... | collective-permute-start | bytes 393224 | tf_op jit(solution)/shard_map/ppermute | solution.py:58
  46.7 3.7 %collective-permute-done.2.refs_2_ = f32[128,256]{1,0:T(8,128)S(1)} collective-permute-done((f32[128,256]{1,0:T(8,128)S(1)}, f32[128,256]{1,0:T(8,128)S(1)}, u32[]{:S(2)}, u32[]{:S(2)}) %collective-permute-start.2) | collective-permute-done | bytes 131104 | tf_op jit(solution)/shard_map/ppermute | solution.py:58
  50.4 0.7 collective-permute-start.1
  51.1 4.7 %collective-permute-done.1.refs_1_ = f32[128,256]{1,0:T(8,128)S(1)} collective-permute-done((f32[128,256]{1,0:T(8,128)S(1)}, f32[128,256]{1,0:T(8,128)S(1)}, u32[]{:S(2)}, u32[]{:S(2)}) %collective-permute-start.1) | collective-permute-done | bytes 131104 | tf_op jit(solution)/shard_map/ppermute | solution.py:58
  55.9 0.0 collective-permute-done.13.refs_5_
  55.9 2.2 %shard_map.42 = (f32[8,512,128]{2,1,0:T(8,128)S(1)}, f32[512,128]{1,0:T(8,128)S(1)}, f32[512,128]{1,0:T(8,128)S(1)}) custom-call(f32[128,256]{1,0:T(8,128)S(1)} %collective-permute-done.refs_0_, f32[128,256]{1,0:T(8,128)S(1)} %collective-permute-done.1.refs_1_, f32[128,256]{1,0:T(8,128)S(1)} %collective-permute-done.2.refs_2_, ...), custom_call_target="tpu_custom_call" | custom-call | tf_op jit(solution)/shard_map/pallas_call | solution.py:377
  58.1 0.0 collective-permute-done.12.refs_5_
  58.1 0.0 copy-start.1
  58.1 2.2 %shard_map.43 = (f32[8,512,128]{2,1,0:T(8,128)S(1)}, f32[512,128]{1,0:T(8,128)S(1)}, f32[512,128]{1,0:T(8,128)S(1)}) custom-call(f32[128,256]{1,0:T(8,128)S(1)} %collective-permute-done.refs_0_, f32[128,256]{1,0:T(8,128)S(1)} %collective-permute-done.1.refs_1_, f32[128,256]{1,0:T(8,128)S(1)} %collective-permute-done.2.refs_2_, ...), custom_call_target="tpu_custom_call" | custom-call | tf_op jit(solution)/shard_map/pallas_call | solution.py:377
  60.4 2.3 %shard_map.44 = (f32[8,512,128]{2,1,0:T(8,128)S(1)}, f32[512,128]{1,0:T(8,128)S(1)}, f32[512,128]{1,0:T(8,128)S(1)}) custom-call(f32[128,256]{1,0:T(8,128)S(1)} %collective-permute-done.refs_0_, f32[128,256]{1,0:T(8,128)S(1)} %collective-permute-done.1.refs_1_, f32[128,256]{1,0:T(8,128)S(1)} %collective-permute-done.2.refs_2_, ...), custom_call_target="tpu_custom_call" | custom-call | tf_op jit(solution)/shard_map/pallas_call | solution.py:377
  62.7 2.3 %shard_map.45 = (f32[8,512,128]{2,1,0:T(8,128)S(1)}, f32[8,128]{1,0:T(8,128)S(1)}) custom-call(f32[128,256]{1,0:T(8,128)S(1)} %collective-permute-done.refs_0_, f32[128,256]{1,0:T(8,128)S(1)} %collective-permute-done.1.refs_1_, f32[128,256]{1,0:T(8,128)S(1)} %collective-permute-done.2.refs_2_, f32[128,256]{1,0:T(8,128)S(1)} %collective-permute-done.3.refs_3_, ...), custom_call_target="tpu_custom_call" | custom-call | tf_op jit(solution)/shard_map/pallas_call | solution.py:377
  65.0 0.9 collective-permute-start.16
  65.8 0.8 collective-permute-start.15
  66.6 0.7 collective-permute-start.14
  67.3 1.7 %collective-permute-done.16.refs_3_ = f32[8,128]{1,0:T(8,128)S(1)} collective-permute-done((f32[8,128]{1,0:T(8,128)S(1)}, f32[8,128]{1,0:T(8,128)S(1)}, u32[]{:S(2)}, u32[]{:S(2)}) %collective-permute-start.16) | collective-permute-done | bytes 4128 | tf_op jit(solution)/shard_map/ppermute | solution.py:58
  69.0 0.0 collective-permute-done.15.refs_2_
  69.0 1.2 collective-permute-done.14.refs_1_
  70.3 1.3 %shard_map.46 = (f32[1024,128]{1,0:T(8,128)S(1)}, f32[8,128]{1,0:T(8,128)S(1)}, f32[512,128]{1,0:T(8,128)S(1)}, f32[512,128]{1,0:T(8,128)S(1)}) custom-call(f32[8,128]{1,0:T(8,128)S(1)} %get-tuple-element.30.refs_0_, f32[8,128]{1,0:T(8,128)S(1)} %collective-permute-done.14.refs_1_, f32[8,128]{1,0:T(8,128)S(1)} %collective-permute-done.15.refs_2_, ...), custom_call_target="tpu_custom_call" | custom-call | tf_op jit(solution)/shard_map/pallas_call | solution.py:377
  71.6 23.4 %all_to_all.22 = f32[32,32,128]{2,1,0:T(8,128)S(1)} all-to-all(f32[32,32,128]{2,1,0:T(8,128)S(1)} %bitcast.8), channel_id=1, replica_groups=mesh['row'=32,'col'=4] {'row'}, dimensions={0} | all-to-all | bytes 1048576 | tf_op jit(solution)/shard_map/all_to_all | solution.py:392
  95.0 2.9 %shard_map.47 = (f32[8,128]{1,0:T(8,128)S(1)}, f32[32,8,128]{2,1,0:T(8,128)S(1)}, f32[32,128]{1,0:T(8,128)S(1)}) custom-call(f32[1024,128]{1,0:T(8,128)S(1)} %bitcast.6, f32[8,128]{1,0:T(8,128)S(1)} %get-tuple-element.36.refs_1_.refs_5_, s32[4,128]{1,0:T(4,128)S(1)} %bitcast.11, f32[512,128]{1,0:T(8,128)S(1)} %get-tuple-element.37.refs_3_.refs_8_.refs_4_, ...), custom_call_target="tpu_custom_call" | custom-call | tf_op jit(solution)/shard_map/pallas_call | solution.py:377
  97.8 0.7 collective-permute-start.19
  98.5 1.0 collective-permute-start.18
  99.5 0.5 collective-permute-start.17
  100.0 1.9 %collective-permute-done.19.refs_3_ = f32[8,128]{1,0:T(8,128)S(1)} collective-permute-done((f32[8,128]{1,0:T(8,128)S(1)}, f32[8,128]{1,0:T(8,128)S(1)}, u32[]{:S(2)}, u32[]{:S(2)}) %collective-permute-start.19) | collective-permute-done | bytes 4128 | tf_op jit(solution)/shard_map/ppermute | solution.py:58
  101.9 1.2 collective-permute-done.17.refs_1_
  103.1 6.1 %shard_map.48 = (f32[512,4096]{1,0:T(8,128)}, f32[1024,128]{1,0:T(8,128)S(1)}, f32[512,4096]{1,0:T(8,128)S(1)}, f32[8,128]{1,0:T(8,128)S(1)}) custom-call(f32[8,128]{1,0:T(8,128)S(1)} %get-tuple-element.39.refs_0_, f32[8,128]{1,0:T(8,128)S(1)} %collective-permute-done.17.refs_1_, f32[8,128]{1,0:T(8,128)S(1)} %collective-permute-done.18.refs_2_, ...), custom_call_target="tpu_custom_call" | custom-call | tf_op jit(solution)/shard_map/pallas_call | solution.py:377
  109.3 16.7 %all_to_all.23 = f32[32,32,128]{2,1,0:T(8,128)S(1)} all-to-all(f32[32,32,128]{2,1,0:T(8,128)S(1)} %bitcast.7), channel_id=1, replica_groups=mesh['row'=32,'col'=4] {'row'}, dimensions={0} | all-to-all | bytes 1048576 | tf_op jit(solution)/shard_map/all_to_all | solution.py:392
  126.0 4.1 %shard_map.49 = f32[512,4096]{1,0:T(8,128)} custom-call(f32[1024,128]{1,0:T(8,128)S(1)} %bitcast.5, f32[512,4096]{1,0:T(8,128)S(1)} %get-tuple-element.44.refs_1_, f32[8,128]{1,0:T(8,128)S(1)} %get-tuple-element.45.refs_2_, f32[32,8,128]{2,1,0:T(8,128)S(1)} %get-tuple-element.41.refs_7_.refs_3_, f32[512,128]{1,0:T(8,128)S(1)} %get-tuple-element.37.refs_3_.refs_8_.refs_4_, ...), custom_call_target="tpu_custom_call" | custom-call | tf_op jit(solution)/shard_map/pallas_call | solution.py:377
  (8 shorter events, 0.1 us)
Async XLA Ops:
  0.6 0.9 copy-start
  1.6 6.9 %collective-permute-start.6 = (f32[128,256]{1,0:T(8,128)S(1)}, f32[128,256]{1,0:T(8,128)S(1)}, u32[]{:S(2)}, u32[]{:S(2)}) collective-permute-start(f32[128,256]{1,0:T(8,128)S(1)} %shard_map.41), channel_id=1, source_target_pairs={{0,24},{1,25},{2,26},{3,27},{4,100},{5,101},{6,102},{7,103},{8,0},... | collective-permute-start | bytes 393224 | tf_op jit(solution)/shard_map/ppermute | solution.py:58
  5.3 5.6 %collective-permute-start.5 = (f32[128,256]{1,0:T(8,128)S(1)}, f32[128,256]{1,0:T(8,128)S(1)}, u32[]{:S(2)}, u32[]{:S(2)}) collective-permute-start(f32[128,256]{1,0:T(8,128)S(1)} %shard_map.41), channel_id=1, source_target_pairs={{0,16},{1,17},{2,18},{3,19},{4,68},{5,69},{6,70},{7,71},{8,24},{9,... | collective-permute-start | bytes 393224 | tf_op jit(solution)/shard_map/ppermute | solution.py:58
  5.6 6.7 %collective-permute-start.4 = (f32[128,256]{1,0:T(8,128)S(1)}, f32[128,256]{1,0:T(8,128)S(1)}, u32[]{:S(2)}, u32[]{:S(2)}) collective-permute-start(f32[128,256]{1,0:T(8,128)S(1)} %shard_map.41), channel_id=1, source_target_pairs={{0,8},{1,9},{2,10},{3,11},{4,36},{5,37},{6,38},{7,39},{8,16},{9,17... | collective-permute-start | bytes 393224 | tf_op jit(solution)/shard_map/ppermute | solution.py:58
  12.3 10.4 %collective-permute-start.11 = (f32[512,256]{1,0:T(8,128)S(1)}, f32[512,256]{1,0:T(8,128)S(1)}, u32[]{:S(2)}, u32[]{:S(2)}) collective-permute-start(f32[512,256]{1,0:T(8,128)S(1)} %pad_maximum_fusion.refs_4_), channel_id=1, source_target_pairs={{0,32},{1,33},{2,34},{3,35},{4,12},{5,13},{6,14},{7,15},{8,40},{9,... | collective-permute-start | bytes 1572872 | tf_op jit(solution)/shard_map/ppermute | solution.py:58
  13.3 13.5 %collective-permute-start.9 = (f32[512,256]{1,0:T(8,128)S(1)}, f32[512,256]{1,0:T(8,128)S(1)}, u32[]{:S(2)}, u32[]{:S(2)}) collective-permute-start(f32[512,256]{1,0:T(8,128)S(1)} %pad_maximum_fusion.refs_4_), channel_id=1, source_target_pairs={{0,96},{1,97},{2,98},{3,99},{4,28},{5,29},{6,30},{7,31},{8,104},{9... | collective-permute-start | bytes 1572872 | tf_op jit(solution)/shard_map/ppermute | solution.py:58
  15.1 14.6 %collective-permute-start.7 = (f32[512,256]{1,0:T(8,128)S(1)}, f32[512,256]{1,0:T(8,128)S(1)}, u32[]{:S(2)}, u32[]{:S(2)}) collective-permute-start(f32[512,256]{1,0:T(8,128)S(1)} %pad_maximum_fusion.refs_4_), channel_id=1, source_target_pairs={{0,64},{1,65},{2,66},{3,67},{4,20},{5,21},{6,22},{7,23},{8,72},{9,... | collective-permute-start | bytes 1572872 | tf_op jit(solution)/shard_map/ppermute | solution.py:58
  16.3 14.9 %collective-permute-start = (f32[128,256]{1,0:T(8,128)S(1)}, f32[128,256]{1,0:T(8,128)S(1)}, u32[]{:S(2)}, u32[]{:S(2)}) collective-permute-start(f32[128,256]{1,0:T(8,128)S(1)} %shard_map.41), channel_id=1, source_target_pairs={{0,0},{4,1},{8,2},{12,3},{16,4},{20,5},{24,6},{28,7},{32,8},{36,9}... | collective-permute-start | bytes 393224 | tf_op jit(solution)/shard_map/ppermute | solution.py:58
  22.6 33.3 %collective-permute-start.13 = (f32[512,256]{1,0:T(8,128)S(1)}, f32[512,256]{1,0:T(8,128)S(1)}, u32[]{:S(2)}, u32[]{:S(2)}) collective-permute-start(f32[512,256]{1,0:T(8,128)S(1)} %pad_maximum_fusion.refs_4_), channel_id=1, source_target_pairs={{0,4},{1,5},{2,6},{3,7},{4,0},{5,1},{6,2},{7,3},{8,12},{9,13},{10,... | collective-permute-start | bytes 1572872 | tf_op jit(solution)/shard_map/ppermute | solution.py:58
  22.7 35.4 %collective-permute-start.12 = (f32[512,256]{1,0:T(8,128)S(1)}, f32[512,256]{1,0:T(8,128)S(1)}, u32[]{:S(2)}, u32[]{:S(2)}) collective-permute-start(f32[512,256]{1,0:T(8,128)S(1)} %collective-permute-done.11.refs_4_), channel_id=1, source_target_pairs={{0,4},{1,5},{2,6},{3,7},{4,0},{5,1},{6,2},{7,3},{8,12},{9,13},{10,... | collective-permute-start | bytes 1572872 | tf_op jit(solution)/shard_map/ppermute | solution.py:58
  26.8 33.6 %collective-permute-start.10 = (f32[512,256]{1,0:T(8,128)S(1)}, f32[512,256]{1,0:T(8,128)S(1)}, u32[]{:S(2)}, u32[]{:S(2)}) collective-permute-start(f32[512,256]{1,0:T(8,128)S(1)} %collective-permute-done.9.refs_4_), channel_id=1, source_target_pairs={{0,4},{1,5},{2,6},{3,7},{4,0},{5,1},{6,2},{7,3},{8,12},{9,13},{10,... | collective-permute-start | bytes 1572872 | tf_op jit(solution)/shard_map/ppermute | solution.py:58
  29.7 33.0 %collective-permute-start.8 = (f32[512,256]{1,0:T(8,128)S(1)}, f32[512,256]{1,0:T(8,128)S(1)}, u32[]{:S(2)}, u32[]{:S(2)}) collective-permute-start(f32[512,256]{1,0:T(8,128)S(1)} %collective-permute-done.7.refs_4_), channel_id=1, source_target_pairs={{0,4},{1,5},{2,6},{3,7},{4,0},{5,1},{6,2},{7,3},{8,12},{9,13},{10,... | collective-permute-start | bytes 1572872 | tf_op jit(solution)/shard_map/ppermute | solution.py:58
  31.2 13.9 %collective-permute-start.3 = (f32[128,256]{1,0:T(8,128)S(1)}, f32[128,256]{1,0:T(8,128)S(1)}, u32[]{:S(2)}, u32[]{:S(2)}) collective-permute-start(f32[128,256]{1,0:T(8,128)S(1)} %collective-permute-done.refs_0_), channel_id=1, source_target_pairs={{0,3},{1,0},{2,1},{3,2},{4,7},{5,4},{6,5},{7,6},{8,11},{9,8},{10,9... | collective-permute-start | bytes 393224 | tf_op jit(solution)/shard_map/ppermute | solution.py:58
  45.1 5.3 %collective-permute-start.2 = (f32[128,256]{1,0:T(8,128)S(1)}, f32[128,256]{1,0:T(8,128)S(1)}, u32[]{:S(2)}, u32[]{:S(2)}) collective-permute-start(f32[128,256]{1,0:T(8,128)S(1)} %collective-permute-done.refs_0_), channel_id=1, source_target_pairs={{0,2},{1,3},{2,0},{3,1},{4,6},{5,7},{6,4},{7,5},{8,10},{9,11},{10,... | collective-permute-start | bytes 393224 | tf_op jit(solution)/shard_map/ppermute | solution.py:58
  50.4 5.4 %collective-permute-start.1 = (f32[128,256]{1,0:T(8,128)S(1)}, f32[128,256]{1,0:T(8,128)S(1)}, u32[]{:S(2)}, u32[]{:S(2)}) collective-permute-start(f32[128,256]{1,0:T(8,128)S(1)} %collective-permute-done.refs_0_), channel_id=1, source_target_pairs={{0,1},{1,2},{2,3},{3,0},{4,5},{5,6},{6,7},{7,4},{8,9},{9,10},{10,1... | collective-permute-start | bytes 393224 | tf_op jit(solution)/shard_map/ppermute | solution.py:58
  58.1 4.5 %copy-start.1 = (s32[512]{0:T(512)S(1)}, s32[512]{0:T(512)}, u32[]{:S(2)}) copy-start(s32[512]{0:T(512)} %param.3) | copy-start | bytes 6148
  65.0 4.0 %collective-permute-start.16 = (f32[8,128]{1,0:T(8,128)S(1)}, f32[8,128]{1,0:T(8,128)S(1)}, u32[]{:S(2)}, u32[]{:S(2)}) collective-permute-start(f32[8,128]{1,0:T(8,128)S(1)} %get-tuple-element.30.refs_0_), channel_id=1, source_target_pairs={{0,2},{1,3},{2,0},{3,1},{4,6},{5,7},{6,4},{7,5},{8,10},{9,11},{10,... | collective-permute-start | bytes 12296 | tf_op jit(solution)/shard_map/ppermute | solution.py:58
  65.8 3.2 %collective-permute-start.15 = (f32[8,128]{1,0:T(8,128)S(1)}, f32[8,128]{1,0:T(8,128)S(1)}, u32[]{:S(2)}, u32[]{:S(2)}) collective-permute-start(f32[8,128]{1,0:T(8,128)S(1)} %get-tuple-element.30.refs_0_), channel_id=1, source_target_pairs={{0,3},{1,0},{2,1},{3,2},{4,7},{5,4},{6,5},{7,6},{8,11},{9,8},{10,9... | collective-permute-start | bytes 12296 | tf_op jit(solution)/shard_map/ppermute | solution.py:58
  66.6 3.7 %collective-permute-start.14 = (f32[8,128]{1,0:T(8,128)S(1)}, f32[8,128]{1,0:T(8,128)S(1)}, u32[]{:S(2)}, u32[]{:S(2)}) collective-permute-start(f32[8,128]{1,0:T(8,128)S(1)} %get-tuple-element.30.refs_0_), channel_id=1, source_target_pairs={{0,1},{1,2},{2,3},{3,0},{4,5},{5,6},{6,7},{7,4},{8,9},{9,10},{10,1... | collective-permute-start | bytes 12296 | tf_op jit(solution)/shard_map/ppermute | solution.py:58
  97.8 4.0 %collective-permute-start.19 = (f32[8,128]{1,0:T(8,128)S(1)}, f32[8,128]{1,0:T(8,128)S(1)}, u32[]{:S(2)}, u32[]{:S(2)}) collective-permute-start(f32[8,128]{1,0:T(8,128)S(1)} %get-tuple-element.39.refs_0_), channel_id=1, source_target_pairs={{0,2},{1,3},{2,0},{3,1},{4,6},{5,7},{6,4},{7,5},{8,10},{9,11},{10,... | collective-permute-start | bytes 12296 | tf_op jit(solution)/shard_map/ppermute | solution.py:58
  98.5 3.4 %collective-permute-start.18 = (f32[8,128]{1,0:T(8,128)S(1)}, f32[8,128]{1,0:T(8,128)S(1)}, u32[]{:S(2)}, u32[]{:S(2)}) collective-permute-start(f32[8,128]{1,0:T(8,128)S(1)} %get-tuple-element.39.refs_0_), channel_id=1, source_target_pairs={{0,3},{1,0},{2,1},{3,2},{4,7},{5,4},{6,5},{7,6},{8,11},{9,8},{10,9... | collective-permute-start | bytes 12296 | tf_op jit(solution)/shard_map/ppermute | solution.py:58
  99.5 3.7 %collective-permute-start.17 = (f32[8,128]{1,0:T(8,128)S(1)}, f32[8,128]{1,0:T(8,128)S(1)}, u32[]{:S(2)}, u32[]{:S(2)}) collective-permute-start(f32[8,128]{1,0:T(8,128)S(1)} %get-tuple-element.39.refs_0_), channel_id=1, source_target_pairs={{0,1},{1,2},{2,3},{3,0},{4,5},{5,6},{6,7},{7,4},{8,9},{9,10},{10,1... | collective-permute-start | bytes 12296 | tf_op jit(solution)/shard_map/ppermute | solution.py:58
where the time goes:
time: 130 us
  blocking collectives  40.1 us (31%)
  starting transfers between devices  36.9 us (28%)
  waiting for transfers between devices  27.9 us (21%)
  Pallas kernels  23.5 us (18%)
    all_to_all x2, blocking collectives, to_all_rows(): return lax.all_to_all(copies, 'row', 0, 0, tiled=True)  40.1 us
    ppermute x20, starting transfers between devices, permute(): return lax.ppermute(a, BOTH, perm)  36.9 us
    ppermute x20, waiting for transfers between devices, permute(): return lax.ppermute(a, BOTH, perm)  27.9 us
    pallas_call x9, Pallas kernels, call(): pl.pallas_call(kernel, out_shape=tuple(shapes), in_specs=[vmem] * len(arg...  23.5 us
  transfers between devices with their start and end apart: 20, of which 12 were waited for; matrix products, arithmetic and copies ran while one was open for 0% of the time, Pallas kernels for 5%

commit v1 on v0

v1 whole, which is shorter than its diff:
```python
import jax
import jax.numpy as jnp
from jax import lax
from jax.experimental import pallas as pl
from jax.experimental.pallas import tpu as pltpu
from jax.sharding import PartitionSpec as P


N_ROW, N_COL, SIDE, CHIPS = 32, 4, 4, 16
SHARD, ROWS, D, LANES = 128, 512, 256, 128
BLOCKS = 32
TILE = 64
HOLE = -1e30
BOTH = ("row", "col")
F32 = jnp.float32


def row_of(y, x, core):
    return (y * SIDE + x) * 2 + core


def pairs(target):
    out = []
    for r in range(N_ROW):
        for c in range(N_COL):
            y, x, core = r // 8, r // 2 % 4, r % 2
            to_y, to_x, to_core, to_c = target(y, x, core, c)
            out.append((r * N_COL + c, row_of(to_y, to_x, to_core) * N_COL + to_c))
    return out


def plane_shift(k, stage):
    def target(y, x, core, c):
        if (core == 0) == (stage == 1):
            return y, (x + k) % SIDE, core, c
        return (y + k) % SIDE, x, core, c

    return pairs(target)


def col_shift(k):
    return pairs(lambda y, x, core, c: (y, x, core, (c + k) % N_COL))


def core_swap():
    return pairs(lambda y, x, core, c: (y, x, 1 - core, c))


def to_row_block():
    out = []
    for r in range(N_ROW):
        for j in range(N_COL):
            out.append(((4 * (r % 8) + j) * N_COL + r // 8, r * N_COL + (j + r // 8 + r // 2 % 4) % 4))
    return out


def permute(a, perm):
    return lax.ppermute(a, BOTH, perm)


def place():
    r, c = lax.axis_index("row"), lax.axis_index("col")
    return r, c


def block_of(n, r):
    k, h, m = n // 8, n // 4 % 2, n % 4
    y, x, core = r // 8, r // 2 % 4, r % 2
    own = core if h == 0 else 1 - core
    a = jnp.where(own == 0, (x - m) % 4, (x - k) % 4)
    b = jnp.where(own == 0, (y - k) % 4, (y - m) % 4)
    return b * 8 + a * 2 + own


def has_diagonal(r, c):
    return jnp.where(r // 8 == c, 1.0, 0.0).astype(F32)


def merge(a, b):
    return jnp.maximum(a[0], b[0]), jnp.maximum(jnp.minimum(a[0], b[0]), jnp.maximum(a[1], b[1]))


def insert(top, x):
    return jnp.maximum(top[0], x), jnp.maximum(top[1], jnp.minimum(top[0], x))


def compact(m1_ref, m2_ref):
    best, second = [], []
    for j in range(4):
        p = (m1_ref[j * 128 : (j + 1) * 128, :].T, m2_ref[j * 128 : (j + 1) * 128, :].T)
        size = 128
        while size > 1:
            size //= 2
            p = merge((p[0][:size], p[1][:size]), (p[0][size:], p[1][size:]))
        best.append(p[0])
        second.append(p[1])
    return jnp.concatenate(best, 0), jnp.concatenate(second, 0)


def store_pair(ref, pair):
    ref[0:4, :] = pair[0]
    ref[4:8, :] = pair[1]


def merged(refs):
    top = (refs[0][0:4, :], refs[0][4:8, :])
    for ref in refs[1:]:
        top = merge(top, (ref[0:4, :], ref[4:8, :]))
    return top


def spread(compacted, ref):
    for j in range(4):
        ref[j * 128 : (j + 1) * 128, :] = jnp.broadcast_to(compacted[j : j + 1, :], (128, 128)).T


def first_diagonal(pref, best, second):
    return 0.5 * (pref - jnp.where(pref >= best, second, best))


def write_sums(acc_ref, tt_ref, diag, r, c, out_ref):
    for n in range(BLOCKS):
        tt_ref[pl.ds(block_of(n, r), 1), :] = jnp.sum(acc_ref[n], axis=0, keepdims=True)
    f = has_diagonal(r, c)
    for j in range(4):
        at = pl.ds(4 * (r % 8) + j, 1)
        tt_ref[at, :] = tt_ref[at, :] + f * diag[j : j + 1, :]
    out_ref[...] = tt_ref[...]


def join_sums(copies_ref, tt_ref):
    parts = [copies_ref[i * BLOCKS : (i + 1) * BLOCKS, :] for i in range(CHIPS)]
    while len(parts) > 1:
        parts = [p + q for p, q in zip(parts[::2], parts[1::2])]
    tt_ref[...] = parts[0]


def diagonal_sums(tt_ref, r):
    return jnp.concatenate([tt_ref[pl.ds(4 * (r % 8) + j, 1), :] for j in range(4)], 0)


def unit_kernel(x_ref, levels_ref, o_ref, pref_ref):
    pref_ref[...] = 0.25 * levels_ref[...].astype(F32) - 1.0
    x = x_ref[...]
    o_ref[...] = x * lax.rsqrt(jnp.sum(x * x, axis=1, keepdims=True) + 1e-06)


def split(x):
    high = x.astype(jnp.bfloat16)
    return high, (x - high.astype(F32)).astype(jnp.bfloat16)


def product(a, b):
    return lax.dot_general(a, b, (((1,), (1,)), ((), ())), preferred_element_type=F32)


def make_product_kernel(k, first, last):
    def kernel(*refs):
        refs = list(refs)
        take = lambda count: [refs.pop(0) for _ in range(count)]
        g = take(4) if first else None
        left = None if first else take(1)[0]
        own_ref, partner_ref = take(2)
        in1, in2 = (None, None) if first else take(2)
        pref_ref = take(1)[0] if last else None
        s_ref = take(1)[0]
        if first:
            left = take(1)[0]
        bs_ref = take(1)[0] if last else None
        m1_ref, m2_ref, p_ref = take(3)
        r, c = place()
        if first:
            for q in range(4):
                h, l = split(g[q][...])
                at = pl.ds(pl.multiple_of((c - q - r // 8 - r // 2 % 4) % 4 * 128, 128), 128)
                left[at, 0:D] = h
                left[at, D : 2 * D] = h
                left[at, 2 * D : 3 * D] = l
        f = has_diagonal(r, c)
        eye = lax.broadcasted_iota(jnp.int32, (128, 128), 0) == lax.broadcasted_iota(jnp.int32, (128, 128), 1)
        holes = jnp.where(eye, F32(HOLE), F32(0.0))
        for half, ref in enumerate((own_ref, partner_ref)):
            high, low = split(ref[...])
            right = jnp.concatenate([high, low, high], axis=1)
            p_ref[half] = product(left[...], right)
        for j in range(4):
            rows = slice(j * 128, (j + 1) * 128)
            if first:
                top = (jnp.full((128, 128), 2 * HOLE, F32), jnp.full((128, 128), 2 * HOLE, F32))
            else:
                top = (in1[rows, :], in2[rows, :])
            for n in range(8):
                here = f * jnp.where(block_of(8 * k + n, r) == 4 * (r % 8) + j, 1.0, 0.0).astype(F32)
                block = p_ref[n // 4, rows, n % 4 * 128 : (n % 4 + 1) * 128] + here * holes
                s_ref[n, rows, :] = block
                top = insert(top, block)
            m1_ref[rows, :] = top[0]
            m2_ref[rows, :] = top[1]
        if last:
            pair = compact(m1_ref, m2_ref)
            pref = jnp.where(f > 0.0, pref_ref[...], 2 * HOLE)
            store_pair(bs_ref, insert(pair, pref))

    return kernel


def first_sums_kernel(*refs):
    pieces, pref_ref, s, refs = refs[:4], refs[4], refs[5:9], refs[9:]
    sum_ref, bs_ref, b_ref, s_ref, acc_ref, tt_ref = refs
    r, c = place()
    best, second = merged(pieces)
    store_pair(bs_ref, (best, second))
    spread(best, b_ref)
    spread(second, s_ref)
    acc_ref[...] = jnp.zeros_like(acc_ref)

    def body(t, carry):
        rows = pl.ds(pl.multiple_of(t * TILE, TILE), TILE)
        b = b_ref[rows, :]
        v = 0.5 * (b - s_ref[rows, :])
        for n in range(BLOCKS):
            x = jnp.where(s[n // 8][n % 8, rows, :] >= b, v, 0.0)
            acc_ref[n] += jnp.sum(x.reshape(TILE // 8, 8, LANES), axis=0)
        return carry

    lax.fori_loop(0, ROWS // TILE, body, 0)
    diag = first_diagonal(pref_ref[...], best, second)
    write_sums(acc_ref, tt_ref, diag, r, c, sum_ref)


def copies_kernel(a_ref, b_ref, out_ref):
    both = a_ref[...] + b_ref[...]
    for i in range(CHIPS):
        out_ref[i * BLOCKS : (i + 1) * BLOCKS, :] = both


def second_top_kernel(*refs):
    copies_ref, bs_ref, pref_ref, b_ref, s_rep, s, refs = *refs[:5], refs[5:9], refs[9:]
    out_ref, entry_ref, tt_ref, half_ref, m1_ref, m2_ref = refs
    r, c = place()
    join_sums(copies_ref, tt_ref)
    for n in range(BLOCKS):
        half_ref[n] = jnp.broadcast_to(0.5 * tt_ref[pl.ds(block_of(n, r), 1), :], (8, LANES))

    def body(t, carry):
        rows = pl.ds(pl.multiple_of(t * TILE, TILE), TILE)
        b = b_ref[rows, :]
        v = 0.25 * (b - s_rep[rows, :])
        top = (jnp.full((TILE, LANES), 2 * HOLE, F32), jnp.full((TILE, LANES), 2 * HOLE, F32))
        for n in range(BLOCKS):
            x = s[n // 8][n % 8, rows, :]
            half = jnp.tile(half_ref[n], (TILE // 8, 1))
            entry = x + jnp.minimum(0.0, half - jnp.where(x >= b, v, 0.0))
            entry_ref[n, rows, :] = entry
            top = insert(top, entry)
        m1_ref[rows, :] = top[0]
        m2_ref[rows, :] = top[1]
        return carry

    lax.fori_loop(0, ROWS // TILE, body, 0)
    pref = pref_ref[...]
    diag = first_diagonal(pref, bs_ref[0:4, :], bs_ref[4:8, :])
    entry = 0.5 * (diagonal_sums(tt_ref, r) - diag) + pref
    entry = jnp.where(has_diagonal(r, c) > 0.0, entry, 2 * HOLE)
    store_pair(out_ref, insert(compact(m1_ref, m2_ref), entry))


def eye_of(j_half):
    i = lax.broadcasted_iota(jnp.int32, (TILE, LANES), 0) + j_half * TILE
    return i == lax.broadcasted_iota(jnp.int32, (TILE, LANES), 1)


def second_sums_kernel(*refs):
    pieces, sum_ref, bs_ref, pref_ref, entry_ref, b_ref, s_rep, s, refs = (
        refs[:4], *refs[4:10], refs[10:14], refs[14:])
    out_hbm, sum2_ref, out_ref, diag_ref, b2_ref, s2_ref, acc_ref, tt_ref, dd_ref, sem = refs
    r, c = place()
    best2, second2 = merged(pieces)
    spread(best2, b2_ref)
    spread(second2, s2_ref)
    pref = pref_ref[...]
    diag1 = first_diagonal(pref, bs_ref[0:4, :], bs_ref[4:8, :])
    avail1 = 0.5 * (diagonal_sums(sum_ref, r) - diag1)
    entry = avail1 + pref
    diag2 = 0.5 * diag1 + 0.5 * (pref - jnp.where(entry >= best2, second2, best2))
    store_pair(diag_ref, (avail1, diag2))
    for j in range(4):
        dd_ref[j] = jnp.broadcast_to(diag2[j : j + 1, :], (8, LANES))
    acc_ref[...] = jnp.zeros_like(acc_ref)
    inside = r // 8 == c

    def copy(t):
        rows = pl.ds(pl.multiple_of(t * TILE, TILE), TILE)
        return pltpu.make_async_copy(out_ref.at[rows, :], out_hbm.at[rows, :], sem.at[t])

    def body(t, carry):
        rows = pl.ds(pl.multiple_of(t * TILE, TILE), TILE)
        b, b2 = b_ref[rows, :], b2_ref[rows, :]
        v = 0.25 * (b - s_rep[rows, :])
        v2 = 0.5 * (b2 - s2_ref[rows, :])
        base = 0.25 * b + 0.5 * b2
        for n in range(BLOCKS):
            x = s[n // 8][n % 8, rows, :]
            gain = jnp.where(x >= b, v, 0.0) + jnp.where(entry_ref[n, rows, :] >= b2, v2, 0.0)
            fresh = (0.75 * x - base) + gain
            out_ref[rows, pl.ds(pl.multiple_of(block_of(n, r) * LANES, LANES), LANES)] = fresh
            acc_ref[n] += jnp.sum(jnp.maximum(fresh, 0.0).reshape(TILE // 8, 8, LANES), axis=0)

        @pl.when(inside)
        def _():
            at = pl.ds(pl.multiple_of((4 * (r % 8) + t // 2) * LANES, LANES), LANES)
            value = jnp.tile(dd_ref[t // 2], (TILE // 8, 1))
            out_ref[rows, at] = jnp.where(eye_of(t % 2), value, out_ref[rows, at])

        copy(t).start()
        return carry

    lax.fori_loop(0, ROWS // TILE, body, 0)
    write_sums(acc_ref, tt_ref, diag2, r, c, sum2_ref)
    for t in range(ROWS // TILE):
        copy(t).wait()


def last_kernel(*refs):
    copies_ref, resp_ref, diag_ref, entry_ref, s, refs = *refs[:4], refs[4:8], refs[8:]
    out_hbm, out_ref, total_ref, least_ref, tt_ref, dd_ref, sem = refs
    r, c = place()
    join_sums(copies_ref, tt_ref)
    for n in range(BLOCKS):
        total = jnp.broadcast_to(tt_ref[pl.ds(block_of(n, r), 1), :], (8, LANES))
        total_ref[n] = total
        least_ref[n] = jnp.minimum(0.0, total)
    diag = 0.5 * diag_ref[0:4, :] + 0.5 * (diagonal_sums(tt_ref, r) - diag_ref[4:8, :])
    for j in range(4):
        dd_ref[j] = jnp.broadcast_to(diag[j : j + 1, :], (8, LANES))
    inside = r // 8 == c

    def copy(t):
        rows = pl.ds(pl.multiple_of(t * TILE, TILE), TILE)
        return pltpu.make_async_copy(out_ref.at[rows, :], out_hbm.at[rows, :], sem.at[t])

    def body(t, carry):
        rows = pl.ds(pl.multiple_of(t * TILE, TILE), TILE)
        for n in range(BLOCKS):
            at = pl.ds(pl.multiple_of(block_of(n, r) * LANES, LANES), LANES)
            before = entry_ref[n, rows, :] - s[n // 8][n % 8, rows, :]
            total = jnp.tile(total_ref[n], (TILE // 8, 1))
            least = jnp.tile(least_ref[n], (TILE // 8, 1))
            out_ref[rows, at] = 0.5 * (before + jnp.minimum(least, total - resp_ref[rows, at]))

        @pl.when(inside)
        def _():
            at = pl.ds(pl.multiple_of((4 * (r % 8) + t // 2) * LANES, LANES), LANES)
            value = jnp.tile(dd_ref[t // 2], (TILE // 8, 1))
            out_ref[rows, at] = jnp.where(eye_of(t % 2), value, out_ref[rows, at])

        copy(t).start()
        return carry

    lax.fori_loop(0, ROWS // TILE, body, 0)
    for t in range(ROWS // TILE):
        copy(t).wait()


def call(kernel, args, outs, scratch=(), megabytes=4):
    vmem = pl.BlockSpec(memory_space=pltpu.VMEM)
    any_space = pl.BlockSpec(memory_space=pl.ANY)
    shapes, specs = [], []
    for shape, where in outs:
        dtype = jnp.bfloat16 if where == "bf16" else F32
        shapes.append(jax.ShapeDtypeStruct(shape, F32) if where == "hbm" else pltpu.VMEM(shape, dtype))
        specs.append(any_space if where == "hbm" else vmem)
    args = [pltpu.with_memory_space_constraint(a, pltpu.VMEM) for a in args]
    return pl.pallas_call(
        kernel,
        out_shape=tuple(shapes),
        in_specs=[vmem] * len(args),
        out_specs=tuple(specs),
        scratch_shapes=list(scratch),
        compiler_params=pltpu.CompilerParams(vmem_limit_bytes=megabytes * 2**20),
    )(*args)


def exchange(pair):
    return [pair] + [permute(pair, col_shift(k)) for k in (1, 3, 2)]


def to_all_rows(sums):
    copies = call(copies_kernel, [sums, permute(sums, core_swap())], [((CHIPS * BLOCKS, LANES), "vmem")])[0]
    groups = [[r for r in range(N_ROW) if r % 2 == core] for core in (0, 1)]
    return lax.all_to_all(copies, "row", 0, 0, tiled=True, axis_index_groups=groups)


def propagate(embeddings, levels):
    levels = levels.reshape(4, LANES)
    unit, pref = call(unit_kernel, [embeddings, levels], [((SHARD, D), "vmem"), ((4, LANES), "vmem")])
    mine = permute(unit, to_row_block())
    line = [unit] + [permute(unit, plane_shift(k, 1)) for k in (1, 2, 3)]
    line = jnp.concatenate(line, axis=0)
    rows = [mine] + [permute(mine, col_shift(k)) for k in (1, 2, 3)]
    own = {0: line}
    for k in (1, 3, 2):
        own[k] = permute(line, plane_shift(k, 2))
    similar = {}
    running = [((ROWS, LANES), "vmem")] * 2
    pair = ((8, LANES), "vmem")
    s_out = ((8, ROWS, LANES), "vmem")
    left_out = ((ROWS, 3 * D), "bf16")
    big = pltpu.VMEM((ROWS, LANES), F32)
    parts = pltpu.VMEM((2, ROWS, 4 * LANES), F32)
    for k in (0, 1, 3, 2):
        partner = permute(own[k], core_swap())
        first, last = k == 0, k == 2
        kernel = make_product_kernel(k, first, last)
        if first:
            similar[k], left, *top = call(kernel, rows + [own[k], partner], [s_out, left_out, *running], [parts])
        elif last:
            similar[k], pieces = call(kernel, [left, own[k], partner, *top, pref], [s_out, pair], [big, big, parts])
        else:
            similar[k], *top = call(kernel, [left, own[k], partner, *top], [s_out, *running], [parts])
    pieces = exchange(pieces)
    s = [similar[k] for k in range(4)]
    rep = ((ROWS, LANES), "vmem")
    flat = ((BLOCKS, LANES), "vmem")
    blocks = ((BLOCKS, ROWS, LANES), "vmem")
    acc, tt = pltpu.VMEM((BLOCKS, 8, LANES), F32), pltpu.VMEM((BLOCKS, LANES), F32)
    small = pltpu.VMEM((4, 8, LANES), F32)
    first, bs, b_rep, s_rep = call(first_sums_kernel, pieces + [pref, *s], [flat, pair, rep, rep], [acc, tt])
    bs2, entries, first = call(
        second_top_kernel, [to_all_rows(first), bs, pref, b_rep, s_rep, *s], [pair, blocks, flat], [acc, big, big]
    )
    pieces = exchange(bs2)
    n_copies = ROWS // TILE
    out = ((ROWS, BLOCKS * LANES), "hbm")
    kept = ((ROWS, BLOCKS * LANES), "vmem")
    responsibility, second, resp, diag = call(
        second_sums_kernel,
        pieces + [first, bs, pref, entries, b_rep, s_rep, *s],
        [out, flat, kept, pair],
        [big, big, acc, tt, small, pltpu.SemaphoreType.DMA((n_copies,))],
    )
    availability = call(
        last_kernel,
        [to_all_rows(second), resp, diag, entries, *s],
        [out],
        [pltpu.VMEM((ROWS, BLOCKS * LANES), F32), acc, acc, tt, small, pltpu.SemaphoreType.DMA((n_copies,))],
        megabytes=12,
    )[0]
    return responsibility, availability


def solution(mesh):
    placed = (P(("col", "row"), None), P("row"))
    return jax.shard_map(
        propagate,
        mesh=mesh,
        in_specs=placed,
        out_specs=(P("row", "col"), P("row", "col")),
        check_vma=False,
    )
```

time: 130 us -> 120 us (0.923)
  blocking collectives: 40.1 us -> 24.3 us
  starting transfers between devices: 36.9 us -> 48.2 us
  Pallas kernels: 23.5 us -> 17.3 us
    all_to_all x2, blocking collectives: 40.1 us -> 24.3 us  [to_all_rows(): lax.all_to_all(copies, 'row', 0, 0, tiled=True, axis_index_groups=groups)]
    ppermute x20 -> x22, starting transfers between devices: 36.9 us -> 48.2 us  [permute(): return lax.ppermute(a, BOTH, perm)]
    pallas_call x9 -> x11, Pallas kernels: 23.5 us -> 17.3 us  [call(): pl.pallas_call(kernel, out_shape=tuple(shapes), in_specs=[vmem] * len(arg...]
    ppermute x20 -> x22, waiting for transfers between devices: 27.9 us -> 27.2 us  [permute(): return lax.ppermute(a, BOTH, perm)]
  transfers between devices with their start and end apart: 20 -> 22, of which waited for: 12 -> 13; matrix products, arithmetic and copies ran while one was open for 0% -> 0% of each run, Pallas kernels for 5% -> 3%
where the time goes in v1:
time: 120 us; the launch traced here: 119 us
  starting transfers between devices  48.2 us (40%)
  waiting for transfers between devices  27.2 us (23%)
  blocking collectives  24.3 us (20%)
  Pallas kernels  17.3 us (14%)
  local copies, waits for them, and re-layouts  1.62 us (1%)
    ppermute x22, starting transfers between devices, permute(): return lax.ppermute(a, BOTH, perm)  48.2 us
    ppermute x22, waiting for transfers between devices, permute(): return lax.ppermute(a, BOTH, perm)  27.2 us
    all_to_all x2, blocking collectives, to_all_rows(): lax.all_to_all(copies, 'row', 0, 0, tiled=True, axis_index_groups=groups)  24.3 us
    pallas_call x11, Pallas kernels, call(): pl.pallas_call(kernel, out_shape=tuple(shapes), in_specs=[vmem] * len(arg...  17.3 us
  transfers between devices with their start and end apart: 22, of which 13 were waited for; matrix products, arithmetic and copies ran while one was open for 0% of the time, Pallas kernels for 3%

profile of v1, /device:TPU:1, one launch (start us, length us, event | category | flops | bytes accessed | tf_op | source)
XLA Modules:
  0.0 119.4 jit_solution(1321387996530715488)
XLA Ops:
  0.6 0.9 copy-done
  1.5 0.7 copy-done.1
  2.2 0.1 shard_map.41
  2.3 2.2 %collective-permute-start.4 = (f32[128,256]{1,0:T(8,128)S(1)}, f32[128,256]{1,0:T(8,128)S(1)}, u32[]{:S(2)}, u32[]{:S(2)}) collective-permute-start(f32[128,256]{1,0:T(8,128)S(1)} %get-tuple-element.27), channel_id=1, source_target_pairs={{0,8},{1,9},{2,10},{3,11},{4,36},{5,37},{6,38},{7,39},{8,16},{9,17... | collective-permute-start | bytes 393224 | tf_op jit(solution)/shard_map/ppermute | solution.py:58
  4.5 1.5 %collective-permute-start.6 = (f32[128,256]{1,0:T(8,128)S(1)}, f32[128,256]{1,0:T(8,128)S(1)}, u32[]{:S(2)}, u32[]{:S(2)}) collective-permute-start(f32[128,256]{1,0:T(8,128)S(1)} %get-tuple-element.27), channel_id=1, source_target_pairs={{0,24},{1,25},{2,26},{3,27},{4,100},{5,101},{6,102},{7,103},{8,0},... | collective-permute-start | bytes 393224 | tf_op jit(solution)/shard_map/ppermute | solution.py:58
  6.0 1.6 %collective-permute-start.5 = (f32[128,256]{1,0:T(8,128)S(1)}, f32[128,256]{1,0:T(8,128)S(1)}, u32[]{:S(2)}, u32[]{:S(2)}) collective-permute-start(f32[128,256]{1,0:T(8,128)S(1)} %get-tuple-element.27), channel_id=1, source_target_pairs={{0,16},{1,17},{2,18},{3,19},{4,68},{5,69},{6,70},{7,71},{8,24},{9,... | collective-permute-start | bytes 393224 | tf_op jit(solution)/shard_map/ppermute | solution.py:58
  7.6 1.0 collective-permute-done.4
  8.6 2.7 %collective-permute-done.5 = f32[128,256]{1,0:T(8,128)S(1)} collective-permute-done((f32[128,256]{1,0:T(8,128)S(1)}, f32[128,256]{1,0:T(8,128)S(1)}, u32[]{:S(2)}, u32[]{:S(2)}) %collective-permute-start.5) | collective-permute-done | bytes 131104 | tf_op jit(solution)/shard_map/ppermute | solution.py:58
  11.4 0.0 collective-permute-done.6
  11.4 1.3 %collective-permute-start.12 = (f32[512,256]{1,0:T(8,128)S(1)}, f32[512,256]{1,0:T(8,128)S(1)}, u32[]{:S(2)}, u32[]{:S(2)}) collective-permute-start(f32[512,256]{1,0:T(8,128)S(1)} %constant_dynamic-update-slice_fusion.refs_4_), channel_id=1, source_target_pairs={{0,32},{1,33},{2,34},{3,35},{4,12},{5,13},{6,14},{7,15},{8,40},{9,... | collective-permute-start | bytes 1572872 | tf_op jit(solution)/shard_map/ppermute | solution.py:58
  12.7 1.6 %collective-permute-start.10 = (f32[512,256]{1,0:T(8,128)S(1)}, f32[512,256]{1,0:T(8,128)S(1)}, u32[]{:S(2)}, u32[]{:S(2)}) collective-permute-start(f32[512,256]{1,0:T(8,128)S(1)} %constant_dynamic-update-slice_fusion.refs_4_), channel_id=1, source_target_pairs={{0,96},{1,97},{2,98},{3,99},{4,28},{5,29},{6,30},{7,31},{8,104},{9... | collective-permute-start | bytes 1572872 | tf_op jit(solution)/shard_map/ppermute | solution.py:58
  14.3 1.4 %collective-permute-start.8 = (f32[512,256]{1,0:T(8,128)S(1)}, f32[512,256]{1,0:T(8,128)S(1)}, u32[]{:S(2)}, u32[]{:S(2)}) collective-permute-start(f32[512,256]{1,0:T(8,128)S(1)} %constant_dynamic-update-slice_fusion.refs_4_), channel_id=1, source_target_pairs={{0,64},{1,65},{2,66},{3,67},{4,20},{5,21},{6,22},{7,23},{8,72},{9,... | collective-permute-start | bytes 1572872 | tf_op jit(solution)/shard_map/ppermute | solution.py:58
  15.7 6.7 %collective-permute-start = (f32[128,256]{1,0:T(8,128)S(1)}, f32[128,256]{1,0:T(8,128)S(1)}, u32[]{:S(2)}, u32[]{:S(2)}) collective-permute-start(f32[128,256]{1,0:T(8,128)S(1)} %get-tuple-element.27), channel_id=1, source_target_pairs={{0,0},{4,1},{8,2},{12,3},{16,4},{20,5},{24,6},{28,7},{32,9},{36,10... | collective-permute-start | bytes 393224 | tf_op jit(solution)/shard_map/ppermute | solution.py:58
  22.4 0.1 collective-permute-start.7
  22.5 1.5 %collective-permute-start.13 = (f32[512,256]{1,0:T(8,128)S(1)}, f32[512,256]{1,0:T(8,128)S(1)}, u32[]{:S(2)}, u32[]{:S(2)}) collective-permute-start(f32[512,256]{1,0:T(8,128)S(1)} %collective-permute-done.12.refs_1_), channel_id=1, source_target_pairs={{0,4},{1,5},{2,6},{3,7},{4,0},{5,1},{6,2},{7,3},{8,12},{9,13},{10,... | collective-permute-start | bytes 1572872 | tf_op jit(solution)/shard_map/ppermute | solution.py:58
  24.0 2.1 %collective-permute-done.10.refs_1_ = f32[512,256]{1,0:T(8,128)S(1)} collective-permute-done((f32[512,256]{1,0:T(8,128)S(1)}, f32[512,256]{1,0:T(8,128)S(1)}, u32[]{:S(2)}, u32[]{:S(2)}) %collective-permute-start.10) | collective-permute-done | bytes 524320 | tf_op jit(solution)/shard_map/ppermute | solution.py:58
  26.1 3.3 %collective-permute-done.8.refs_1_ = f32[512,256]{1,0:T(8,128)S(1)} collective-permute-done((f32[512,256]{1,0:T(8,128)S(1)}, f32[512,256]{1,0:T(8,128)S(1)}, u32[]{:S(2)}, u32[]{:S(2)}) %collective-permute-start.8) | collective-permute-done | bytes 524320 | tf_op jit(solution)/shard_map/ppermute | solution.py:58
  29.3 1.6 %collective-permute-start.9 = (f32[512,256]{1,0:T(8,128)S(1)}, f32[512,256]{1,0:T(8,128)S(1)}, u32[]{:S(2)}, u32[]{:S(2)}) collective-permute-start(f32[512,256]{1,0:T(8,128)S(1)} %collective-permute-done.8.refs_1_), channel_id=1, source_target_pairs={{0,4},{1,5},{2,6},{3,7},{4,0},{5,1},{6,2},{7,3},{8,12},{9,13},{10,... | collective-permute-start | bytes 1572872 | tf_op jit(solution)/shard_map/ppermute | solution.py:58
  31.0 12.0 %collective-permute-start.3 = (f32[128,256]{1,0:T(8,128)S(1)}, f32[128,256]{1,0:T(8,128)S(1)}, u32[]{:S(2)}, u32[]{:S(2)}) collective-permute-start(f32[128,256]{1,0:T(8,128)S(1)} %collective-permute-done.refs_0_), channel_id=1, source_target_pairs={{0,3},{1,0},{2,1},{3,2},{4,7},{5,4},{6,5},{7,6},{8,11},{9,8},{10,9... | collective-permute-start | bytes 393224 | tf_op jit(solution)/shard_map/ppermute | solution.py:58
  42.9 1.9 %collective-permute-done.3.refs_3_ = f32[128,256]{1,0:T(8,128)S(1)} collective-permute-done((f32[128,256]{1,0:T(8,128)S(1)}, f32[128,256]{1,0:T(8,128)S(1)}, u32[]{:S(2)}, u32[]{:S(2)}) %collective-permute-start.3) | collective-permute-done | bytes 131104 | tf_op jit(solution)/shard_map/ppermute | solution.py:58
  44.9 1.6 %collective-permute-start.2 = (f32[128,256]{1,0:T(8,128)S(1)}, f32[128,256]{1,0:T(8,128)S(1)}, u32[]{:S(2)}, u32[]{:S(2)}) collective-permute-start(f32[128,256]{1,0:T(8,128)S(1)} %collective-permute-done.refs_0_), channel_id=1, source_target_pairs={{0,2},{1,3},{2,0},{3,1},{4,6},{5,7},{6,4},{7,5},{8,10},{9,11},{10,... | collective-permute-start | bytes 393224 | tf_op jit(solution)/shard_map/ppermute | solution.py:58
  46.5 3.7 %collective-permute-done.2.refs_2_ = f32[128,256]{1,0:T(8,128)S(1)} collective-permute-done((f32[128,256]{1,0:T(8,128)S(1)}, f32[128,256]{1,0:T(8,128)S(1)}, u32[]{:S(2)}, u32[]{:S(2)}) %collective-permute-start.2) | collective-permute-done | bytes 131104 | tf_op jit(solution)/shard_map/ppermute | solution.py:58
  50.2 0.7 collective-permute-start.1
  50.9 4.7 %collective-permute-done.1.refs_1_ = f32[128,256]{1,0:T(8,128)S(1)} collective-permute-done((f32[128,256]{1,0:T(8,128)S(1)}, f32[128,256]{1,0:T(8,128)S(1)}, u32[]{:S(2)}, u32[]{:S(2)}) %collective-permute-start.1) | collective-permute-done | bytes 131104 | tf_op jit(solution)/shard_map/ppermute | solution.py:58
  55.6 1.2 shard_map.42
  56.9 1.1 shard_map.43
  58.0 1.1 shard_map.44
  59.2 1.3 %shard_map.45 = (f32[8,512,128]{2,1,0:T(8,128)S(1)}, f32[8,128]{1,0:T(8,128)S(1)}) custom-call(bf16[512,768]{1,0:T(8,128)(2,1)S(1)} %get-tuple-element.28.refs_0_, f32[512,256]{1,0:T(8,128)S(1)} %collective-permute-done.8.refs_1_, f32[512,256]{1,0:T(8,128)S(1)} %collective-permute-done.9.refs_2_, f32[512,128]{1,0:T(8,128)S(1)} %get-tuple-element.33.refs_3_, ...), custom_call_target="tpu_custom_call" | custom-call | tf_op jit(solution)/shard_map/pallas_call | solution.py:374
  60.4 0.8 collective-permute-start.16
  61.3 0.8 collective-permute-start.15
  62.0 0.7 collective-permute-start.14
  62.7 1.7 %collective-permute-done.16.refs_3_ = f32[8,128]{1,0:T(8,128)S(1)} collective-permute-done((f32[8,128]{1,0:T(8,128)S(1)}, f32[8,128]{1,0:T(8,128)S(1)}, u32[]{:S(2)}, u32[]{:S(2)}) %collective-permute-start.16) | collective-permute-done | bytes 4128 | tf_op jit(solution)/shard_map/ppermute | solution.py:58
  64.5 1.2 %collective-permute-done.14.refs_1_ = f32[8,128]{1,0:T(8,128)S(1)} collective-permute-done((f32[8,128]{1,0:T(8,128)S(1)}, f32[8,128]{1,0:T(8,128)S(1)}, u32[]{:S(2)}, u32[]{:S(2)}) %collective-permute-start.14) | collective-permute-done | bytes 4128 | tf_op jit(solution)/shard_map/ppermute | solution.py:58
  65.7 1.3 %shard_map.46 = (f32[32,128]{1,0:T(8,128)S(1)}, f32[8,128]{1,0:T(8,128)S(1)}, f32[512,128]{1,0:T(8,128)S(1)}, f32[512,128]{1,0:T(8,128)S(1)}) custom-call(f32[8,128]{1,0:T(8,128)S(1)} %get-tuple-element.36.refs_0_, f32[8,128]{1,0:T(8,128)S(1)} %collective-permute-done.14.refs_1_, f32[8,128]{1,0:T(8,128)S(1)} %collective-permute-done.15.refs_2_, ...), custom_call_target="tpu_custom_call" | custom-call | tf_op jit(solution)/shard_map/pallas_call | solution.py:374
  67.0 6.3 %collective-permute-start.17 = (f32[32,128]{1,0:T(8,128)S(1)}, f32[32,128]{1,0:T(8,128)S(1)}, u32[]{:S(2)}, u32[]{:S(2)}) collective-permute-start(f32[32,128]{1,0:T(8,128)S(1)} %get-tuple-element.41.a_ref), channel_id=1, source_target_pairs={{0,4},{1,5},{2,6},{3,7},{4,0},{5,1},{6,2},{7,3},{8,12},{9,13},{10,... | collective-permute-start | bytes 49160 | tf_op jit(solution)/shard_map/ppermute | solution.py:58
  73.3 0.8 collective-permute-done.17.b_ref
  74.1 13.5 %all_to_all.22 = f32[16,32,128]{2,1,0:T(8,128)S(1)} all-to-all(f32[16,32,128]{2,1,0:T(8,128)S(1)} %bitcast.7), channel_id=1, replica_groups={{0,8,16,24,32,40,48,56,64,72,80,88,96,104,112,120},{4,12,20,28,36,44,52..., dimensions={0} | all-to-all | bytes 524288 | tf_op jit(solution)/shard_map/all_to_all | solution.py:391
  87.6 2.6 %shard_map.48 = (f32[8,128]{1,0:T(8,128)S(1)}, f32[32,512,128]{2,1,0:T(8,128)S(1)}, f32[32,128]{1,0:T(8,128)S(1)}) custom-call(f32[512,128]{1,0:T(8,128)S(1)} %bitcast.6, f32[8,128]{1,0:T(8,128)S(1)} %get-tuple-element.42.refs_1_.refs_5_, f32[4,128]{1,0:T(4,128)S(1)} %get-tuple-element.35.refs_5_.refs_4_.refs_2_.refs_6_, ...), custom_call_target="tpu_custom_call" | custom-call | tf_op jit(solution)/shard_map/pallas_call | solution.py:374
  90.2 1.4 %collective-permute-start.20 = (f32[8,128]{1,0:T(8,128)S(1)}, f32[8,128]{1,0:T(8,128)S(1)}, u32[]{:S(2)}, u32[]{:S(2)}) collective-permute-start(f32[8,128]{1,0:T(8,128)S(1)} %get-tuple-element.45.refs_0_), channel_id=1, source_target_pairs={{0,2},{1,3},{2,0},{3,1},{4,6},{5,7},{6,4},{7,5},{8,10},{9,11},{10,... | collective-permute-start | bytes 12296 | tf_op jit(solution)/shard_map/ppermute | solution.py:58
  91.6 0.5 collective-permute-start.19
  92.1 0.9 collective-permute-start.18
  93.1 1.1 collective-permute-done.20.refs_3_
  94.2 1.9 %collective-permute-done.18.refs_1_ = f32[8,128]{1,0:T(8,128)S(1)} collective-permute-done((f32[8,128]{1,0:T(8,128)S(1)}, f32[8,128]{1,0:T(8,128)S(1)}, u32[]{:S(2)}, u32[]{:S(2)}) %collective-permute-start.18) | collective-permute-done | bytes 4128 | tf_op jit(solution)/shard_map/ppermute | solution.py:58
  96.1 4.8 %shard_map.49 = (f32[512,4096]{1,0:T(8,128)}, f32[32,128]{1,0:T(8,128)S(1)}, f32[512,4096]{1,0:T(8,128)S(1)}, f32[8,128]{1,0:T(8,128)S(1)}) custom-call(f32[8,128]{1,0:T(8,128)S(1)} %get-tuple-element.45.refs_0_, f32[8,128]{1,0:T(8,128)S(1)} %collective-permute-done.18.refs_1_, f32[8,128]{1,0:T(8,128)S(1)} %collective-permute-done.19.refs_2_, ...), custom_call_target="tpu_custom_call" | custom-call | tf_op jit(solution)/shard_map/pallas_call | solution.py:374
  100.9 3.0 %collective-permute-start.21 = (f32[32,128]{1,0:T(8,128)S(1)}, f32[32,128]{1,0:T(8,128)S(1)}, u32[]{:S(2)}, u32[]{:S(2)}) collective-permute-start(f32[32,128]{1,0:T(8,128)S(1)} %get-tuple-element.49.a_ref), channel_id=1, source_target_pairs={{0,4},{1,5},{2,6},{3,7},{4,0},{5,1},{6,2},{7,3},{8,12},{9,13},{10,... | collective-permute-start | bytes 49160 | tf_op jit(solution)/shard_map/ppermute | solution.py:58
  103.9 0.8 collective-permute-done.21.b_ref
  104.8 10.8 %all_to_all.23 = f32[16,32,128]{2,1,0:T(8,128)S(1)} all-to-all(f32[16,32,128]{2,1,0:T(8,128)S(1)} %bitcast.8), channel_id=1, replica_groups={{0,8,16,24,32,40,48,56,64,72,80,88,96,104,112,120},{4,12,20,28,36,44,52..., dimensions={0} | all-to-all | bytes 524288 | tf_op jit(solution)/shard_map/all_to_all | solution.py:391
  115.6 3.8 %shard_map.51 = f32[512,4096]{1,0:T(8,128)} custom-call(f32[512,128]{1,0:T(8,128)S(1)} %bitcast.5, f32[512,4096]{1,0:T(8,128)S(1)} %get-tuple-element.50.refs_1_, f32[8,128]{1,0:T(8,128)S(1)} %get-tuple-element.51.refs_2_, f32[32,512,128]{2,1,0:T(8,128)S(1)} %get-tuple-element.47.refs_7_.refs_3_, ...), custom_call_target="tpu_custom_call" | custom-call | tf_op jit(solution)/shard_map/pallas_call | solution.py:374
  (17 shorter events, 0.1 us)
Async XLA Ops:
  0.6 0.9 copy-start
  1.5 0.7 copy-start.1
  2.3 6.3 %collective-permute-start.4 = (f32[128,256]{1,0:T(8,128)S(1)}, f32[128,256]{1,0:T(8,128)S(1)}, u32[]{:S(2)}, u32[]{:S(2)}) collective-permute-start(f32[128,256]{1,0:T(8,128)S(1)} %get-tuple-element.27), channel_id=1, source_target_pairs={{0,8},{1,9},{2,10},{3,11},{4,36},{5,37},{6,38},{7,39},{8,16},{9,17... | collective-permute-start | bytes 393224 | tf_op jit(solution)/shard_map/ppermute | solution.py:58
  4.5 6.9 %collective-permute-start.6 = (f32[128,256]{1,0:T(8,128)S(1)}, f32[128,256]{1,0:T(8,128)S(1)}, u32[]{:S(2)}, u32[]{:S(2)}) collective-permute-start(f32[128,256]{1,0:T(8,128)S(1)} %get-tuple-element.27), channel_id=1, source_target_pairs={{0,24},{1,25},{2,26},{3,27},{4,100},{5,101},{6,102},{7,103},{8,0},... | collective-permute-start | bytes 393224 | tf_op jit(solution)/shard_map/ppermute | solution.py:58
  6.0 5.3 %collective-permute-start.5 = (f32[128,256]{1,0:T(8,128)S(1)}, f32[128,256]{1,0:T(8,128)S(1)}, u32[]{:S(2)}, u32[]{:S(2)}) collective-permute-start(f32[128,256]{1,0:T(8,128)S(1)} %get-tuple-element.27), channel_id=1, source_target_pairs={{0,16},{1,17},{2,18},{3,19},{4,68},{5,69},{6,70},{7,71},{8,24},{9,... | collective-permute-start | bytes 393224 | tf_op jit(solution)/shard_map/ppermute | solution.py:58
  11.4 11.1 %collective-permute-start.12 = (f32[512,256]{1,0:T(8,128)S(1)}, f32[512,256]{1,0:T(8,128)S(1)}, u32[]{:S(2)}, u32[]{:S(2)}) collective-permute-start(f32[512,256]{1,0:T(8,128)S(1)} %constant_dynamic-update-slice_fusion.refs_4_), channel_id=1, source_target_pairs={{0,32},{1,33},{2,34},{3,35},{4,12},{5,13},{6,14},{7,15},{8,40},{9,... | collective-permute-start | bytes 1572872 | tf_op jit(solution)/shard_map/ppermute | solution.py:58
  12.7 13.4 %collective-permute-start.10 = (f32[512,256]{1,0:T(8,128)S(1)}, f32[512,256]{1,0:T(8,128)S(1)}, u32[]{:S(2)}, u32[]{:S(2)}) collective-permute-start(f32[512,256]{1,0:T(8,128)S(1)} %constant_dynamic-update-slice_fusion.refs_4_), channel_id=1, source_target_pairs={{0,96},{1,97},{2,98},{3,99},{4,28},{5,29},{6,30},{7,31},{8,104},{9... | collective-permute-start | bytes 1572872 | tf_op jit(solution)/shard_map/ppermute | solution.py:58
  14.3 15.0 %collective-permute-start.8 = (f32[512,256]{1,0:T(8,128)S(1)}, f32[512,256]{1,0:T(8,128)S(1)}, u32[]{:S(2)}, u32[]{:S(2)}) collective-permute-start(f32[512,256]{1,0:T(8,128)S(1)} %constant_dynamic-update-slice_fusion.refs_4_), channel_id=1, source_target_pairs={{0,64},{1,65},{2,66},{3,67},{4,20},{5,21},{6,22},{7,23},{8,72},{9,... | collective-permute-start | bytes 1572872 | tf_op jit(solution)/shard_map/ppermute | solution.py:58
  15.7 15.3 %collective-permute-start = (f32[128,256]{1,0:T(8,128)S(1)}, f32[128,256]{1,0:T(8,128)S(1)}, u32[]{:S(2)}, u32[]{:S(2)}) collective-permute-start(f32[128,256]{1,0:T(8,128)S(1)} %get-tuple-element.27), channel_id=1, source_target_pairs={{0,0},{4,1},{8,2},{12,3},{16,4},{20,5},{24,6},{28,7},{32,9},{36,10... | collective-permute-start | bytes 393224 | tf_op jit(solution)/shard_map/ppermute | solution.py:58
  22.4 33.3 %collective-permute-start.7 = (f32[512,256]{1,0:T(8,128)S(1)}, f32[512,256]{1,0:T(8,128)S(1)}, u32[]{:S(2)}, u32[]{:S(2)}) collective-permute-start(f32[512,256]{1,0:T(8,128)S(1)} %constant_dynamic-update-slice_fusion.refs_4_), channel_id=1, source_target_pairs={{0,4},{1,5},{2,6},{3,7},{4,0},{5,1},{6,2},{7,3},{8,12},{9,13},{10,... | collective-permute-start | bytes 1572872 | tf_op jit(solution)/shard_map/ppermute | solution.py:58
  22.5 34.4 %collective-permute-start.13 = (f32[512,256]{1,0:T(8,128)S(1)}, f32[512,256]{1,0:T(8,128)S(1)}, u32[]{:S(2)}, u32[]{:S(2)}) collective-permute-start(f32[512,256]{1,0:T(8,128)S(1)} %collective-permute-done.12.refs_1_), channel_id=1, source_target_pairs={{0,4},{1,5},{2,6},{3,7},{4,0},{5,1},{6,2},{7,3},{8,12},{9,13},{10,... | collective-permute-start | bytes 1572872 | tf_op jit(solution)/shard_map/ppermute | solution.py:58
  26.1 31.9 %collective-permute-start.11 = (f32[512,256]{1,0:T(8,128)S(1)}, f32[512,256]{1,0:T(8,128)S(1)}, u32[]{:S(2)}, u32[]{:S(2)}) collective-permute-start(f32[512,256]{1,0:T(8,128)S(1)} %collective-permute-done.10.refs_1_), channel_id=1, source_target_pairs={{0,4},{1,5},{2,6},{3,7},{4,0},{5,1},{6,2},{7,3},{8,12},{9,13},{10,... | collective-permute-start | bytes 1572872 | tf_op jit(solution)/shard_map/ppermute | solution.py:58
  29.3 29.8 %collective-permute-start.9 = (f32[512,256]{1,0:T(8,128)S(1)}, f32[512,256]{1,0:T(8,128)S(1)}, u32[]{:S(2)}, u32[]{:S(2)}) collective-permute-start(f32[512,256]{1,0:T(8,128)S(1)} %collective-permute-done.8.refs_1_), channel_id=1, source_target_pairs={{0,4},{1,5},{2,6},{3,7},{4,0},{5,1},{6,2},{7,3},{8,12},{9,13},{10,... | collective-permute-start | bytes 1572872 | tf_op jit(solution)/shard_map/ppermute | solution.py:58
  31.0 13.9 %collective-permute-start.3 = (f32[128,256]{1,0:T(8,128)S(1)}, f32[128,256]{1,0:T(8,128)S(1)}, u32[]{:S(2)}, u32[]{:S(2)}) collective-permute-start(f32[128,256]{1,0:T(8,128)S(1)} %collective-permute-done.refs_0_), channel_id=1, source_target_pairs={{0,3},{1,0},{2,1},{3,2},{4,7},{5,4},{6,5},{7,6},{8,11},{9,8},{10,9... | collective-permute-start | bytes 393224 | tf_op jit(solution)/shard_map/ppermute | solution.py:58
  44.9 5.3 %collective-permute-start.2 = (f32[128,256]{1,0:T(8,128)S(1)}, f32[128,256]{1,0:T(8,128)S(1)}, u32[]{:S(2)}, u32[]{:S(2)}) collective-permute-start(f32[128,256]{1,0:T(8,128)S(1)} %collective-permute-done.refs_0_), channel_id=1, source_target_pairs={{0,2},{1,3},{2,0},{3,1},{4,6},{5,7},{6,4},{7,5},{8,10},{9,11},{10,... | collective-permute-start | bytes 393224 | tf_op jit(solution)/shard_map/ppermute | solution.py:58
  50.2 5.4 %collective-permute-start.1 = (f32[128,256]{1,0:T(8,128)S(1)}, f32[128,256]{1,0:T(8,128)S(1)}, u32[]{:S(2)}, u32[]{:S(2)}) collective-permute-start(f32[128,256]{1,0:T(8,128)S(1)} %collective-permute-done.refs_0_), channel_id=1, source_target_pairs={{0,1},{1,2},{2,3},{3,0},{4,5},{5,6},{6,7},{7,4},{8,9},{9,10},{10,1... | collective-permute-start | bytes 393224 | tf_op jit(solution)/shard_map/ppermute | solution.py:58
  60.4 4.0 %collective-permute-start.16 = (f32[8,128]{1,0:T(8,128)S(1)}, f32[8,128]{1,0:T(8,128)S(1)}, u32[]{:S(2)}, u32[]{:S(2)}) collective-permute-start(f32[8,128]{1,0:T(8,128)S(1)} %get-tuple-element.36.refs_0_), channel_id=1, source_target_pairs={{0,2},{1,3},{2,0},{3,1},{4,6},{5,7},{6,4},{7,5},{8,10},{9,11},{10,... | collective-permute-start | bytes 12296 | tf_op jit(solution)/shard_map/ppermute | solution.py:58
  61.3 3.2 %collective-permute-start.15 = (f32[8,128]{1,0:T(8,128)S(1)}, f32[8,128]{1,0:T(8,128)S(1)}, u32[]{:S(2)}, u32[]{:S(2)}) collective-permute-start(f32[8,128]{1,0:T(8,128)S(1)} %get-tuple-element.36.refs_0_), channel_id=1, source_target_pairs={{0,3},{1,0},{2,1},{3,2},{4,7},{5,4},{6,5},{7,6},{8,11},{9,8},{10,9... | collective-permute-start | bytes 12296 | tf_op jit(solution)/shard_map/ppermute | solution.py:58
  62.0 3.7 %collective-permute-start.14 = (f32[8,128]{1,0:T(8,128)S(1)}, f32[8,128]{1,0:T(8,128)S(1)}, u32[]{:S(2)}, u32[]{:S(2)}) collective-permute-start(f32[8,128]{1,0:T(8,128)S(1)} %get-tuple-element.36.refs_0_), channel_id=1, source_target_pairs={{0,1},{1,2},{2,3},{3,0},{4,5},{5,6},{6,7},{7,4},{8,9},{9,10},{10,1... | collective-permute-start | bytes 12296 | tf_op jit(solution)/shard_map/ppermute | solution.py:58
  67.0 7.1 %collective-permute-start.17 = (f32[32,128]{1,0:T(8,128)S(1)}, f32[32,128]{1,0:T(8,128)S(1)}, u32[]{:S(2)}, u32[]{:S(2)}) collective-permute-start(f32[32,128]{1,0:T(8,128)S(1)} %get-tuple-element.41.a_ref), channel_id=1, source_target_pairs={{0,4},{1,5},{2,6},{3,7},{4,0},{5,1},{6,2},{7,3},{8,12},{9,13},{10,... | collective-permute-start | bytes 49160 | tf_op jit(solution)/shard_map/ppermute | solution.py:58
  90.2 4.0 %collective-permute-start.20 = (f32[8,128]{1,0:T(8,128)S(1)}, f32[8,128]{1,0:T(8,128)S(1)}, u32[]{:S(2)}, u32[]{:S(2)}) collective-permute-start(f32[8,128]{1,0:T(8,128)S(1)} %get-tuple-element.45.refs_0_), channel_id=1, source_target_pairs={{0,2},{1,3},{2,0},{3,1},{4,6},{5,7},{6,4},{7,5},{8,10},{9,11},{10,... | collective-permute-start | bytes 12296 | tf_op jit(solution)/shard_map/ppermute | solution.py:58
  91.6 2.6 %collective-permute-start.19 = (f32[8,128]{1,0:T(8,128)S(1)}, f32[8,128]{1,0:T(8,128)S(1)}, u32[]{:S(2)}, u32[]{:S(2)}) collective-permute-start(f32[8,128]{1,0:T(8,128)S(1)} %get-tuple-element.45.refs_0_), channel_id=1, source_target_pairs={{0,3},{1,0},{2,1},{3,2},{4,7},{5,4},{6,5},{7,6},{8,11},{9,8},{10,9... | collective-permute-start | bytes 12296 | tf_op jit(solution)/shard_map/ppermute | solution.py:58
  92.1 4.0 %collective-permute-start.18 = (f32[8,128]{1,0:T(8,128)S(1)}, f32[8,128]{1,0:T(8,128)S(1)}, u32[]{:S(2)}, u32[]{:S(2)}) collective-permute-start(f32[8,128]{1,0:T(8,128)S(1)} %get-tuple-element.45.refs_0_), channel_id=1, source_target_pairs={{0,1},{1,2},{2,3},{3,0},{4,5},{5,6},{6,7},{7,4},{8,9},{9,10},{10,1... | collective-permute-start | bytes 12296 | tf_op jit(solution)/shard_map/ppermute | solution.py:58
  100.9 3.8 %collective-permute-start.21 = (f32[32,128]{1,0:T(8,128)S(1)}, f32[32,128]{1,0:T(8,128)S(1)}, u32[]{:S(2)}, u32[]{:S(2)}) collective-permute-start(f32[32,128]{1,0:T(8,128)S(1)} %get-tuple-element.49.a_ref), channel_id=1, source_target_pairs={{0,4},{1,5},{2,6},{3,7},{4,0},{5,1},{6,2},{7,3},{8,12},{9,13},{10,... | collective-permute-start | bytes 49160 | tf_op jit(solution)/shard_map/ppermute | solution.py:58

commit v2 on v1

--- a/solution.py
+++ b/solution.py
@@ -46,12 +46,16 @@
     return pairs(lambda y, x, core, c: (y, x, 1 - core, c))
 
 
+def turn(y, x, core):
+    return 2 * (x % 2) + core + y
+
+
+def col_turn():
+    return pairs(lambda y, x, core, c: (y, x, core, (c + turn(y, x, core)) % N_COL))
+
+
 def to_row_block():
-    out = []
-    for r in range(N_ROW):
-        for j in range(N_COL):
-            out.append(((4 * (r % 8) + j) * N_COL + r // 8, r * N_COL + (j + r // 8 + r // 2 % 4) % 4))
-    return out
+    return pairs(lambda y, x, core, c: ((c - turn(y, x, core)) % N_COL, y, x // 2, c))
 
 
 def permute(a, perm):
@@ -394,7 +398,7 @@
 def propagate(embeddings, levels):
     levels = levels.reshape(4, LANES)
     unit, pref = call(unit_kernel, [embeddings, levels], [((SHARD, D), "vmem"), ((4, LANES), "vmem")])
-    mine = permute(unit, to_row_block())
+    mine = permute(permute(unit, col_turn()), to_row_block())
     line = [unit] + [permute(unit, plane_shift(k, 1)) for k in (1, 2, 3)]
     line = jnp.concatenate(line, axis=0)
     rows = [mine] + [permute(mine, col_shift(k)) for k in (1, 2, 3)]

time: 120 us -> 116 us (0.967)
  starting transfers between devices: 48.2 us -> 41.7 us
  blocking collectives: 24.3 us -> 26.3 us
    ppermute x22 -> x23, starting transfers between devices: 48.2 us -> 41.7 us  [permute(): return lax.ppermute(a, BOTH, perm)]
    all_to_all x2, blocking collectives: 24.3 us -> 26.3 us  [to_all_rows(): lax.all_to_all(copies, 'row', 0, 0, tiled=True, axis_index_groups=groups)]
    ppermute x22 -> x23, waiting for transfers between devices: 27.2 us -> 27.7 us  [permute(): return lax.ppermute(a, BOTH, perm)]
  transfers between devices with their start and end apart: 22 -> 23, of which waited for: 13 -> 13; matrix products, arithmetic and copies ran while one was open for 0% -> 0% of each run, Pallas kernels for 3% -> 3%
where the time goes in v2:
time: 116 us; the launch traced here: 115 us
  starting transfers between devices  41.7 us (36%)
  waiting for transfers between devices  27.7 us (24%)
  blocking collectives  26.3 us (23%)
  Pallas kernels  17.3 us (15%)
  local copies, waits for them, and re-layouts  1.62 us (1%)
    ppermute x23, starting transfers between devices, permute(): return lax.ppermute(a, BOTH, perm)  41.7 us
    ppermute x23, waiting for transfers between devices, permute(): return lax.ppermute(a, BOTH, perm)  27.7 us
    all_to_all x2, blocking collectives, to_all_rows(): lax.all_to_all(copies, 'row', 0, 0, tiled=True, axis_index_groups=groups)  26.3 us
    pallas_call x11, Pallas kernels, call(): pl.pallas_call(kernel, out_shape=tuple(shapes), in_specs=[vmem] * len(arg...  17.3 us
  transfers between devices with their start and end apart: 23, of which 13 were waited for; matrix products, arithmetic and copies ran while one was open for 0% of the time, Pallas kernels for 3%

profile of v2, /device:TPU:1, one launch (start us, length us, event | category | flops | bytes accessed | tf_op | source)
XLA Modules:
  0.0 115.4 jit_solution(16013437773856983483)
XLA Ops:
  0.6 0.9 copy-done
  1.5 0.7 copy-done.1
  2.2 0.1 shard_map.41
  2.3 2.2 %collective-permute-start.5 = (f32[128,256]{1,0:T(8,128)S(1)}, f32[128,256]{1,0:T(8,128)S(1)}, u32[]{:S(2)}, u32[]{:S(2)}) collective-permute-start(f32[128,256]{1,0:T(8,128)S(1)} %get-tuple-element.27), channel_id=1, source_target_pairs={{0,8},{1,9},{2,10},{3,11},{4,36},{5,37},{6,38},{7,39},{8,16},{9,17... | collective-permute-start | bytes 393224 | tf_op jit(solution)/shard_map/ppermute | solution.py:62
  4.5 1.5 %collective-permute-start.7 = (f32[128,256]{1,0:T(8,128)S(1)}, f32[128,256]{1,0:T(8,128)S(1)}, u32[]{:S(2)}, u32[]{:S(2)}) collective-permute-start(f32[128,256]{1,0:T(8,128)S(1)} %get-tuple-element.27), channel_id=1, source_target_pairs={{0,24},{1,25},{2,26},{3,27},{4,100},{5,101},{6,102},{7,103},{8,0},... | collective-permute-start | bytes 393224 | tf_op jit(solution)/shard_map/ppermute | solution.py:62
  6.0 1.6 %collective-permute-start.6 = (f32[128,256]{1,0:T(8,128)S(1)}, f32[128,256]{1,0:T(8,128)S(1)}, u32[]{:S(2)}, u32[]{:S(2)}) collective-permute-start(f32[128,256]{1,0:T(8,128)S(1)} %get-tuple-element.27), channel_id=1, source_target_pairs={{0,16},{1,17},{2,18},{3,19},{4,68},{5,69},{6,70},{7,71},{8,24},{9,... | collective-permute-start | bytes 393224 | tf_op jit(solution)/shard_map/ppermute | solution.py:62
  7.6 1.0 collective-permute-done.5
  8.6 2.7 %collective-permute-done.6 = f32[128,256]{1,0:T(8,128)S(1)} collective-permute-done((f32[128,256]{1,0:T(8,128)S(1)}, f32[128,256]{1,0:T(8,128)S(1)}, u32[]{:S(2)}, u32[]{:S(2)}) %collective-permute-start.6) | collective-permute-done | bytes 131104 | tf_op jit(solution)/shard_map/ppermute | solution.py:62
  11.4 1.3 %collective-permute-start.13 = (f32[512,256]{1,0:T(8,128)S(1)}, f32[512,256]{1,0:T(8,128)S(1)}, u32[]{:S(2)}, u32[]{:S(2)}) collective-permute-start(f32[512,256]{1,0:T(8,128)S(1)} %constant_dynamic-update-slice_fusion.refs_4_), channel_id=1, source_target_pairs={{0,32},{1,33},{2,34},{3,35},{4,12},{5,13},{6,14},{7,15},{8,40},{9,... | collective-permute-start | bytes 1572872 | tf_op jit(solution)/shard_map/ppermute | solution.py:62
  12.7 1.6 %collective-permute-start.11 = (f32[512,256]{1,0:T(8,128)S(1)}, f32[512,256]{1,0:T(8,128)S(1)}, u32[]{:S(2)}, u32[]{:S(2)}) collective-permute-start(f32[512,256]{1,0:T(8,128)S(1)} %constant_dynamic-update-slice_fusion.refs_4_), channel_id=1, source_target_pairs={{0,96},{1,97},{2,98},{3,99},{4,28},{5,29},{6,30},{7,31},{8,104},{9... | collective-permute-start | bytes 1572872 | tf_op jit(solution)/shard_map/ppermute | solution.py:62
  14.3 1.4 %collective-permute-start.9 = (f32[512,256]{1,0:T(8,128)S(1)}, f32[512,256]{1,0:T(8,128)S(1)}, u32[]{:S(2)}, u32[]{:S(2)}) collective-permute-start(f32[512,256]{1,0:T(8,128)S(1)} %constant_dynamic-update-slice_fusion.refs_4_), channel_id=1, source_target_pairs={{0,64},{1,65},{2,66},{3,67},{4,20},{5,21},{6,22},{7,23},{8,72},{9,... | collective-permute-start | bytes 1572872 | tf_op jit(solution)/shard_map/ppermute | solution.py:62
  15.7 3.5 %collective-permute-start = (f32[128,256]{1,0:T(8,128)S(1)}, f32[128,256]{1,0:T(8,128)S(1)}, u32[]{:S(2)}, u32[]{:S(2)}) collective-permute-start(f32[128,256]{1,0:T(8,128)S(1)} %get-tuple-element.27), channel_id=1, source_target_pairs={{0,0},{1,1},{2,2},{3,3},{4,5},{5,6},{6,7},{7,4},{8,10},{9,11},{10,... | collective-permute-start | bytes 393224 | tf_op jit(solution)/shard_map/ppermute | solution.py:62
  19.2 4.5 %collective-permute-done = f32[128,256]{1,0:T(8,128)S(1)} collective-permute-done((f32[128,256]{1,0:T(8,128)S(1)}, f32[128,256]{1,0:T(8,128)S(1)}, u32[]{:S(2)}, u32[]{:S(2)}) %collective-permute-start) | collective-permute-done | bytes 131104 | tf_op jit(solution)/shard_map/ppermute | solution.py:62
  23.7 6.2 %collective-permute-start.1 = (f32[128,256]{1,0:T(8,128)S(1)}, f32[128,256]{1,0:T(8,128)S(1)}, u32[]{:S(2)}, u32[]{:S(2)}) collective-permute-start(f32[128,256]{1,0:T(8,128)S(1)} %collective-permute-done), channel_id=1, source_target_pairs={{0,0},{1,33},{2,66},{3,99},{4,96},{5,1},{6,34},{7,67},{8,64},{9,97... | collective-permute-start | bytes 393224 | tf_op jit(solution)/shard_map/ppermute | solution.py:62
  30.0 0.5 collective-permute-start.14
  30.5 0.1 collective-permute-start.12
  30.6 0.4 collective-permute-start.10
  31.0 0.8 collective-permute-done.1.refs_0_
  31.9 6.5 %collective-permute-start.4 = (f32[128,256]{1,0:T(8,128)S(1)}, f32[128,256]{1,0:T(8,128)S(1)}, u32[]{:S(2)}, u32[]{:S(2)}) collective-permute-start(f32[128,256]{1,0:T(8,128)S(1)} %collective-permute-done.1.refs_0_), channel_id=1, source_target_pairs={{0,3},{1,0},{2,1},{3,2},{4,7},{5,4},{6,5},{7,6},{8,11},{9,8},{10,9... | collective-permute-start | bytes 393224 | tf_op jit(solution)/shard_map/ppermute | solution.py:62
  38.3 1.9 %collective-permute-done.4.refs_3_ = f32[128,256]{1,0:T(8,128)S(1)} collective-permute-done((f32[128,256]{1,0:T(8,128)S(1)}, f32[128,256]{1,0:T(8,128)S(1)}, u32[]{:S(2)}, u32[]{:S(2)}) %collective-permute-start.4) | collective-permute-done | bytes 131104 | tf_op jit(solution)/shard_map/ppermute | solution.py:62
  40.3 2.9 %collective-permute-start.3 = (f32[128,256]{1,0:T(8,128)S(1)}, f32[128,256]{1,0:T(8,128)S(1)}, u32[]{:S(2)}, u32[]{:S(2)}) collective-permute-start(f32[128,256]{1,0:T(8,128)S(1)} %collective-permute-done.1.refs_0_), channel_id=1, source_target_pairs={{0,2},{1,3},{2,0},{3,1},{4,6},{5,7},{6,4},{7,5},{8,10},{9,11},{10,... | collective-permute-start | bytes 393224 | tf_op jit(solution)/shard_map/ppermute | solution.py:62
  43.2 3.2 %collective-permute-done.3.refs_2_ = f32[128,256]{1,0:T(8,128)S(1)} collective-permute-done((f32[128,256]{1,0:T(8,128)S(1)}, f32[128,256]{1,0:T(8,128)S(1)}, u32[]{:S(2)}, u32[]{:S(2)}) %collective-permute-start.3) | collective-permute-done | bytes 131104 | tf_op jit(solution)/shard_map/ppermute | solution.py:62
  46.4 0.6 collective-permute-start.2
  47.0 5.4 %collective-permute-done.2.refs_1_ = f32[128,256]{1,0:T(8,128)S(1)} collective-permute-done((f32[128,256]{1,0:T(8,128)S(1)}, f32[128,256]{1,0:T(8,128)S(1)}, u32[]{:S(2)}, u32[]{:S(2)}) %collective-permute-start.2) | collective-permute-done | bytes 131104 | tf_op jit(solution)/shard_map/ppermute | solution.py:62
  52.4 1.2 %shard_map.42 = (f32[8,512,128]{2,1,0:T(8,128)S(1)}, bf16[512,768]{1,0:T(8,128)(2,1)S(1)}, f32[512,128]{1,0:T(8,128)S(1)}, f32[512,128]{1,0:T(8,128)S(1)}) custom-call(f32[128,256]{1,0:T(8,128)S(1)} %collective-permute-done.1.refs_0_, f32[128,256]{1,0:T(8,128)S(1)} %collective-permute-done.2.refs_1_, f32[128,256]{1,0:T(8,128)S(1)} %collective-permute-done.3.refs_2_, ...), custom_call_target="tpu_custom_call" | custom-call | tf_op jit(solution)/shard_map/pallas_call | solution.py:378
  53.6 1.1 shard_map.43
  54.7 1.1 shard_map.44
  55.9 1.3 %shard_map.45 = (f32[8,512,128]{2,1,0:T(8,128)S(1)}, f32[8,128]{1,0:T(8,128)S(1)}) custom-call(bf16[512,768]{1,0:T(8,128)(2,1)S(1)} %get-tuple-element.28.refs_0_, f32[512,256]{1,0:T(8,128)S(1)} %collective-permute-done.9.refs_1_, f32[512,256]{1,0:T(8,128)S(1)} %collective-permute-done.10.refs_2_, f32[512,128]{1,0:T(8,128)S(1)} %get-tuple-element.33.refs_3_, ...), custom_call_target="tpu_custom_call" | custom-call | tf_op jit(solution)/shard_map/pallas_call | solution.py:378
  57.2 1.1 collective-permute-start.17
  58.3 1.1 collective-permute-start.16
  59.4 0.5 collective-permute-start.15
  59.9 1.3 %collective-permute-done.17.refs_3_ = f32[8,128]{1,0:T(8,128)S(1)} collective-permute-done((f32[8,128]{1,0:T(8,128)S(1)}, f32[8,128]{1,0:T(8,128)S(1)}, u32[]{:S(2)}, u32[]{:S(2)}) %collective-permute-start.17) | collective-permute-done | bytes 4128 | tf_op jit(solution)/shard_map/ppermute | solution.py:62
  61.2 2.2 %collective-permute-done.15.refs_1_ = f32[8,128]{1,0:T(8,128)S(1)} collective-permute-done((f32[8,128]{1,0:T(8,128)S(1)}, f32[8,128]{1,0:T(8,128)S(1)}, u32[]{:S(2)}, u32[]{:S(2)}) %collective-permute-start.15) | collective-permute-done | bytes 4128 | tf_op jit(solution)/shard_map/ppermute | solution.py:62
  63.4 1.3 %shard_map.46 = (f32[32,128]{1,0:T(8,128)S(1)}, f32[8,128]{1,0:T(8,128)S(1)}, f32[512,128]{1,0:T(8,128)S(1)}, f32[512,128]{1,0:T(8,128)S(1)}) custom-call(f32[8,128]{1,0:T(8,128)S(1)} %get-tuple-element.36.refs_0_, f32[8,128]{1,0:T(8,128)S(1)} %collective-permute-done.15.refs_1_, f32[8,128]{1,0:T(8,128)S(1)} %collective-permute-done.16.refs_2_, ...), custom_call_target="tpu_custom_call" | custom-call | tf_op jit(solution)/shard_map/pallas_call | solution.py:378
  64.6 2.7 %collective-permute-start.18 = (f32[32,128]{1,0:T(8,128)S(1)}, f32[32,128]{1,0:T(8,128)S(1)}, u32[]{:S(2)}, u32[]{:S(2)}) collective-permute-start(f32[32,128]{1,0:T(8,128)S(1)} %get-tuple-element.41.a_ref), channel_id=1, source_target_pairs={{0,4},{1,5},{2,6},{3,7},{4,0},{5,1},{6,2},{7,3},{8,12},{9,13},{10,... | collective-permute-start | bytes 49160 | tf_op jit(solution)/shard_map/ppermute | solution.py:62
  67.3 0.8 collective-permute-done.18.b_ref
  68.2 15.5 %all_to_all.22 = f32[16,32,128]{2,1,0:T(8,128)S(1)} all-to-all(f32[16,32,128]{2,1,0:T(8,128)S(1)} %bitcast.7), channel_id=1, replica_groups={{0,8,16,24,32,40,48,56,64,72,80,88,96,104,112,120},{4,12,20,28,36,44,52..., dimensions={0} | all-to-all | bytes 524288 | tf_op jit(solution)/shard_map/all_to_all | solution.py:395
  83.7 2.6 %shard_map.48 = (f32[8,128]{1,0:T(8,128)S(1)}, f32[32,512,128]{2,1,0:T(8,128)S(1)}, f32[32,128]{1,0:T(8,128)S(1)}) custom-call(f32[512,128]{1,0:T(8,128)S(1)} %bitcast.6, f32[8,128]{1,0:T(8,128)S(1)} %get-tuple-element.42.refs_1_.refs_5_, f32[4,128]{1,0:T(4,128)S(1)} %get-tuple-element.35.refs_5_.refs_4_.refs_2_.refs_6_, ...), custom_call_target="tpu_custom_call" | custom-call | tf_op jit(solution)/shard_map/pallas_call | solution.py:378
  86.3 1.4 %collective-permute-start.21 = (f32[8,128]{1,0:T(8,128)S(1)}, f32[8,128]{1,0:T(8,128)S(1)}, u32[]{:S(2)}, u32[]{:S(2)}) collective-permute-start(f32[8,128]{1,0:T(8,128)S(1)} %get-tuple-element.45.refs_0_), channel_id=1, source_target_pairs={{0,2},{1,3},{2,0},{3,1},{4,6},{5,7},{6,4},{7,5},{8,10},{9,11},{10,... | collective-permute-start | bytes 12296 | tf_op jit(solution)/shard_map/ppermute | solution.py:62
  87.7 0.5 collective-permute-start.20
  88.2 1.0 collective-permute-start.19
  89.2 1.1 collective-permute-done.21.refs_3_
  90.3 1.8 %collective-permute-done.19.refs_1_ = f32[8,128]{1,0:T(8,128)S(1)} collective-permute-done((f32[8,128]{1,0:T(8,128)S(1)}, f32[8,128]{1,0:T(8,128)S(1)}, u32[]{:S(2)}, u32[]{:S(2)}) %collective-permute-start.19) | collective-permute-done | bytes 4128 | tf_op jit(solution)/shard_map/ppermute | solution.py:62
  92.1 4.8 %shard_map.49 = (f32[512,4096]{1,0:T(8,128)}, f32[32,128]{1,0:T(8,128)S(1)}, f32[512,4096]{1,0:T(8,128)S(1)}, f32[8,128]{1,0:T(8,128)S(1)}) custom-call(f32[8,128]{1,0:T(8,128)S(1)} %get-tuple-element.45.refs_0_, f32[8,128]{1,0:T(8,128)S(1)} %collective-permute-done.19.refs_1_, f32[8,128]{1,0:T(8,128)S(1)} %collective-permute-done.20.refs_2_, ...), custom_call_target="tpu_custom_call" | custom-call | tf_op jit(solution)/shard_map/pallas_call | solution.py:378
  97.0 3.0 %collective-permute-start.22 = (f32[32,128]{1,0:T(8,128)S(1)}, f32[32,128]{1,0:T(8,128)S(1)}, u32[]{:S(2)}, u32[]{:S(2)}) collective-permute-start(f32[32,128]{1,0:T(8,128)S(1)} %get-tuple-element.49.a_ref), channel_id=1, source_target_pairs={{0,4},{1,5},{2,6},{3,7},{4,0},{5,1},{6,2},{7,3},{8,12},{9,13},{10,... | collective-permute-start | bytes 49160 | tf_op jit(solution)/shard_map/ppermute | solution.py:62
  100.0 0.8 collective-permute-done.22.b_ref
  100.8 10.8 %all_to_all.23 = f32[16,32,128]{2,1,0:T(8,128)S(1)} all-to-all(f32[16,32,128]{2,1,0:T(8,128)S(1)} %bitcast.8), channel_id=1, replica_groups={{0,8,16,24,32,40,48,56,64,72,80,88,96,104,112,120},{4,12,20,28,36,44,52..., dimensions={0} | all-to-all | bytes 524288 | tf_op jit(solution)/shard_map/all_to_all | solution.py:395
  111.6 3.8 %shard_map.51 = f32[512,4096]{1,0:T(8,128)} custom-call(f32[512,128]{1,0:T(8,128)S(1)} %bitcast.5, f32[512,4096]{1,0:T(8,128)S(1)} %get-tuple-element.50.refs_1_, f32[8,128]{1,0:T(8,128)S(1)} %get-tuple-element.51.refs_2_, f32[32,512,128]{2,1,0:T(8,128)S(1)} %get-tuple-element.47.refs_7_.refs_3_, ...), custom_call_target="tpu_custom_call" | custom-call | tf_op jit(solution)/shard_map/pallas_call | solution.py:378
  (19 shorter events, 0.2 us)
Async XLA Ops:
  0.6 0.9 copy-start
  1.5 0.7 copy-start.1
  2.3 6.3 %collective-permute-start.5 = (f32[128,256]{1,0:T(8,128)S(1)}, f32[128,256]{1,0:T(8,128)S(1)}, u32[]{:S(2)}, u32[]{:S(2)}) collective-permute-start(f32[128,256]{1,0:T(8,128)S(1)} %get-tuple-element.27), channel_id=1, source_target_pairs={{0,8},{1,9},{2,10},{3,11},{4,36},{5,37},{6,38},{7,39},{8,16},{9,17... | collective-permute-start | bytes 393224 | tf_op jit(solution)/shard_map/ppermute | solution.py:62
  4.5 6.9 %collective-permute-start.7 = (f32[128,256]{1,0:T(8,128)S(1)}, f32[128,256]{1,0:T(8,128)S(1)}, u32[]{:S(2)}, u32[]{:S(2)}) collective-permute-start(f32[128,256]{1,0:T(8,128)S(1)} %get-tuple-element.27), channel_id=1, source_target_pairs={{0,24},{1,25},{2,26},{3,27},{4,100},{5,101},{6,102},{7,103},{8,0},... | collective-permute-start | bytes 393224 | tf_op jit(solution)/shard_map/ppermute | solution.py:62
  6.0 5.3 %collective-permute-start.6 = (f32[128,256]{1,0:T(8,128)S(1)}, f32[128,256]{1,0:T(8,128)S(1)}, u32[]{:S(2)}, u32[]{:S(2)}) collective-permute-start(f32[128,256]{1,0:T(8,128)S(1)} %get-tuple-element.27), channel_id=1, source_target_pairs={{0,16},{1,17},{2,18},{3,19},{4,68},{5,69},{6,70},{7,71},{8,24},{9,... | collective-permute-start | bytes 393224 | tf_op jit(solution)/shard_map/ppermute | solution.py:62
  11.4 18.6 %collective-permute-start.13 = (f32[512,256]{1,0:T(8,128)S(1)}, f32[512,256]{1,0:T(8,128)S(1)}, u32[]{:S(2)}, u32[]{:S(2)}) collective-permute-start(f32[512,256]{1,0:T(8,128)S(1)} %constant_dynamic-update-slice_fusion.refs_4_), channel_id=1, source_target_pairs={{0,32},{1,33},{2,34},{3,35},{4,12},{5,13},{6,14},{7,15},{8,40},{9,... | collective-permute-start | bytes 1572872 | tf_op jit(solution)/shard_map/ppermute | solution.py:62
  12.7 17.9 %collective-permute-start.11 = (f32[512,256]{1,0:T(8,128)S(1)}, f32[512,256]{1,0:T(8,128)S(1)}, u32[]{:S(2)}, u32[]{:S(2)}) collective-permute-start(f32[512,256]{1,0:T(8,128)S(1)} %constant_dynamic-update-slice_fusion.refs_4_), channel_id=1, source_target_pairs={{0,96},{1,97},{2,98},{3,99},{4,28},{5,29},{6,30},{7,31},{8,104},{9... | collective-permute-start | bytes 1572872 | tf_op jit(solution)/shard_map/ppermute | solution.py:62
  14.3 16.3 %collective-permute-start.9 = (f32[512,256]{1,0:T(8,128)S(1)}, f32[512,256]{1,0:T(8,128)S(1)}, u32[]{:S(2)}, u32[]{:S(2)}) collective-permute-start(f32[512,256]{1,0:T(8,128)S(1)} %constant_dynamic-update-slice_fusion.refs_4_), channel_id=1, source_target_pairs={{0,64},{1,65},{2,66},{3,67},{4,20},{5,21},{6,22},{7,23},{8,72},{9,... | collective-permute-start | bytes 1572872 | tf_op jit(solution)/shard_map/ppermute | solution.py:62
  15.7 8.0 %collective-permute-start = (f32[128,256]{1,0:T(8,128)S(1)}, f32[128,256]{1,0:T(8,128)S(1)}, u32[]{:S(2)}, u32[]{:S(2)}) collective-permute-start(f32[128,256]{1,0:T(8,128)S(1)} %get-tuple-element.27), channel_id=1, source_target_pairs={{0,0},{1,1},{2,2},{3,3},{4,5},{5,6},{6,7},{7,4},{8,10},{9,11},{10,... | collective-permute-start | bytes 393224 | tf_op jit(solution)/shard_map/ppermute | solution.py:62
  23.7 8.2 %collective-permute-start.1 = (f32[128,256]{1,0:T(8,128)S(1)}, f32[128,256]{1,0:T(8,128)S(1)}, u32[]{:S(2)}, u32[]{:S(2)}) collective-permute-start(f32[128,256]{1,0:T(8,128)S(1)} %collective-permute-done), channel_id=1, source_target_pairs={{0,0},{1,33},{2,66},{3,99},{4,96},{5,1},{6,34},{7,67},{8,64},{9,97... | collective-permute-start | bytes 393224 | tf_op jit(solution)/shard_map/ppermute | solution.py:62
  29.9 22.4 %collective-permute-start.8 = (f32[512,256]{1,0:T(8,128)S(1)}, f32[512,256]{1,0:T(8,128)S(1)}, u32[]{:S(2)}, u32[]{:S(2)}) collective-permute-start(f32[512,256]{1,0:T(8,128)S(1)} %constant_dynamic-update-slice_fusion.refs_4_), channel_id=1, source_target_pairs={{0,4},{1,5},{2,6},{3,7},{4,0},{5,1},{6,2},{7,3},{8,12},{9,13},{10,... | collective-permute-start | bytes 1572872 | tf_op jit(solution)/shard_map/ppermute | solution.py:62
  30.0 23.5 %collective-permute-start.14 = (f32[512,256]{1,0:T(8,128)S(1)}, f32[512,256]{1,0:T(8,128)S(1)}, u32[]{:S(2)}, u32[]{:S(2)}) collective-permute-start(f32[512,256]{1,0:T(8,128)S(1)} %collective-permute-done.13.refs_1_), channel_id=1, source_target_pairs={{0,4},{1,5},{2,6},{3,7},{4,0},{5,1},{6,2},{7,3},{8,12},{9,13},{10,... | collective-permute-start | bytes 1572872 | tf_op jit(solution)/shard_map/ppermute | solution.py:62
  30.5 24.2 %collective-permute-start.12 = (f32[512,256]{1,0:T(8,128)S(1)}, f32[512,256]{1,0:T(8,128)S(1)}, u32[]{:S(2)}, u32[]{:S(2)}) collective-permute-start(f32[512,256]{1,0:T(8,128)S(1)} %collective-permute-done.11.refs_1_), channel_id=1, source_target_pairs={{0,4},{1,5},{2,6},{3,7},{4,0},{5,1},{6,2},{7,3},{8,12},{9,13},{10,... | collective-permute-start | bytes 1572872 | tf_op jit(solution)/shard_map/ppermute | solution.py:62
  30.6 25.3 %collective-permute-start.10 = (f32[512,256]{1,0:T(8,128)S(1)}, f32[512,256]{1,0:T(8,128)S(1)}, u32[]{:S(2)}, u32[]{:S(2)}) collective-permute-start(f32[512,256]{1,0:T(8,128)S(1)} %collective-permute-done.9.refs_1_), channel_id=1, source_target_pairs={{0,4},{1,5},{2,6},{3,7},{4,0},{5,1},{6,2},{7,3},{8,12},{9,13},{10,... | collective-permute-start | bytes 1572872 | tf_op jit(solution)/shard_map/ppermute | solution.py:62
  31.9 8.4 %collective-permute-start.4 = (f32[128,256]{1,0:T(8,128)S(1)}, f32[128,256]{1,0:T(8,128)S(1)}, u32[]{:S(2)}, u32[]{:S(2)}) collective-permute-start(f32[128,256]{1,0:T(8,128)S(1)} %collective-permute-done.1.refs_0_), channel_id=1, source_target_pairs={{0,3},{1,0},{2,1},{3,2},{4,7},{5,4},{6,5},{7,6},{8,11},{9,8},{10,9... | collective-permute-start | bytes 393224 | tf_op jit(solution)/shard_map/ppermute | solution.py:62
  40.3 6.1 %collective-permute-start.3 = (f32[128,256]{1,0:T(8,128)S(1)}, f32[128,256]{1,0:T(8,128)S(1)}, u32[]{:S(2)}, u32[]{:S(2)}) collective-permute-start(f32[128,256]{1,0:T(8,128)S(1)} %collective-permute-done.1.refs_0_), channel_id=1, source_target_pairs={{0,2},{1,3},{2,0},{3,1},{4,6},{5,7},{6,4},{7,5},{8,10},{9,11},{10,... | collective-permute-start | bytes 393224 | tf_op jit(solution)/shard_map/ppermute | solution.py:62
  46.4 6.0 %collective-permute-start.2 = (f32[128,256]{1,0:T(8,128)S(1)}, f32[128,256]{1,0:T(8,128)S(1)}, u32[]{:S(2)}, u32[]{:S(2)}) collective-permute-start(f32[128,256]{1,0:T(8,128)S(1)} %collective-permute-done.1.refs_0_), channel_id=1, source_target_pairs={{0,1},{1,2},{2,3},{3,0},{4,5},{5,6},{6,7},{7,4},{8,9},{9,10},{10,1... | collective-permute-start | bytes 393224 | tf_op jit(solution)/shard_map/ppermute | solution.py:62
  57.2 4.0 %collective-permute-start.17 = (f32[8,128]{1,0:T(8,128)S(1)}, f32[8,128]{1,0:T(8,128)S(1)}, u32[]{:S(2)}, u32[]{:S(2)}) collective-permute-start(f32[8,128]{1,0:T(8,128)S(1)} %get-tuple-element.36.refs_0_), channel_id=1, source_target_pairs={{0,2},{1,3},{2,0},{3,1},{4,6},{5,7},{6,4},{7,5},{8,10},{9,11},{10,... | collective-permute-start | bytes 12296 | tf_op jit(solution)/shard_map/ppermute | solution.py:62
  58.3 2.9 %collective-permute-start.16 = (f32[8,128]{1,0:T(8,128)S(1)}, f32[8,128]{1,0:T(8,128)S(1)}, u32[]{:S(2)}, u32[]{:S(2)}) collective-permute-start(f32[8,128]{1,0:T(8,128)S(1)} %get-tuple-element.36.refs_0_), channel_id=1, source_target_pairs={{0,3},{1,0},{2,1},{3,2},{4,7},{5,4},{6,5},{7,6},{8,11},{9,8},{10,9... | collective-permute-start | bytes 12296 | tf_op jit(solution)/shard_map/ppermute | solution.py:62
  59.4 4.0 %collective-permute-start.15 = (f32[8,128]{1,0:T(8,128)S(1)}, f32[8,128]{1,0:T(8,128)S(1)}, u32[]{:S(2)}, u32[]{:S(2)}) collective-permute-start(f32[8,128]{1,0:T(8,128)S(1)} %get-tuple-element.36.refs_0_), channel_id=1, source_target_pairs={{0,1},{1,2},{2,3},{3,0},{4,5},{5,6},{6,7},{7,4},{8,9},{9,10},{10,1... | collective-permute-start | bytes 12296 | tf_op jit(solution)/shard_map/ppermute | solution.py:62
  64.6 3.5 %collective-permute-start.18 = (f32[32,128]{1,0:T(8,128)S(1)}, f32[32,128]{1,0:T(8,128)S(1)}, u32[]{:S(2)}, u32[]{:S(2)}) collective-permute-start(f32[32,128]{1,0:T(8,128)S(1)} %get-tuple-element.41.a_ref), channel_id=1, source_target_pairs={{0,4},{1,5},{2,6},{3,7},{4,0},{5,1},{6,2},{7,3},{8,12},{9,13},{10,... | collective-permute-start | bytes 49160 | tf_op jit(solution)/shard_map/ppermute | solution.py:62
  86.3 4.0 %collective-permute-start.21 = (f32[8,128]{1,0:T(8,128)S(1)}, f32[8,128]{1,0:T(8,128)S(1)}, u32[]{:S(2)}, u32[]{:S(2)}) collective-permute-start(f32[8,128]{1,0:T(8,128)S(1)} %get-tuple-element.45.refs_0_), channel_id=1, source_target_pairs={{0,2},{1,3},{2,0},{3,1},{4,6},{5,7},{6,4},{7,5},{8,10},{9,11},{10,... | collective-permute-start | bytes 12296 | tf_op jit(solution)/shard_map/ppermute | solution.py:62
  87.7 2.6 %collective-permute-start.20 = (f32[8,128]{1,0:T(8,128)S(1)}, f32[8,128]{1,0:T(8,128)S(1)}, u32[]{:S(2)}, u32[]{:S(2)}) collective-permute-start(f32[8,128]{1,0:T(8,128)S(1)} %get-tuple-element.45.refs_0_), channel_id=1, source_target_pairs={{0,3},{1,0},{2,1},{3,2},{4,7},{5,4},{6,5},{7,6},{8,11},{9,8},{10,9... | collective-permute-start | bytes 12296 | tf_op jit(solution)/shard_map/ppermute | solution.py:62
  88.2 4.0 %collective-permute-start.19 = (f32[8,128]{1,0:T(8,128)S(1)}, f32[8,128]{1,0:T(8,128)S(1)}, u32[]{:S(2)}, u32[]{:S(2)}) collective-permute-start(f32[8,128]{1,0:T(8,128)S(1)} %get-tuple-element.45.refs_0_), channel_id=1, source_target_pairs={{0,1},{1,2},{2,3},{3,0},{4,5},{5,6},{6,7},{7,4},{8,9},{9,10},{10,1... | collective-permute-start | bytes 12296 | tf_op jit(solution)/shard_map/ppermute | solution.py:62
  97.0 3.8 %collective-permute-start.22 = (f32[32,128]{1,0:T(8,128)S(1)}, f32[32,128]{1,0:T(8,128)S(1)}, u32[]{:S(2)}, u32[]{:S(2)}) collective-permute-start(f32[32,128]{1,0:T(8,128)S(1)} %get-tuple-element.49.a_ref), channel_id=1, source_target_pairs={{0,4},{1,5},{2,6},{3,7},{4,0},{5,1},{6,2},{7,3},{8,12},{9,13},{10,... | collective-permute-start | bytes 49160 | tf_op jit(solution)/shard_map/ppermute | solution.py:62

commit v3 on v2

--- a/solution.py
+++ b/solution.py
@@ -74,6 +74,11 @@
     a = jnp.where(own == 0, (x - m) % 4, (x - k) % 4)
     b = jnp.where(own == 0, (y - k) % 4, (y - m) % 4)
     return b * 8 + a * 2 + own
+
+
+def offsets(at_ref, r):
+    for n in range(BLOCKS):
+        at_ref[n] = block_of(n, r) * LANES
 
 
 def has_diagonal(r, c):
@@ -277,8 +282,9 @@
 def second_sums_kernel(*refs):
     pieces, sum_ref, bs_ref, pref_ref, entry_ref, b_ref, s_rep, s, refs = (
         refs[:4], *refs[4:10], refs[10:14], refs[14:])
-    out_hbm, sum2_ref, out_ref, diag_ref, b2_ref, s2_ref, acc_ref, tt_ref, dd_ref, sem = refs
+    out_hbm, sum2_ref, out_ref, diag_ref, b2_ref, s2_ref, acc_ref, tt_ref, dd_ref, sem, at_ref = refs
     r, c = place()
+    offsets(at_ref, r)
     best2, second2 = merged(pieces)
     spread(best2, b2_ref)
     spread(second2, s2_ref)
@@ -307,7 +313,7 @@
             x = s[n // 8][n % 8, rows, :]
             gain = jnp.where(x >= b, v, 0.0) + jnp.where(entry_ref[n, rows, :] >= b2, v2, 0.0)
             fresh = (0.75 * x - base) + gain
-            out_ref[rows, pl.ds(pl.multiple_of(block_of(n, r) * LANES, LANES), LANES)] = fresh
+            out_ref[rows, pl.ds(pl.multiple_of(at_ref[n], LANES), LANES)] = fresh
             acc_ref[n] += jnp.sum(jnp.maximum(fresh, 0.0).reshape(TILE // 8, 8, LANES), axis=0)
 
         @pl.when(inside)
@@ -327,8 +333,9 @@
 
 def last_kernel(*refs):
     copies_ref, resp_ref, diag_ref, entry_ref, s, refs = *refs[:4], refs[4:8], refs[8:]
-    out_hbm, out_ref, total_ref, least_ref, tt_ref, dd_ref, sem = refs
+    out_hbm, out_ref, total_ref, least_ref, tt_ref, dd_ref, sem, at_ref = refs
     r, c = place()
+    offsets(at_ref, r)
     join_sums(copies_ref, tt_ref)
     for n in range(BLOCKS):
         total = jnp.broadcast_to(tt_ref[pl.ds(block_of(n, r), 1), :], (8, LANES))
@@ -346,7 +353,7 @@
     def body(t, carry):
         rows = pl.ds(pl.multiple_of(t * TILE, TILE), TILE)
         for n in range(BLOCKS):
-            at = pl.ds(pl.multiple_of(block_of(n, r) * LANES, LANES), LANES)
+            at = pl.ds(pl.multiple_of(at_ref[n], LANES), LANES)
             before = entry_ref[n, rows, :] - s[n // 8][n % 8, rows, :]
             total = jnp.tile(total_ref[n], (TILE // 8, 1))
             least = jnp.tile(least_ref[n], (TILE // 8, 1))
@@ -435,19 +442,20 @@
     )
     pieces = exchange(bs2)
     n_copies = ROWS // TILE
+    table = pltpu.SMEM((BLOCKS,), jnp.int32)
     out = ((ROWS, BLOCKS * LANES), "hbm")
     kept = ((ROWS, BLOCKS * LANES), "vmem")
     responsibility, second, resp, diag = call(
         second_sums_kernel,
         pieces + [first, bs, pref, entries, b_rep, s_rep, *s],
         [out, flat, kept, pair],
-        [big, big, acc, tt, small, pltpu.SemaphoreType.DMA((n_copies,))],
+        [big, big, acc, tt, small, pltpu.SemaphoreType.DMA((n_copies,)), table],
     )
     availability = call(
         last_kernel,
         [to_all_rows(second), resp, diag, entries, *s],
         [out],
-        [pltpu.VMEM((ROWS, BLOCKS * LANES), F32), acc, acc, tt, small, pltpu.SemaphoreType.DMA((n_copies,))],
+        [pltpu.VMEM((ROWS, BLOCKS * LANES), F32), acc, acc, tt, small, pltpu.SemaphoreType.DMA((n_copies,)), table],
         megabytes=12,
     )[0]
     return responsibility, availability

time: 116 us -> 115 us (level)
  no operation moved by 1% of the time
where the time goes in v3:
time: 115 us
  starting transfers between devices  41.7 us (36%)
  waiting for transfers between devices  27.7 us (24%)
  blocking collectives  26.3 us (23%)
  Pallas kernels  17 us (15%)
  local copies, waits for them, and re-layouts  1.62 us (1%)
    ppermute x23, starting transfers between devices, permute(): return lax.ppermute(a, BOTH, perm)  41.7 us
    ppermute x23, waiting for transfers between devices, permute(): return lax.ppermute(a, BOTH, perm)  27.7 us
    all_to_all x2, blocking collectives, to_all_rows(): lax.all_to_all(copies, 'row', 0, 0, tiled=True, axis_index_groups=groups)  26.3 us
    pallas_call x11, Pallas kernels, call(): pl.pallas_call(kernel, out_shape=tuple(shapes), in_specs=[vmem] * len(arg...  17 us
  transfers between devices with their start and end apart: 23, of which 13 were waited for; matrix products, arithmetic and copies ran while one was open for 0% of the time, Pallas kernels for 3%

profile of v3, /device:TPU:1, one launch (start us, length us, event | category | flops | bytes accessed | tf_op | source)
XLA Modules:
  0.0 115.2 jit_solution(314313404431194337)
XLA Ops:
  0.6 0.9 copy-done
  1.5 0.7 copy-done.1
  2.2 0.1 shard_map.41
  2.3 2.2 %collective-permute-start.5 = (f32[128,256]{1,0:T(8,128)S(1)}, f32[128,256]{1,0:T(8,128)S(1)}, u32[]{:S(2)}, u32[]{:S(2)}) collective-permute-start(f32[128,256]{1,0:T(8,128)S(1)} %get-tuple-element.27), channel_id=1, source_target_pairs={{0,8},{1,9},{2,10},{3,11},{4,36},{5,37},{6,38},{7,39},{8,16},{9,17... | collective-permute-start | bytes 393224 | tf_op jit(solution)/shard_map/ppermute | solution.py:62
  4.5 1.5 %collective-permute-start.7 = (f32[128,256]{1,0:T(8,128)S(1)}, f32[128,256]{1,0:T(8,128)S(1)}, u32[]{:S(2)}, u32[]{:S(2)}) collective-permute-start(f32[128,256]{1,0:T(8,128)S(1)} %get-tuple-element.27), channel_id=1, source_target_pairs={{0,24},{1,25},{2,26},{3,27},{4,100},{5,101},{6,102},{7,103},{8,0},... | collective-permute-start | bytes 393224 | tf_op jit(solution)/shard_map/ppermute | solution.py:62
  6.0 1.6 %collective-permute-start.6 = (f32[128,256]{1,0:T(8,128)S(1)}, f32[128,256]{1,0:T(8,128)S(1)}, u32[]{:S(2)}, u32[]{:S(2)}) collective-permute-start(f32[128,256]{1,0:T(8,128)S(1)} %get-tuple-element.27), channel_id=1, source_target_pairs={{0,16},{1,17},{2,18},{3,19},{4,68},{5,69},{6,70},{7,71},{8,24},{9,... | collective-permute-start | bytes 393224 | tf_op jit(solution)/shard_map/ppermute | solution.py:62
  7.6 1.0 collective-permute-done.5
  8.6 2.7 %collective-permute-done.6 = f32[128,256]{1,0:T(8,128)S(1)} collective-permute-done((f32[128,256]{1,0:T(8,128)S(1)}, f32[128,256]{1,0:T(8,128)S(1)}, u32[]{:S(2)}, u32[]{:S(2)}) %collective-permute-start.6) | collective-permute-done | bytes 131104 | tf_op jit(solution)/shard_map/ppermute | solution.py:62
  11.4 1.3 %collective-permute-start.13 = (f32[512,256]{1,0:T(8,128)S(1)}, f32[512,256]{1,0:T(8,128)S(1)}, u32[]{:S(2)}, u32[]{:S(2)}) collective-permute-start(f32[512,256]{1,0:T(8,128)S(1)} %constant_dynamic-update-slice_fusion.refs_4_), channel_id=1, source_target_pairs={{0,32},{1,33},{2,34},{3,35},{4,12},{5,13},{6,14},{7,15},{8,40},{9,... | collective-permute-start | bytes 1572872 | tf_op jit(solution)/shard_map/ppermute | solution.py:62
  12.7 1.6 %collective-permute-start.11 = (f32[512,256]{1,0:T(8,128)S(1)}, f32[512,256]{1,0:T(8,128)S(1)}, u32[]{:S(2)}, u32[]{:S(2)}) collective-permute-start(f32[512,256]{1,0:T(8,128)S(1)} %constant_dynamic-update-slice_fusion.refs_4_), channel_id=1, source_target_pairs={{0,96},{1,97},{2,98},{3,99},{4,28},{5,29},{6,30},{7,31},{8,104},{9... | collective-permute-start | bytes 1572872 | tf_op jit(solution)/shard_map/ppermute | solution.py:62
  14.3 1.4 %collective-permute-start.9 = (f32[512,256]{1,0:T(8,128)S(1)}, f32[512,256]{1,0:T(8,128)S(1)}, u32[]{:S(2)}, u32[]{:S(2)}) collective-permute-start(f32[512,256]{1,0:T(8,128)S(1)} %constant_dynamic-update-slice_fusion.refs_4_), channel_id=1, source_target_pairs={{0,64},{1,65},{2,66},{3,67},{4,20},{5,21},{6,22},{7,23},{8,72},{9,... | collective-permute-start | bytes 1572872 | tf_op jit(solution)/shard_map/ppermute | solution.py:62
  15.7 3.5 %collective-permute-start = (f32[128,256]{1,0:T(8,128)S(1)}, f32[128,256]{1,0:T(8,128)S(1)}, u32[]{:S(2)}, u32[]{:S(2)}) collective-permute-start(f32[128,256]{1,0:T(8,128)S(1)} %get-tuple-element.27), channel_id=1, source_target_pairs={{0,0},{1,1},{2,2},{3,3},{4,5},{5,6},{6,7},{7,4},{8,10},{9,11},{10,... | collective-permute-start | bytes 393224 | tf_op jit(solution)/shard_map/ppermute | solution.py:62
  19.2 4.5 %collective-permute-done = f32[128,256]{1,0:T(8,128)S(1)} collective-permute-done((f32[128,256]{1,0:T(8,128)S(1)}, f32[128,256]{1,0:T(8,128)S(1)}, u32[]{:S(2)}, u32[]{:S(2)}) %collective-permute-start) | collective-permute-done | bytes 131104 | tf_op jit(solution)/shard_map/ppermute | solution.py:62
  23.7 6.2 %collective-permute-start.1 = (f32[128,256]{1,0:T(8,128)S(1)}, f32[128,256]{1,0:T(8,128)S(1)}, u32[]{:S(2)}, u32[]{:S(2)}) collective-permute-start(f32[128,256]{1,0:T(8,128)S(1)} %collective-permute-done), channel_id=1, source_target_pairs={{0,0},{1,33},{2,66},{3,99},{4,96},{5,1},{6,34},{7,67},{8,64},{9,97... | collective-permute-start | bytes 393224 | tf_op jit(solution)/shard_map/ppermute | solution.py:62
  30.0 0.5 collective-permute-start.14
  30.5 0.1 collective-permute-start.12
  30.6 0.4 collective-permute-start.10
  31.0 0.8 collective-permute-done.1.refs_0_
  31.9 6.5 %collective-permute-start.4 = (f32[128,256]{1,0:T(8,128)S(1)}, f32[128,256]{1,0:T(8,128)S(1)}, u32[]{:S(2)}, u32[]{:S(2)}) collective-permute-start(f32[128,256]{1,0:T(8,128)S(1)} %collective-permute-done.1.refs_0_), channel_id=1, source_target_pairs={{0,3},{1,0},{2,1},{3,2},{4,7},{5,4},{6,5},{7,6},{8,11},{9,8},{10,9... | collective-permute-start | bytes 393224 | tf_op jit(solution)/shard_map/ppermute | solution.py:62
  38.3 1.9 %collective-permute-done.4.refs_3_ = f32[128,256]{1,0:T(8,128)S(1)} collective-permute-done((f32[128,256]{1,0:T(8,128)S(1)}, f32[128,256]{1,0:T(8,128)S(1)}, u32[]{:S(2)}, u32[]{:S(2)}) %collective-permute-start.4) | collective-permute-done | bytes 131104 | tf_op jit(solution)/shard_map/ppermute | solution.py:62
  40.3 2.9 %collective-permute-start.3 = (f32[128,256]{1,0:T(8,128)S(1)}, f32[128,256]{1,0:T(8,128)S(1)}, u32[]{:S(2)}, u32[]{:S(2)}) collective-permute-start(f32[128,256]{1,0:T(8,128)S(1)} %collective-permute-done.1.refs_0_), channel_id=1, source_target_pairs={{0,2},{1,3},{2,0},{3,1},{4,6},{5,7},{6,4},{7,5},{8,10},{9,11},{10,... | collective-permute-start | bytes 393224 | tf_op jit(solution)/shard_map/ppermute | solution.py:62
  43.2 3.2 %collective-permute-done.3.refs_2_ = f32[128,256]{1,0:T(8,128)S(1)} collective-permute-done((f32[128,256]{1,0:T(8,128)S(1)}, f32[128,256]{1,0:T(8,128)S(1)}, u32[]{:S(2)}, u32[]{:S(2)}) %collective-permute-start.3) | collective-permute-done | bytes 131104 | tf_op jit(solution)/shard_map/ppermute | solution.py:62
  46.4 0.6 collective-permute-start.2
  47.0 5.4 %collective-permute-done.2.refs_1_ = f32[128,256]{1,0:T(8,128)S(1)} collective-permute-done((f32[128,256]{1,0:T(8,128)S(1)}, f32[128,256]{1,0:T(8,128)S(1)}, u32[]{:S(2)}, u32[]{:S(2)}) %collective-permute-start.2) | collective-permute-done | bytes 131104 | tf_op jit(solution)/shard_map/ppermute | solution.py:62
  52.4 1.2 %shard_map.42 = (f32[8,512,128]{2,1,0:T(8,128)S(1)}, bf16[512,768]{1,0:T(8,128)(2,1)S(1)}, f32[512,128]{1,0:T(8,128)S(1)}, f32[512,128]{1,0:T(8,128)S(1)}) custom-call(f32[128,256]{1,0:T(8,128)S(1)} %collective-permute-done.1.refs_0_, f32[128,256]{1,0:T(8,128)S(1)} %collective-permute-done.2.refs_1_, f32[128,256]{1,0:T(8,128)S(1)} %collective-permute-done.3.refs_2_, ...), custom_call_target="tpu_custom_call" | custom-call | tf_op jit(solution)/shard_map/pallas_call | solution.py:385
  53.6 1.1 shard_map.43
  54.7 1.1 shard_map.44
  55.9 1.3 %shard_map.45 = (f32[8,512,128]{2,1,0:T(8,128)S(1)}, f32[8,128]{1,0:T(8,128)S(1)}) custom-call(bf16[512,768]{1,0:T(8,128)(2,1)S(1)} %get-tuple-element.28.refs_0_, f32[512,256]{1,0:T(8,128)S(1)} %collective-permute-done.9.refs_1_, f32[512,256]{1,0:T(8,128)S(1)} %collective-permute-done.10.refs_2_, f32[512,128]{1,0:T(8,128)S(1)} %get-tuple-element.33.refs_3_, ...), custom_call_target="tpu_custom_call" | custom-call | tf_op jit(solution)/shard_map/pallas_call | solution.py:385
  57.2 1.1 collective-permute-start.17
  58.3 1.1 collective-permute-start.16
  59.4 0.5 collective-permute-start.15
  59.9 1.3 %collective-permute-done.17.refs_3_ = f32[8,128]{1,0:T(8,128)S(1)} collective-permute-done((f32[8,128]{1,0:T(8,128)S(1)}, f32[8,128]{1,0:T(8,128)S(1)}, u32[]{:S(2)}, u32[]{:S(2)}) %collective-permute-start.17) | collective-permute-done | bytes 4128 | tf_op jit(solution)/shard_map/ppermute | solution.py:62
  61.2 2.2 %collective-permute-done.15.refs_1_ = f32[8,128]{1,0:T(8,128)S(1)} collective-permute-done((f32[8,128]{1,0:T(8,128)S(1)}, f32[8,128]{1,0:T(8,128)S(1)}, u32[]{:S(2)}, u32[]{:S(2)}) %collective-permute-start.15) | collective-permute-done | bytes 4128 | tf_op jit(solution)/shard_map/ppermute | solution.py:62
  63.4 1.3 %shard_map.46 = (f32[32,128]{1,0:T(8,128)S(1)}, f32[8,128]{1,0:T(8,128)S(1)}, f32[512,128]{1,0:T(8,128)S(1)}, f32[512,128]{1,0:T(8,128)S(1)}) custom-call(f32[8,128]{1,0:T(8,128)S(1)} %get-tuple-element.36.refs_0_, f32[8,128]{1,0:T(8,128)S(1)} %collective-permute-done.15.refs_1_, f32[8,128]{1,0:T(8,128)S(1)} %collective-permute-done.16.refs_2_, ...), custom_call_target="tpu_custom_call" | custom-call | tf_op jit(solution)/shard_map/pallas_call | solution.py:385
  64.6 2.7 %collective-permute-start.18 = (f32[32,128]{1,0:T(8,128)S(1)}, f32[32,128]{1,0:T(8,128)S(1)}, u32[]{:S(2)}, u32[]{:S(2)}) collective-permute-start(f32[32,128]{1,0:T(8,128)S(1)} %get-tuple-element.41.a_ref), channel_id=1, source_target_pairs={{0,4},{1,5},{2,6},{3,7},{4,0},{5,1},{6,2},{7,3},{8,12},{9,13},{10,... | collective-permute-start | bytes 49160 | tf_op jit(solution)/shard_map/ppermute | solution.py:62
  67.3 0.8 collective-permute-done.18.b_ref
  68.2 15.5 %all_to_all.22 = f32[16,32,128]{2,1,0:T(8,128)S(1)} all-to-all(f32[16,32,128]{2,1,0:T(8,128)S(1)} %bitcast.7), channel_id=1, replica_groups={{0,8,16,24,32,40,48,56,64,72,80,88,96,104,112,120},{4,12,20,28,36,44,52..., dimensions={0} | all-to-all | bytes 524288 | tf_op jit(solution)/shard_map/all_to_all | solution.py:402
  83.7 2.6 %shard_map.48 = (f32[8,128]{1,0:T(8,128)S(1)}, f32[32,512,128]{2,1,0:T(8,128)S(1)}, f32[32,128]{1,0:T(8,128)S(1)}) custom-call(f32[512,128]{1,0:T(8,128)S(1)} %bitcast.6, f32[8,128]{1,0:T(8,128)S(1)} %get-tuple-element.42.refs_1_.refs_5_, f32[4,128]{1,0:T(4,128)S(1)} %get-tuple-element.35.refs_5_.refs_4_.refs_2_.refs_6_, ...), custom_call_target="tpu_custom_call" | custom-call | tf_op jit(solution)/shard_map/pallas_call | solution.py:385
  86.3 1.4 %collective-permute-start.21 = (f32[8,128]{1,0:T(8,128)S(1)}, f32[8,128]{1,0:T(8,128)S(1)}, u32[]{:S(2)}, u32[]{:S(2)}) collective-permute-start(f32[8,128]{1,0:T(8,128)S(1)} %get-tuple-element.45.refs_0_), channel_id=1, source_target_pairs={{0,2},{1,3},{2,0},{3,1},{4,6},{5,7},{6,4},{7,5},{8,10},{9,11},{10,... | collective-permute-start | bytes 12296 | tf_op jit(solution)/shard_map/ppermute | solution.py:62
  87.7 0.5 collective-permute-start.20
  88.2 1.0 collective-permute-start.19
  89.2 1.1 collective-permute-done.21.refs_3_
  90.3 1.8 %collective-permute-done.19.refs_1_ = f32[8,128]{1,0:T(8,128)S(1)} collective-permute-done((f32[8,128]{1,0:T(8,128)S(1)}, f32[8,128]{1,0:T(8,128)S(1)}, u32[]{:S(2)}, u32[]{:S(2)}) %collective-permute-start.19) | collective-permute-done | bytes 4128 | tf_op jit(solution)/shard_map/ppermute | solution.py:62
  92.1 4.6 %shard_map.49 = (f32[512,4096]{1,0:T(8,128)}, f32[32,128]{1,0:T(8,128)S(1)}, f32[512,4096]{1,0:T(8,128)S(1)}, f32[8,128]{1,0:T(8,128)S(1)}) custom-call(f32[8,128]{1,0:T(8,128)S(1)} %get-tuple-element.45.refs_0_, f32[8,128]{1,0:T(8,128)S(1)} %collective-permute-done.19.refs_1_, f32[8,128]{1,0:T(8,128)S(1)} %collective-permute-done.20.refs_2_, ...), custom_call_target="tpu_custom_call" | custom-call | tf_op jit(solution)/shard_map/pallas_call | solution.py:385
  96.7 3.0 %collective-permute-start.22 = (f32[32,128]{1,0:T(8,128)S(1)}, f32[32,128]{1,0:T(8,128)S(1)}, u32[]{:S(2)}, u32[]{:S(2)}) collective-permute-start(f32[32,128]{1,0:T(8,128)S(1)} %get-tuple-element.49.a_ref), channel_id=1, source_target_pairs={{0,4},{1,5},{2,6},{3,7},{4,0},{5,1},{6,2},{7,3},{8,12},{9,13},{10,... | collective-permute-start | bytes 49160 | tf_op jit(solution)/shard_map/ppermute | solution.py:62
  99.7 0.8 collective-permute-done.22.b_ref
  100.6 10.8 %all_to_all.23 = f32[16,32,128]{2,1,0:T(8,128)S(1)} all-to-all(f32[16,32,128]{2,1,0:T(8,128)S(1)} %bitcast.8), channel_id=1, replica_groups={{0,8,16,24,32,40,48,56,64,72,80,88,96,104,112,120},{4,12,20,28,36,44,52..., dimensions={0} | all-to-all | bytes 524288 | tf_op jit(solution)/shard_map/all_to_all | solution.py:402
  111.4 3.8 %shard_map.51 = f32[512,4096]{1,0:T(8,128)} custom-call(f32[512,128]{1,0:T(8,128)S(1)} %bitcast.5, f32[512,4096]{1,0:T(8,128)S(1)} %get-tuple-element.50.refs_1_, f32[8,128]{1,0:T(8,128)S(1)} %get-tuple-element.51.refs_2_, f32[32,512,128]{2,1,0:T(8,128)S(1)} %get-tuple-element.47.refs_7_.refs_3_, ...), custom_call_target="tpu_custom_call" | custom-call | tf_op jit(solution)/shard_map/pallas_call | solution.py:385
  (19 shorter events, 0.2 us)
Async XLA Ops:
  0.6 0.9 copy-start
  1.5 0.7 copy-start.1
  2.3 6.3 %collective-permute-start.5 = (f32[128,256]{1,0:T(8,128)S(1)}, f32[128,256]{1,0:T(8,128)S(1)}, u32[]{:S(2)}, u32[]{:S(2)}) collective-permute-start(f32[128,256]{1,0:T(8,128)S(1)} %get-tuple-element.27), channel_id=1, source_target_pairs={{0,8},{1,9},{2,10},{3,11},{4,36},{5,37},{6,38},{7,39},{8,16},{9,17... | collective-permute-start | bytes 393224 | tf_op jit(solution)/shard_map/ppermute | solution.py:62
  4.5 6.9 %collective-permute-start.7 = (f32[128,256]{1,0:T(8,128)S(1)}, f32[128,256]{1,0:T(8,128)S(1)}, u32[]{:S(2)}, u32[]{:S(2)}) collective-permute-start(f32[128,256]{1,0:T(8,128)S(1)} %get-tuple-element.27), channel_id=1, source_target_pairs={{0,24},{1,25},{2,26},{3,27},{4,100},{5,101},{6,102},{7,103},{8,0},... | collective-permute-start | bytes 393224 | tf_op jit(solution)/shard_map/ppermute | solution.py:62
  6.0 5.3 %collective-permute-start.6 = (f32[128,256]{1,0:T(8,128)S(1)}, f32[128,256]{1,0:T(8,128)S(1)}, u32[]{:S(2)}, u32[]{:S(2)}) collective-permute-start(f32[128,256]{1,0:T(8,128)S(1)} %get-tuple-element.27), channel_id=1, source_target_pairs={{0,16},{1,17},{2,18},{3,19},{4,68},{5,69},{6,70},{7,71},{8,24},{9,... | collective-permute-start | bytes 393224 | tf_op jit(solution)/shard_map/ppermute | solution.py:62
  11.4 18.6 %collective-permute-start.13 = (f32[512,256]{1,0:T(8,128)S(1)}, f32[512,256]{1,0:T(8,128)S(1)}, u32[]{:S(2)}, u32[]{:S(2)}) collective-permute-start(f32[512,256]{1,0:T(8,128)S(1)} %constant_dynamic-update-slice_fusion.refs_4_), channel_id=1, source_target_pairs={{0,32},{1,33},{2,34},{3,35},{4,12},{5,13},{6,14},{7,15},{8,40},{9,... | collective-permute-start | bytes 1572872 | tf_op jit(solution)/shard_map/ppermute | solution.py:62
  12.7 17.9 %collective-permute-start.11 = (f32[512,256]{1,0:T(8,128)S(1)}, f32[512,256]{1,0:T(8,128)S(1)}, u32[]{:S(2)}, u32[]{:S(2)}) collective-permute-start(f32[512,256]{1,0:T(8,128)S(1)} %constant_dynamic-update-slice_fusion.refs_4_), channel_id=1, source_target_pairs={{0,96},{1,97},{2,98},{3,99},{4,28},{5,29},{6,30},{7,31},{8,104},{9... | collective-permute-start | bytes 1572872 | tf_op jit(solution)/shard_map/ppermute | solution.py:62
  14.3 16.3 %collective-permute-start.9 = (f32[512,256]{1,0:T(8,128)S(1)}, f32[512,256]{1,0:T(8,128)S(1)}, u32[]{:S(2)}, u32[]{:S(2)}) collective-permute-start(f32[512,256]{1,0:T(8,128)S(1)} %constant_dynamic-update-slice_fusion.refs_4_), channel_id=1, source_target_pairs={{0,64},{1,65},{2,66},{3,67},{4,20},{5,21},{6,22},{7,23},{8,72},{9,... | collective-permute-start | bytes 1572872 | tf_op jit(solution)/shard_map/ppermute | solution.py:62
  15.7 8.0 %collective-permute-start = (f32[128,256]{1,0:T(8,128)S(1)}, f32[128,256]{1,0:T(8,128)S(1)}, u32[]{:S(2)}, u32[]{:S(2)}) collective-permute-start(f32[128,256]{1,0:T(8,128)S(1)} %get-tuple-element.27), channel_id=1, source_target_pairs={{0,0},{1,1},{2,2},{3,3},{4,5},{5,6},{6,7},{7,4},{8,10},{9,11},{10,... | collective-permute-start | bytes 393224 | tf_op jit(solution)/shard_map/ppermute | solution.py:62
  23.7 8.2 %collective-permute-start.1 = (f32[128,256]{1,0:T(8,128)S(1)}, f32[128,256]{1,0:T(8,128)S(1)}, u32[]{:S(2)}, u32[]{:S(2)}) collective-permute-start(f32[128,256]{1,0:T(8,128)S(1)} %collective-permute-done), channel_id=1, source_target_pairs={{0,0},{1,33},{2,66},{3,99},{4,96},{5,1},{6,34},{7,67},{8,64},{9,97... | collective-permute-start | bytes 393224 | tf_op jit(solution)/shard_map/ppermute | solution.py:62
  29.9 22.4 %collective-permute-start.8 = (f32[512,256]{1,0:T(8,128)S(1)}, f32[512,256]{1,0:T(8,128)S(1)}, u32[]{:S(2)}, u32[]{:S(2)}) collective-permute-start(f32[512,256]{1,0:T(8,128)S(1)} %constant_dynamic-update-slice_fusion.refs_4_), channel_id=1, source_target_pairs={{0,4},{1,5},{2,6},{3,7},{4,0},{5,1},{6,2},{7,3},{8,12},{9,13},{10,... | collective-permute-start | bytes 1572872 | tf_op jit(solution)/shard_map/ppermute | solution.py:62
  30.0 23.5 %collective-permute-start.14 = (f32[512,256]{1,0:T(8,128)S(1)}, f32[512,256]{1,0:T(8,128)S(1)}, u32[]{:S(2)}, u32[]{:S(2)}) collective-permute-start(f32[512,256]{1,0:T(8,128)S(1)} %collective-permute-done.13.refs_1_), channel_id=1, source_target_pairs={{0,4},{1,5},{2,6},{3,7},{4,0},{5,1},{6,2},{7,3},{8,12},{9,13},{10,... | collective-permute-start | bytes 1572872 | tf_op jit(solution)/shard_map/ppermute | solution.py:62
  30.5 24.2 %collective-permute-start.12 = (f32[512,256]{1,0:T(8,128)S(1)}, f32[512,256]{1,0:T(8,128)S(1)}, u32[]{:S(2)}, u32[]{:S(2)}) collective-permute-start(f32[512,256]{1,0:T(8,128)S(1)} %collective-permute-done.11.refs_1_), channel_id=1, source_target_pairs={{0,4},{1,5},{2,6},{3,7},{4,0},{5,1},{6,2},{7,3},{8,12},{9,13},{10,... | collective-permute-start | bytes 1572872 | tf_op jit(solution)/shard_map/ppermute | solution.py:62
  30.6 25.3 %collective-permute-start.10 = (f32[512,256]{1,0:T(8,128)S(1)}, f32[512,256]{1,0:T(8,128)S(1)}, u32[]{:S(2)}, u32[]{:S(2)}) collective-permute-start(f32[512,256]{1,0:T(8,128)S(1)} %collective-permute-done.9.refs_1_), channel_id=1, source_target_pairs={{0,4},{1,5},{2,6},{3,7},{4,0},{5,1},{6,2},{7,3},{8,12},{9,13},{10,... | collective-permute-start | bytes 1572872 | tf_op jit(solution)/shard_map/ppermute | solution.py:62
  31.9 8.4 %collective-permute-start.4 = (f32[128,256]{1,0:T(8,128)S(1)}, f32[128,256]{1,0:T(8,128)S(1)}, u32[]{:S(2)}, u32[]{:S(2)}) collective-permute-start(f32[128,256]{1,0:T(8,128)S(1)} %collective-permute-done.1.refs_0_), channel_id=1, source_target_pairs={{0,3},{1,0},{2,1},{3,2},{4,7},{5,4},{6,5},{7,6},{8,11},{9,8},{10,9... | collective-permute-start | bytes 393224 | tf_op jit(solution)/shard_map/ppermute | solution.py:62
  40.3 6.1 %collective-permute-start.3 = (f32[128,256]{1,0:T(8,128)S(1)}, f32[128,256]{1,0:T(8,128)S(1)}, u32[]{:S(2)}, u32[]{:S(2)}) collective-permute-start(f32[128,256]{1,0:T(8,128)S(1)} %collective-permute-done.1.refs_0_), channel_id=1, source_target_pairs={{0,2},{1,3},{2,0},{3,1},{4,6},{5,7},{6,4},{7,5},{8,10},{9,11},{10,... | collective-permute-start | bytes 393224 | tf_op jit(solution)/shard_map/ppermute | solution.py:62
  46.4 6.0 %collective-permute-start.2 = (f32[128,256]{1,0:T(8,128)S(1)}, f32[128,256]{1,0:T(8,128)S(1)}, u32[]{:S(2)}, u32[]{:S(2)}) collective-permute-start(f32[128,256]{1,0:T(8,128)S(1)} %collective-permute-done.1.refs_0_), channel_id=1, source_target_pairs={{0,1},{1,2},{2,3},{3,0},{4,5},{5,6},{6,7},{7,4},{8,9},{9,10},{10,1... | collective-permute-start | bytes 393224 | tf_op jit(solution)/shard_map/ppermute | solution.py:62
  57.2 4.0 %collective-permute-start.17 = (f32[8,128]{1,0:T(8,128)S(1)}, f32[8,128]{1,0:T(8,128)S(1)}, u32[]{:S(2)}, u32[]{:S(2)}) collective-permute-start(f32[8,128]{1,0:T(8,128)S(1)} %get-tuple-element.36.refs_0_), channel_id=1, source_target_pairs={{0,2},{1,3},{2,0},{3,1},{4,6},{5,7},{6,4},{7,5},{8,10},{9,11},{10,... | collective-permute-start | bytes 12296 | tf_op jit(solution)/shard_map/ppermute | solution.py:62
  58.3 2.9 %collective-permute-start.16 = (f32[8,128]{1,0:T(8,128)S(1)}, f32[8,128]{1,0:T(8,128)S(1)}, u32[]{:S(2)}, u32[]{:S(2)}) collective-permute-start(f32[8,128]{1,0:T(8,128)S(1)} %get-tuple-element.36.refs_0_), channel_id=1, source_target_pairs={{0,3},{1,0},{2,1},{3,2},{4,7},{5,4},{6,5},{7,6},{8,11},{9,8},{10,9... | collective-permute-start | bytes 12296 | tf_op jit(solution)/shard_map/ppermute | solution.py:62
  59.4 4.0 %collective-permute-start.15 = (f32[8,128]{1,0:T(8,128)S(1)}, f32[8,128]{1,0:T(8,128)S(1)}, u32[]{:S(2)}, u32[]{:S(2)}) collective-permute-start(f32[8,128]{1,0:T(8,128)S(1)} %get-tuple-element.36.refs_0_), channel_id=1, source_target_pairs={{0,1},{1,2},{2,3},{3,0},{4,5},{5,6},{6,7},{7,4},{8,9},{9,10},{10,1... | collective-permute-start | bytes 12296 | tf_op jit(solution)/shard_map/ppermute | solution.py:62
  64.6 3.5 %collective-permute-start.18 = (f32[32,128]{1,0:T(8,128)S(1)}, f32[32,128]{1,0:T(8,128)S(1)}, u32[]{:S(2)}, u32[]{:S(2)}) collective-permute-start(f32[32,128]{1,0:T(8,128)S(1)} %get-tuple-element.41.a_ref), channel_id=1, source_target_pairs={{0,4},{1,5},{2,6},{3,7},{4,0},{5,1},{6,2},{7,3},{8,12},{9,13},{10,... | collective-permute-start | bytes 49160 | tf_op jit(solution)/shard_map/ppermute | solution.py:62
  86.3 4.0 %collective-permute-start.21 = (f32[8,128]{1,0:T(8,128)S(1)}, f32[8,128]{1,0:T(8,128)S(1)}, u32[]{:S(2)}, u32[]{:S(2)}) collective-permute-start(f32[8,128]{1,0:T(8,128)S(1)} %get-tuple-element.45.refs_0_), channel_id=1, source_target_pairs={{0,2},{1,3},{2,0},{3,1},{4,6},{5,7},{6,4},{7,5},{8,10},{9,11},{10,... | collective-permute-start | bytes 12296 | tf_op jit(solution)/shard_map/ppermute | solution.py:62
  87.7 2.6 %collective-permute-start.20 = (f32[8,128]{1,0:T(8,128)S(1)}, f32[8,128]{1,0:T(8,128)S(1)}, u32[]{:S(2)}, u32[]{:S(2)}) collective-permute-start(f32[8,128]{1,0:T(8,128)S(1)} %get-tuple-element.45.refs_0_), channel_id=1, source_target_pairs={{0,3},{1,0},{2,1},{3,2},{4,7},{5,4},{6,5},{7,6},{8,11},{9,8},{10,9... | collective-permute-start | bytes 12296 | tf_op jit(solution)/shard_map/ppermute | solution.py:62
  88.2 4.0 %collective-permute-start.19 = (f32[8,128]{1,0:T(8,128)S(1)}, f32[8,128]{1,0:T(8,128)S(1)}, u32[]{:S(2)}, u32[]{:S(2)}) collective-permute-start(f32[8,128]{1,0:T(8,128)S(1)} %get-tuple-element.45.refs_0_), channel_id=1, source_target_pairs={{0,1},{1,2},{2,3},{3,0},{4,5},{5,6},{6,7},{7,4},{8,9},{9,10},{10,1... | collective-permute-start | bytes 12296 | tf_op jit(solution)/shard_map/ppermute | solution.py:62
  96.7 3.8 %collective-permute-start.22 = (f32[32,128]{1,0:T(8,128)S(1)}, f32[32,128]{1,0:T(8,128)S(1)}, u32[]{:S(2)}, u32[]{:S(2)}) collective-permute-start(f32[32,128]{1,0:T(8,128)S(1)} %get-tuple-element.49.a_ref), channel_id=1, source_target_pairs={{0,4},{1,5},{2,6},{3,7},{4,0},{5,1},{6,2},{7,3},{8,12},{9,13},{10,... | collective-permute-start | bytes 49160 | tf_op jit(solution)/shard_map/ppermute | solution.py:62

commit v4 on v3

--- a/solution.py
+++ b/solution.py
@@ -10,6 +10,7 @@
 SHARD, ROWS, D, LANES = 128, 512, 256, 128
 BLOCKS = 32
 TILE = 64
+EARLY = 6
 HOLE = -1e30
 BOTH = ("row", "col")
 F32 = jnp.float32
@@ -148,8 +149,14 @@
     return jnp.concatenate([tt_ref[pl.ds(4 * (r % 8) + j, 1), :] for j in range(4)], 0)
 
 
-def unit_kernel(x_ref, levels_ref, o_ref, pref_ref):
+def preference_kernel(levels_ref, pref_ref):
     pref_ref[...] = 0.25 * levels_ref[...].astype(F32) - 1.0
+
+
+def unit_kernel(x_hbm, o_ref, x_ref, sem):
+    copy = pltpu.make_async_copy(x_hbm, x_ref, sem)
+    copy.start()
+    copy.wait()
     x = x_ref[...]
     o_ref[...] = x * lax.rsqrt(jnp.sum(x * x, axis=1, keepdims=True) + 1e-06)
 
@@ -322,13 +329,24 @@
             value = jnp.tile(dd_ref[t // 2], (TILE // 8, 1))
             out_ref[rows, at] = jnp.where(eye_of(t % 2), value, out_ref[rows, at])
 
-        copy(t).start()
+
+        @pl.when(t < EARLY)
+        def _():
+            copy(t).start()
+
         return carry
 
     lax.fori_loop(0, ROWS // TILE, body, 0)
     write_sums(acc_ref, tt_ref, diag2, r, c, sum2_ref)
-    for t in range(ROWS // TILE):
+    for t in range(EARLY):
         copy(t).wait()
+
+
+def rest_kernel(resp_ref, given_hbm, out_hbm, sem):
+    rows = pl.ds(EARLY * TILE, ROWS - EARLY * TILE)
+    copy = pltpu.make_async_copy(resp_ref.at[rows, :], out_hbm.at[rows, :], sem)
+    copy.start()
+    copy.wait()
 
 
 def last_kernel(*refs):
@@ -404,7 +422,16 @@
 
 def propagate(embeddings, levels):
     levels = levels.reshape(4, LANES)
-    unit, pref = call(unit_kernel, [embeddings, levels], [((SHARD, D), "vmem"), ((4, LANES), "vmem")])
+    unit = pl.pallas_call(
+        unit_kernel,
+        out_shape=pltpu.VMEM((SHARD, D), F32),
+        in_specs=[pl.BlockSpec(memory_space=pl.ANY)],
+        out_specs=pl.BlockSpec(memory_space=pltpu.VMEM),
+        scratch_shapes=[pltpu.VMEM((SHARD, D), F32), pltpu.SemaphoreType.DMA(())],
+        compiler_params=pltpu.CompilerParams(vmem_limit_bytes=4 * 2**20),
+        name="unit",
+    )(embeddings)
+    pref = call(preference_kernel, [levels], [((4, LANES), "vmem")])[0]
     mine = permute(permute(unit, col_turn()), to_row_block())
     line = [unit] + [permute(unit, plane_shift(k, 1)) for k in (1, 2, 3)]
     line = jnp.concatenate(line, axis=0)
@@ -451,6 +478,16 @@
         [out, flat, kept, pair],
         [big, big, acc, tt, small, pltpu.SemaphoreType.DMA((n_copies,)), table],
     )
+    responsibility = pl.pallas_call(
+        rest_kernel,
+        out_shape=jax.ShapeDtypeStruct((ROWS, BLOCKS * LANES), F32),
+        in_specs=[pl.BlockSpec(memory_space=pltpu.VMEM), pl.BlockSpec(memory_space=pl.ANY)],
+        out_specs=pl.BlockSpec(memory_space=pl.ANY),
+        scratch_shapes=[pltpu.SemaphoreType.DMA(())],
+        input_output_aliases={1: 0},
+        compiler_params=pltpu.CompilerParams(vmem_limit_bytes=4 * 2**20),
+        name="rest",
+    )(pltpu.with_memory_space_constraint(resp, pltpu.VMEM), responsibility)
     availability = call(
         last_kernel,
         [to_all_rows(second), resp, diag, entries, *s],

time: 115 us -> 131 us (1.14)
  local copies, waits for them, and re-layouts: 1.62 us -> 19.9 us
  blocking collectives: 26.3 us -> 14.7 us
  waiting for transfers between devices: 27.7 us -> 34.6 us
  Pallas kernels: 17 us -> 18.4 us
    unnamed x7 -> x26, local copies, waits for them, and re-layouts: 1.61 us -> 19.9 us
    all_to_all x2 -> x1, blocking collectives: 26.3 us -> 14.7 us  [to_all_rows(): lax.all_to_all(copies, 'row', 0, 0, tiled=True, axis_index_groups=groups)]
    all_to_all x0 -> x1, waiting for transfers between devices: none -> 3.68 us  [to_all_rows(): lax.all_to_all(copies, 'row', 0, 0, tiled=True, axis_index_groups=groups)]
    all_to_all x0 -> x1, starting transfers between devices: none -> 3.53 us  [to_all_rows(): lax.all_to_all(copies, 'row', 0, 0, tiled=True, axis_index_groups=groups)]
    ppermute x23, starting transfers between devices: 41.7 us -> 38.4 us  [permute(): return lax.ppermute(a, BOTH, perm)]
    ppermute x23, waiting for transfers between devices: 27.7 us -> 30.9 us  [permute(): return lax.ppermute(a, BOTH, perm)]
    pallas_call x0 -> x2, Pallas kernels: none -> 1.57 us  [the longest x1 1.33 us: propagate(): pl.pallas_call(rest_kernel, out_shape=jax.ShapeDtypeStruct((ROWS, BLOCKS...]
  transfers between devices with their start and end apart: 23 -> 24, of which waited for: 13 -> 15; matrix products, arithmetic and copies ran while one was open for 0% -> 0% of each run, Pallas kernels for 3% -> 4%
where the time goes in v4:
time: 131 us; the launch traced here: 130 us
  starting transfers between devices  41.9 us (32%)
  waiting for transfers between devices  34.6 us (26%)
  local copies, waits for them, and re-layouts  19.9 us (15%)
  Pallas kernels  18.4 us (14%)
  blocking collectives  14.7 us (11%)
    ppermute x23, starting transfers between devices, permute(): return lax.ppermute(a, BOTH, perm)  38.4 us
    ppermute x23, waiting for transfers between devices, permute(): return lax.ppermute(a, BOTH, perm)  30.9 us
    unnamed x26, local copies, waits for them, and re-layouts  19.9 us
    pallas_call x11, Pallas kernels, call(): pl.pallas_call(kernel, out_shape=tuple(shapes), in_specs=[vmem] * len(arg...  16.8 us
    all_to_all x1, blocking collectives, to_all_rows(): lax.all_to_all(copies, 'row', 0, 0, tiled=True, axis_index_groups=groups)  14.7 us
    all_to_all x1, waiting for transfers between devices, to_all_rows(): lax.all_to_all(copies, 'row', 0, 0, tiled=True, axis_index_groups=groups)  3.68 us
    all_to_all x1, starting transfers between devices, to_all_rows(): lax.all_to_all(copies, 'row', 0, 0, tiled=True, axis_index_groups=groups)  3.53 us
  transfers between devices with their start and end apart: 24, of which 15 were waited for; matrix products, arithmetic and copies ran while one was open for 0% of the time, Pallas kernels for 4%

profile of v4, /device:TPU:1, one launch (start us, length us, event | category | flops | bytes accessed | tf_op | source)
XLA Modules:
  0.0 130.5 jit_solution(2151658048129495452)
XLA Ops:
  0.6 0.9 copy-done.11
  1.8 3.6 %collective-permute-start.7 = (f32[128,256]{1,0:T(8,128)S(1)}, f32[128,256]{1,0:T(8,128)S(1)}, u32[]{:S(2)}, u32[]{:S(2)}) collective-permute-start(f32[128,256]{1,0:T(8,128)S(1)} %unit.1), channel_id=1, source_target_pairs={{0,24},{1,25},{2,26},{3,27},{4,100},{5,101},{6,102},{7,103},{8,0},... | collective-permute-start | bytes 393224 | tf_op jit(solution)/shard_map/ppermute | solution.py:63
  6.5 2.3 %collective-permute-done.7 = f32[128,256]{1,0:T(8,128)S(1)} collective-permute-done((f32[128,256]{1,0:T(8,128)S(1)}, f32[128,256]{1,0:T(8,128)S(1)}, u32[]{:S(2)}, u32[]{:S(2)}) %collective-permute-start.7) | collective-permute-done | bytes 131104 | tf_op jit(solution)/shard_map/ppermute | solution.py:63
  8.7 2.3 %collective-permute-done.6 = f32[128,256]{1,0:T(8,128)S(1)} collective-permute-done((f32[128,256]{1,0:T(8,128)S(1)}, f32[128,256]{1,0:T(8,128)S(1)}, u32[]{:S(2)}, u32[]{:S(2)}) %collective-permute-start.6) | collective-permute-done | bytes 131104 | tf_op jit(solution)/shard_map/ppermute | solution.py:63
  11.0 1.4 %collective-permute-done.5 = f32[128,256]{1,0:T(8,128)S(1)} collective-permute-done((f32[128,256]{1,0:T(8,128)S(1)}, f32[128,256]{1,0:T(8,128)S(1)}, u32[]{:S(2)}, u32[]{:S(2)}) %collective-permute-start.5) | collective-permute-done | bytes 131104 | tf_op jit(solution)/shard_map/ppermute | solution.py:63
  12.5 1.0 collective-permute-start.13
  13.5 1.8 %collective-permute-start.11 = (f32[512,256]{1,0:T(8,128)S(1)}, f32[512,256]{1,0:T(8,128)S(1)}, u32[]{:S(2)}, u32[]{:S(2)}) collective-permute-start(f32[512,256]{1,0:T(8,128)S(1)} %pad_maximum_fusion.refs_4_), channel_id=1, source_target_pairs={{0,96},{1,97},{2,98},{3,99},{4,28},{5,29},{6,30},{7,31},{8,104},{9... | collective-permute-start | bytes 1572872 | tf_op jit(solution)/shard_map/ppermute | solution.py:63
  15.2 1.2 collective-permute-start.9
  16.5 3.5 %collective-permute-start = (f32[128,256]{1,0:T(8,128)S(1)}, f32[128,256]{1,0:T(8,128)S(1)}, u32[]{:S(2)}, u32[]{:S(2)}) collective-permute-start(f32[128,256]{1,0:T(8,128)S(1)} %unit.1), channel_id=1, source_target_pairs={{0,0},{1,1},{2,2},{3,3},{4,5},{5,6},{6,7},{7,4},{8,10},{9,11},{10,... | collective-permute-start | bytes 393224 | tf_op jit(solution)/shard_map/ppermute | solution.py:63
  20.0 4.5 %collective-permute-done = f32[128,256]{1,0:T(8,128)S(1)} collective-permute-done((f32[128,256]{1,0:T(8,128)S(1)}, f32[128,256]{1,0:T(8,128)S(1)}, u32[]{:S(2)}, u32[]{:S(2)}) %collective-permute-start) | collective-permute-done | bytes 131104 | tf_op jit(solution)/shard_map/ppermute | solution.py:63
  24.5 5.9 %collective-permute-start.1 = (f32[128,256]{1,0:T(8,128)S(1)}, f32[128,256]{1,0:T(8,128)S(1)}, u32[]{:S(2)}, u32[]{:S(2)}) collective-permute-start(f32[128,256]{1,0:T(8,128)S(1)} %collective-permute-done), channel_id=1, source_target_pairs={{0,0},{1,33},{2,66},{3,99},{4,96},{5,1},{6,34},{7,67},{8,64},{9,97... | collective-permute-start | bytes 393224 | tf_op jit(solution)/shard_map/ppermute | solution.py:63
  31.4 0.8 collective-permute-done.1.refs_0_
  32.2 6.0 %collective-permute-start.4 = (f32[128,256]{1,0:T(8,128)S(1)}, f32[128,256]{1,0:T(8,128)S(1)}, u32[]{:S(2)}, u32[]{:S(2)}) collective-permute-start(f32[128,256]{1,0:T(8,128)S(1)} %collective-permute-done.1.refs_0_), channel_id=1, source_target_pairs={{0,3},{1,0},{2,1},{3,2},{4,7},{5,4},{6,5},{7,6},{8,11},{9,8},{10,9... | collective-permute-start | bytes 393224 | tf_op jit(solution)/shard_map/ppermute | solution.py:63
  38.3 2.1 %collective-permute-done.4.refs_3_ = f32[128,256]{1,0:T(8,128)S(1)} collective-permute-done((f32[128,256]{1,0:T(8,128)S(1)}, f32[128,256]{1,0:T(8,128)S(1)}, u32[]{:S(2)}, u32[]{:S(2)}) %collective-permute-start.4) | collective-permute-done | bytes 131104 | tf_op jit(solution)/shard_map/ppermute | solution.py:63
  40.4 2.6 %collective-permute-start.3 = (f32[128,256]{1,0:T(8,128)S(1)}, f32[128,256]{1,0:T(8,128)S(1)}, u32[]{:S(2)}, u32[]{:S(2)}) collective-permute-start(f32[128,256]{1,0:T(8,128)S(1)} %collective-permute-done.1.refs_0_), channel_id=1, source_target_pairs={{0,2},{1,3},{2,0},{3,1},{4,6},{5,7},{6,4},{7,5},{8,10},{9,11},{10,... | collective-permute-start | bytes 393224 | tf_op jit(solution)/shard_map/ppermute | solution.py:63
  43.0 4.2 %collective-permute-done.3.refs_2_ = f32[128,256]{1,0:T(8,128)S(1)} collective-permute-done((f32[128,256]{1,0:T(8,128)S(1)}, f32[128,256]{1,0:T(8,128)S(1)}, u32[]{:S(2)}, u32[]{:S(2)}) %collective-permute-start.3) | collective-permute-done | bytes 131104 | tf_op jit(solution)/shard_map/ppermute | solution.py:63
  48.1 5.8 %collective-permute-done.2.refs_1_ = f32[128,256]{1,0:T(8,128)S(1)} collective-permute-done((f32[128,256]{1,0:T(8,128)S(1)}, f32[128,256]{1,0:T(8,128)S(1)}, u32[]{:S(2)}, u32[]{:S(2)}) %collective-permute-start.2) | collective-permute-done | bytes 131104 | tf_op jit(solution)/shard_map/ppermute | solution.py:63
  53.9 1.2 shard_map.41
  55.1 1.1 shard_map.42
  56.2 1.1 shard_map.43
  57.4 1.2 shard_map.45
  58.9 1.1 collective-permute-start.16
  60.5 2.2 %collective-permute-done.17.refs_3_ = f32[8,128]{1,0:T(8,128)S(1)} collective-permute-done((f32[8,128]{1,0:T(8,128)S(1)}, f32[8,128]{1,0:T(8,128)S(1)}, u32[]{:S(2)}, u32[]{:S(2)}) %collective-permute-start.17) | collective-permute-done | bytes 4128 | tf_op jit(solution)/shard_map/ppermute | solution.py:63
  62.7 1.0 collective-permute-done.15.refs_1_
  63.6 1.3 shard_map.46
  64.9 2.8 %collective-permute-start.18 = (f32[32,128]{1,0:T(8,128)S(1)}, f32[32,128]{1,0:T(8,128)S(1)}, u32[]{:S(2)}, u32[]{:S(2)}) collective-permute-start(f32[32,128]{1,0:T(8,128)S(1)} %get-tuple-element.37.a_ref), channel_id=1, source_target_pairs={{0,4},{1,5},{2,6},{3,7},{4,0},{5,1},{6,2},{7,3},{8,12},{9,13},{10,... | collective-permute-start | bytes 49160 | tf_op jit(solution)/shard_map/ppermute | solution.py:63
  67.7 0.8 collective-permute-done.18.b_ref
  68.5 14.7 %all_to_all.22 = f32[16,32,128]{2,1,0:T(8,128)S(1)} all-to-all(f32[16,32,128]{2,1,0:T(8,128)S(1)} %bitcast.7), channel_id=1, replica_groups={{0,8,16,24,32,40,48,56,64,72,80,88,96,104,112,120},{4,12,20,28,36,44,52..., dimensions={0} | all-to-all | bytes 524288 | tf_op jit(solution)/shard_map/all_to_all | solution.py:420
  83.3 2.6 %shard_map.48 = (f32[8,128]{1,0:T(8,128)S(1)}, f32[32,512,128]{2,1,0:T(8,128)S(1)}, f32[32,128]{1,0:T(8,128)S(1)}) custom-call(f32[512,128]{1,0:T(8,128)S(1)} %bitcast.6, f32[8,128]{1,0:T(8,128)S(1)} %get-tuple-element.38.refs_1_.refs_5_, f32[4,128]{1,0:T(4,128)S(1)} %shard_map.44.refs_5_.refs_4_.refs_2_.refs_6_, ...), custom_call_target="tpu_custom_call" | custom-call | tf_op jit(solution)/shard_map/pallas_call | solution.py:403
  85.8 1.3 collective-permute-start.21
  87.6 1.0 collective-permute-start.19
  88.6 1.3 %collective-permute-done.21.refs_3_ = f32[8,128]{1,0:T(8,128)S(1)} collective-permute-done((f32[8,128]{1,0:T(8,128)S(1)}, f32[8,128]{1,0:T(8,128)S(1)}, u32[]{:S(2)}, u32[]{:S(2)}) %collective-permute-start.21) | collective-permute-done | bytes 4128 | tf_op jit(solution)/shard_map/ppermute | solution.py:63
  89.9 1.4 %collective-permute-done.19.refs_1_ = f32[8,128]{1,0:T(8,128)S(1)} collective-permute-done((f32[8,128]{1,0:T(8,128)S(1)}, f32[8,128]{1,0:T(8,128)S(1)}, u32[]{:S(2)}, u32[]{:S(2)}) %collective-permute-start.19) | collective-permute-done | bytes 4128 | tf_op jit(solution)/shard_map/ppermute | solution.py:63
  91.3 3.8 %shard_map.49 = (f32[512,4096]{1,0:T(8,128)}, f32[32,128]{1,0:T(8,128)S(1)}, f32[512,4096]{1,0:T(8,128)S(1)}, f32[8,128]{1,0:T(8,128)S(1)}) custom-call(f32[8,128]{1,0:T(8,128)S(1)} %get-tuple-element.41.refs_0_, f32[8,128]{1,0:T(8,128)S(1)} %collective-permute-done.19.refs_1_, f32[8,128]{1,0:T(8,128)S(1)} %collective-permute-done.20.refs_2_, ...), custom_call_target="tpu_custom_call" | custom-call | tf_op jit(solution)/shard_map/pallas_call | solution.py:403
  95.1 3.4 %copy-done.2 = f32[512,4096]{1,0:T(8,128)} copy-done((f32[512,4096]{1,0:T(8,128)}, f32[512,4096]{1,0:T(8,128)S(1)}, u32[]{:S(2)}) %copy-start.2) | copy-done | bytes 8388632
  98.4 3.2 %collective-permute-start.22 = (f32[32,128]{1,0:T(8,128)S(1)}, f32[32,128]{1,0:T(8,128)S(1)}, u32[]{:S(2)}, u32[]{:S(2)}) collective-permute-start(f32[32,128]{1,0:T(8,128)S(1)} %get-tuple-element.46.a_ref), channel_id=1, source_target_pairs={{0,4},{1,5},{2,6},{3,7},{4,0},{5,1},{6,2},{7,3},{8,12},{9,13},{10,... | collective-permute-start | bytes 49160 | tf_op jit(solution)/shard_map/ppermute | solution.py:63
  101.6 0.8 collective-permute-done.22.b_ref
  102.5 0.7 shard_map.50
  103.2 3.5 %all-to-all-start.1 = ((f32[16,32,128]{2,1,0:T(8,128)}), f32[16,32,128]{2,1,0:T(8,128)S(1)}, u32[]{:S(2)}, u32[]{:S(2)}) async-start(f32[16,32,128]{2,1,0:T(8,128)} %bitcast.3), calls=%async_computation.1 | async-start | bytes 524288 | tf_op jit(solution)/shard_map/all_to_all | solution.py:420
  106.8 3.4 %copy-done.3 = f32[512,4096]{1,0:T(8,128)S(1)} copy-done((f32[512,4096]{1,0:T(8,128)S(1)}, f32[512,4096]{1,0:T(8,128)}, u32[]{:S(2)}) %copy-start.3) | copy-done | bytes 8388632
  110.1 1.3 %rest.1 = f32[512,4096]{1,0:T(8,128)} custom-call(f32[512,4096]{1,0:T(8,128)S(1)} %copy-done.3, f32[512,4096]{1,0:T(8,128)} %get-tuple-element.45.given_hbm), custom_call_target="tpu_custom_call", output_to_operand_aliasing={{}: (1, {})} | custom-call | tf_op jit(solution)/shard_map/rest/pallas_call | solution.py:481
  111.5 3.7 %all-to-all-done.1 = f32[16,32,128]{2,1,0:T(8,128)S(1)} async-done(((f32[16,32,128]{2,1,0:T(8,128)}), f32[16,32,128]{2,1,0:T(8,128)S(1)}, u32[]{:S(2)}, u32[]{:S(2)}) %all-to-all-start.1) | async-done | bytes 262176 | tf_op jit(solution)/shard_map/all_to_all | solution.py:420
  115.2 3.4 %copy-done.1 = f32[32,512,128]{2,1,0:T(8,128)S(1)} copy-done((f32[32,512,128]{2,1,0:T(8,128)S(1)}, f32[32,512,128]{2,1,0:T(8,128)}, u32[]{:S(2)}) %copy-start.1) | copy-done | bytes 8388632
  118.5 3.4 %copy-done.4 = f32[512,4096]{1,0:T(8,128)S(1)} copy-done((f32[512,4096]{1,0:T(8,128)S(1)}, f32[512,4096]{1,0:T(8,128)}, u32[]{:S(2)}) %copy-start.4) | copy-done | bytes 8388632
  121.9 1.6 %copy-done.6 = f32[8,512,128]{2,1,0:T(8,128)S(1)} copy-done((f32[8,512,128]{2,1,0:T(8,128)S(1)}, f32[8,512,128]{2,1,0:T(8,128)}, u32[]{:S(2)}) %copy-start.6) | copy-done | bytes 2097176
  123.5 1.6 %copy-done.8 = f32[8,512,128]{2,1,0:T(8,128)S(1)} copy-done((f32[8,512,128]{2,1,0:T(8,128)S(1)}, f32[8,512,128]{2,1,0:T(8,128)}, u32[]{:S(2)}) %copy-start.8) | copy-done | bytes 2097176
  125.1 1.6 %copy-done.10 = f32[8,512,128]{2,1,0:T(8,128)S(1)} copy-done((f32[8,512,128]{2,1,0:T(8,128)S(1)}, f32[8,512,128]{2,1,0:T(8,128)}, u32[]{:S(2)}) %copy-start.10) | copy-done | bytes 2097176
  126.7 3.8 %shard_map.51 = f32[512,4096]{1,0:T(8,128)} custom-call(f32[512,128]{1,0:T(8,128)S(1)} %bitcast.5, f32[512,4096]{1,0:T(8,128)S(1)} %copy-done.4, f32[8,128]{1,0:T(8,128)S(1)} %get-tuple-element.47.refs_2_, f32[32,512,128]{2,1,0:T(8,128)S(1)} %copy-done.1, f32[8,512,128]{2,1,0:T(8,128)S(1)} %get-tuple-element.33.refs_5_.refs_10_.refs_4_, ...), custom_call_target="tpu_custom_call" | custom-call | tf_op jit(solution)/shard_map/pallas_call | solution.py:403
  (41 shorter events, 4.6 us)
Async XLA Ops:
  0.6 0.9 copy-start.11
  1.8 6.9 %collective-permute-start.7 = (f32[128,256]{1,0:T(8,128)S(1)}, f32[128,256]{1,0:T(8,128)S(1)}, u32[]{:S(2)}, u32[]{:S(2)}) collective-permute-start(f32[128,256]{1,0:T(8,128)S(1)} %unit.1), channel_id=1, source_target_pairs={{0,24},{1,25},{2,26},{3,27},{4,100},{5,101},{6,102},{7,103},{8,0},... | collective-permute-start | bytes 393224 | tf_op jit(solution)/shard_map/ppermute | solution.py:63
  5.4 5.6 %collective-permute-start.6 = (f32[128,256]{1,0:T(8,128)S(1)}, f32[128,256]{1,0:T(8,128)S(1)}, u32[]{:S(2)}, u32[]{:S(2)}) collective-permute-start(f32[128,256]{1,0:T(8,128)S(1)} %unit.1), channel_id=1, source_target_pairs={{0,16},{1,17},{2,18},{3,19},{4,68},{5,69},{6,70},{7,71},{8,24},{9,... | collective-permute-start | bytes 393224 | tf_op jit(solution)/shard_map/ppermute | solution.py:63
  5.8 6.7 %collective-permute-start.5 = (f32[128,256]{1,0:T(8,128)S(1)}, f32[128,256]{1,0:T(8,128)S(1)}, u32[]{:S(2)}, u32[]{:S(2)}) collective-permute-start(f32[128,256]{1,0:T(8,128)S(1)} %unit.1), channel_id=1, source_target_pairs={{0,8},{1,9},{2,10},{3,11},{4,36},{5,37},{6,38},{7,39},{8,16},{9,17... | collective-permute-start | bytes 393224 | tf_op jit(solution)/shard_map/ppermute | solution.py:63
  12.5 17.9 %collective-permute-start.13 = (f32[512,256]{1,0:T(8,128)S(1)}, f32[512,256]{1,0:T(8,128)S(1)}, u32[]{:S(2)}, u32[]{:S(2)}) collective-permute-start(f32[512,256]{1,0:T(8,128)S(1)} %pad_maximum_fusion.refs_4_), channel_id=1, source_target_pairs={{0,32},{1,33},{2,34},{3,35},{4,12},{5,13},{6,14},{7,15},{8,40},{9,... | collective-permute-start | bytes 1572872 | tf_op jit(solution)/shard_map/ppermute | solution.py:63
  13.5 17.5 %collective-permute-start.11 = (f32[512,256]{1,0:T(8,128)S(1)}, f32[512,256]{1,0:T(8,128)S(1)}, u32[]{:S(2)}, u32[]{:S(2)}) collective-permute-start(f32[512,256]{1,0:T(8,128)S(1)} %pad_maximum_fusion.refs_4_), channel_id=1, source_target_pairs={{0,96},{1,97},{2,98},{3,99},{4,28},{5,29},{6,30},{7,31},{8,104},{9... | collective-permute-start | bytes 1572872 | tf_op jit(solution)/shard_map/ppermute | solution.py:63
  15.2 15.8 %collective-permute-start.9 = (f32[512,256]{1,0:T(8,128)S(1)}, f32[512,256]{1,0:T(8,128)S(1)}, u32[]{:S(2)}, u32[]{:S(2)}) collective-permute-start(f32[512,256]{1,0:T(8,128)S(1)} %pad_maximum_fusion.refs_4_), channel_id=1, source_target_pairs={{0,64},{1,65},{2,66},{3,67},{4,20},{5,21},{6,22},{7,23},{8,72},{9,... | collective-permute-start | bytes 1572872 | tf_op jit(solution)/shard_map/ppermute | solution.py:63
  16.5 8.0 %collective-permute-start = (f32[128,256]{1,0:T(8,128)S(1)}, f32[128,256]{1,0:T(8,128)S(1)}, u32[]{:S(2)}, u32[]{:S(2)}) collective-permute-start(f32[128,256]{1,0:T(8,128)S(1)} %unit.1), channel_id=1, source_target_pairs={{0,0},{1,1},{2,2},{3,3},{4,5},{5,6},{6,7},{7,4},{8,10},{9,11},{10,... | collective-permute-start | bytes 393224 | tf_op jit(solution)/shard_map/ppermute | solution.py:63
  24.5 7.8 %collective-permute-start.1 = (f32[128,256]{1,0:T(8,128)S(1)}, f32[128,256]{1,0:T(8,128)S(1)}, u32[]{:S(2)}, u32[]{:S(2)}) collective-permute-start(f32[128,256]{1,0:T(8,128)S(1)} %collective-permute-done), channel_id=1, source_target_pairs={{0,0},{1,33},{2,66},{3,99},{4,96},{5,1},{6,34},{7,67},{8,64},{9,97... | collective-permute-start | bytes 393224 | tf_op jit(solution)/shard_map/ppermute | solution.py:63
  30.3 23.5 %collective-permute-start.8 = (f32[512,256]{1,0:T(8,128)S(1)}, f32[512,256]{1,0:T(8,128)S(1)}, u32[]{:S(2)}, u32[]{:S(2)}) collective-permute-start(f32[512,256]{1,0:T(8,128)S(1)} %pad_maximum_fusion.refs_4_), channel_id=1, source_target_pairs={{0,4},{1,5},{2,6},{3,7},{4,0},{5,1},{6,2},{7,3},{8,12},{9,13},{10,... | collective-permute-start | bytes 1572872 | tf_op jit(solution)/shard_map/ppermute | solution.py:63
  30.4 24.6 %collective-permute-start.14 = (f32[512,256]{1,0:T(8,128)S(1)}, f32[512,256]{1,0:T(8,128)S(1)}, u32[]{:S(2)}, u32[]{:S(2)}) collective-permute-start(f32[512,256]{1,0:T(8,128)S(1)} %collective-permute-done.13.refs_1_), channel_id=1, source_target_pairs={{0,4},{1,5},{2,6},{3,7},{4,0},{5,1},{6,2},{7,3},{8,12},{9,13},{10,... | collective-permute-start | bytes 1572872 | tf_op jit(solution)/shard_map/ppermute | solution.py:63
  30.9 25.3 %collective-permute-start.12 = (f32[512,256]{1,0:T(8,128)S(1)}, f32[512,256]{1,0:T(8,128)S(1)}, u32[]{:S(2)}, u32[]{:S(2)}) collective-permute-start(f32[512,256]{1,0:T(8,128)S(1)} %collective-permute-done.11.refs_1_), channel_id=1, source_target_pairs={{0,4},{1,5},{2,6},{3,7},{4,0},{5,1},{6,2},{7,3},{8,12},{9,13},{10,... | collective-permute-start | bytes 1572872 | tf_op jit(solution)/shard_map/ppermute | solution.py:63
  31.0 26.3 %collective-permute-start.10 = (f32[512,256]{1,0:T(8,128)S(1)}, f32[512,256]{1,0:T(8,128)S(1)}, u32[]{:S(2)}, u32[]{:S(2)}) collective-permute-start(f32[512,256]{1,0:T(8,128)S(1)} %collective-permute-done.9.refs_1_), channel_id=1, source_target_pairs={{0,4},{1,5},{2,6},{3,7},{4,0},{5,1},{6,2},{7,3},{8,12},{9,13},{10,... | collective-permute-start | bytes 1572872 | tf_op jit(solution)/shard_map/ppermute | solution.py:63
  32.2 8.1 %collective-permute-start.4 = (f32[128,256]{1,0:T(8,128)S(1)}, f32[128,256]{1,0:T(8,128)S(1)}, u32[]{:S(2)}, u32[]{:S(2)}) collective-permute-start(f32[128,256]{1,0:T(8,128)S(1)} %collective-permute-done.1.refs_0_), channel_id=1, source_target_pairs={{0,3},{1,0},{2,1},{3,2},{4,7},{5,4},{6,5},{7,6},{8,11},{9,8},{10,9... | collective-permute-start | bytes 393224 | tf_op jit(solution)/shard_map/ppermute | solution.py:63
  40.4 6.8 %collective-permute-start.3 = (f32[128,256]{1,0:T(8,128)S(1)}, f32[128,256]{1,0:T(8,128)S(1)}, u32[]{:S(2)}, u32[]{:S(2)}) collective-permute-start(f32[128,256]{1,0:T(8,128)S(1)} %collective-permute-done.1.refs_0_), channel_id=1, source_target_pairs={{0,2},{1,3},{2,0},{3,1},{4,6},{5,7},{6,4},{7,5},{8,10},{9,11},{10,... | collective-permute-start | bytes 393224 | tf_op jit(solution)/shard_map/ppermute | solution.py:63
  47.2 6.7 %collective-permute-start.2 = (f32[128,256]{1,0:T(8,128)S(1)}, f32[128,256]{1,0:T(8,128)S(1)}, u32[]{:S(2)}, u32[]{:S(2)}) collective-permute-start(f32[128,256]{1,0:T(8,128)S(1)} %collective-permute-done.1.refs_0_), channel_id=1, source_target_pairs={{0,1},{1,2},{2,3},{3,0},{4,5},{5,6},{6,7},{7,4},{8,9},{9,10},{10,1... | collective-permute-start | bytes 393224 | tf_op jit(solution)/shard_map/ppermute | solution.py:63
  47.4 0.7 copy-start.12
  56.2 35.1 %copy-start.5 = (f32[8,512,128]{2,1,0:T(8,128)}, f32[8,512,128]{2,1,0:T(8,128)S(1)}, u32[]{:S(2)}) copy-start(f32[8,512,128]{2,1,0:T(8,128)S(1)} %get-tuple-element.34.refs_6_.refs_11_.refs_5_) | copy-start | bytes 6291460
  57.3 33.9 %copy-start.7 = (f32[8,512,128]{2,1,0:T(8,128)}, f32[8,512,128]{2,1,0:T(8,128)S(1)}, u32[]{:S(2)}) copy-start(f32[8,512,128]{2,1,0:T(8,128)S(1)} %get-tuple-element.36.refs_8_.refs_13_.refs_7_) | copy-start | bytes 6291460
  58.6 32.6 %copy-start.9 = (f32[8,512,128]{2,1,0:T(8,128)}, f32[8,512,128]{2,1,0:T(8,128)S(1)}, u32[]{:S(2)}) copy-start(f32[8,512,128]{2,1,0:T(8,128)S(1)} %get-tuple-element.35.refs_7_.refs_12_.refs_6_) | copy-start | bytes 6291460
  58.6 4.0 %collective-permute-start.17 = (f32[8,128]{1,0:T(8,128)S(1)}, f32[8,128]{1,0:T(8,128)S(1)}, u32[]{:S(2)}, u32[]{:S(2)}) collective-permute-start(f32[8,128]{1,0:T(8,128)S(1)} %get-tuple-element.32.refs_0_), channel_id=1, source_target_pairs={{0,2},{1,3},{2,0},{3,1},{4,6},{5,7},{6,4},{7,5},{8,10},{9,11},{10,... | collective-permute-start | bytes 12296 | tf_op jit(solution)/shard_map/ppermute | solution.py:63
  58.9 3.8 %collective-permute-start.16 = (f32[8,128]{1,0:T(8,128)S(1)}, f32[8,128]{1,0:T(8,128)S(1)}, u32[]{:S(2)}, u32[]{:S(2)}) collective-permute-start(f32[8,128]{1,0:T(8,128)S(1)} %get-tuple-element.32.refs_0_), channel_id=1, source_target_pairs={{0,3},{1,0},{2,1},{3,2},{4,7},{5,4},{6,5},{7,6},{8,11},{9,8},{10,9... | collective-permute-start | bytes 12296 | tf_op jit(solution)/shard_map/ppermute | solution.py:63
  60.0 3.7 %collective-permute-start.15 = (f32[8,128]{1,0:T(8,128)S(1)}, f32[8,128]{1,0:T(8,128)S(1)}, u32[]{:S(2)}, u32[]{:S(2)}) collective-permute-start(f32[8,128]{1,0:T(8,128)S(1)} %get-tuple-element.32.refs_0_), channel_id=1, source_target_pairs={{0,1},{1,2},{2,3},{3,0},{4,5},{5,6},{6,7},{7,4},{8,9},{9,10},{10,1... | collective-permute-start | bytes 12296 | tf_op jit(solution)/shard_map/ppermute | solution.py:63
  64.9 3.6 %collective-permute-start.18 = (f32[32,128]{1,0:T(8,128)S(1)}, f32[32,128]{1,0:T(8,128)S(1)}, u32[]{:S(2)}, u32[]{:S(2)}) collective-permute-start(f32[32,128]{1,0:T(8,128)S(1)} %get-tuple-element.37.a_ref), channel_id=1, source_target_pairs={{0,4},{1,5},{2,6},{3,7},{4,0},{5,1},{6,2},{7,3},{8,12},{9,13},{10,... | collective-permute-start | bytes 49160 | tf_op jit(solution)/shard_map/ppermute | solution.py:63
  85.8 9.2 %copy-start = (f32[32,512,128]{2,1,0:T(8,128)}, f32[32,512,128]{2,1,0:T(8,128)S(1)}, u32[]{:S(2)}) copy-start(f32[32,512,128]{2,1,0:T(8,128)S(1)} %get-tuple-element.43.refs_7_.refs_3_) | copy-start | bytes 25165828
  85.8 4.0 %collective-permute-start.21 = (f32[8,128]{1,0:T(8,128)S(1)}, f32[8,128]{1,0:T(8,128)S(1)}, u32[]{:S(2)}, u32[]{:S(2)}) collective-permute-start(f32[8,128]{1,0:T(8,128)S(1)} %get-tuple-element.41.refs_0_), channel_id=1, source_target_pairs={{0,2},{1,3},{2,0},{3,1},{4,6},{5,7},{6,4},{7,5},{8,10},{9,11},{10,... | collective-permute-start | bytes 12296 | tf_op jit(solution)/shard_map/ppermute | solution.py:63
  87.1 2.8 %collective-permute-start.20 = (f32[8,128]{1,0:T(8,128)S(1)}, f32[8,128]{1,0:T(8,128)S(1)}, u32[]{:S(2)}, u32[]{:S(2)}) collective-permute-start(f32[8,128]{1,0:T(8,128)S(1)} %get-tuple-element.41.refs_0_), channel_id=1, source_target_pairs={{0,3},{1,0},{2,1},{3,2},{4,7},{5,4},{6,5},{7,6},{8,11},{9,8},{10,9... | collective-permute-start | bytes 12296 | tf_op jit(solution)/shard_map/ppermute | solution.py:63
  87.6 3.7 %collective-permute-start.19 = (f32[8,128]{1,0:T(8,128)S(1)}, f32[8,128]{1,0:T(8,128)S(1)}, u32[]{:S(2)}, u32[]{:S(2)}) collective-permute-start(f32[8,128]{1,0:T(8,128)S(1)} %get-tuple-element.41.refs_0_), channel_id=1, source_target_pairs={{0,1},{1,2},{2,3},{3,0},{4,5},{5,6},{6,7},{7,4},{8,9},{9,10},{10,1... | collective-permute-start | bytes 12296 | tf_op jit(solution)/shard_map/ppermute | solution.py:63
  95.0 3.4 %copy-start.2 = (f32[512,4096]{1,0:T(8,128)}, f32[512,4096]{1,0:T(8,128)S(1)}, u32[]{:S(2)}) copy-start(f32[512,4096]{1,0:T(8,128)S(1)} %get-tuple-element.44.resp_ref.refs_1_) | copy-start | bytes 25165828
  98.4 4.0 %collective-permute-start.22 = (f32[32,128]{1,0:T(8,128)S(1)}, f32[32,128]{1,0:T(8,128)S(1)}, u32[]{:S(2)}, u32[]{:S(2)}) collective-permute-start(f32[32,128]{1,0:T(8,128)S(1)} %get-tuple-element.46.a_ref), channel_id=1, source_target_pairs={{0,4},{1,5},{2,6},{3,7},{4,0},{5,1},{6,2},{7,3},{8,12},{9,13},{10,... | collective-permute-start | bytes 49160 | tf_op jit(solution)/shard_map/ppermute | solution.py:63
  103.2 11.9 %all-to-all-start.1 = ((f32[16,32,128]{2,1,0:T(8,128)}), f32[16,32,128]{2,1,0:T(8,128)S(1)}, u32[]{:S(2)}, u32[]{:S(2)}) async-start(f32[16,32,128]{2,1,0:T(8,128)} %bitcast.3), calls=%async_computation.1 | async-start | bytes 524288 | tf_op jit(solution)/shard_map/all_to_all | solution.py:420
  106.8 3.4 %copy-start.3 = (f32[512,4096]{1,0:T(8,128)S(1)}, f32[512,4096]{1,0:T(8,128)}, u32[]{:S(2)}) copy-start(f32[512,4096]{1,0:T(8,128)} %copy-done.2) | copy-start | bytes 25165828
  115.2 3.4 %copy-start.1 = (f32[32,512,128]{2,1,0:T(8,128)S(1)}, f32[32,512,128]{2,1,0:T(8,128)}, u32[]{:S(2)}) copy-start(f32[32,512,128]{2,1,0:T(8,128)} %copy-done) | copy-start | bytes 25165828
  118.5 3.4 %copy-start.4 = (f32[512,4096]{1,0:T(8,128)S(1)}, f32[512,4096]{1,0:T(8,128)}, u32[]{:S(2)}) copy-start(f32[512,4096]{1,0:T(8,128)} %copy-done.2) | copy-start | bytes 25165828
  121.9 1.6 %copy-start.6 = (f32[8,512,128]{2,1,0:T(8,128)S(1)}, f32[8,512,128]{2,1,0:T(8,128)}, u32[]{:S(2)}) copy-start(f32[8,512,128]{2,1,0:T(8,128)} %copy-done.5) | copy-start | bytes 6291460
  123.5 1.6 %copy-start.8 = (f32[8,512,128]{2,1,0:T(8,128)S(1)}, f32[8,512,128]{2,1,0:T(8,128)}, u32[]{:S(2)}) copy-start(f32[8,512,128]{2,1,0:T(8,128)} %copy-done.7) | copy-start | bytes 6291460
  125.1 1.6 %copy-start.10 = (f32[8,512,128]{2,1,0:T(8,128)S(1)}, f32[8,512,128]{2,1,0:T(8,128)}, u32[]{:S(2)}) copy-start(f32[8,512,128]{2,1,0:T(8,128)} %copy-done.9) | copy-start | bytes 6291460
